TPU v7x, 32 devices: a whole 2x2x4 slice. The times are simulated.
32 devices in a mesh: dp: 4 (over y, core), fsdp: 8 (over z, x).
Axes of the slice: x: 2, y: 2, z: 4, core: 2. Of those that a mesh axis runs over, the one named last changes fastest.
Arguments:
- tokens: bfloat16 [65536, 512], P(('dp', 'fsdp')), may hold values from -6 to 6
- lengths: int32 [256], replicated, may hold values from 0 to 2048, as said below
- assignment: int32 [256], replicated, may hold values from 0 to 31, as said below
- weights: bfloat16 [2097152], P(('dp', 'fsdp')), may hold values from -1.5 to 1.5
- vectors: bfloat16 [5120], P(('dp', 'fsdp')), may hold values from -1.6 to 1.8
- cotangent: bfloat16 [65536, 512], P(('dp', 'fsdp')), may hold values from -6 to 6
Outputs:
- layer_output: bfloat16 [65536, 512], P(('dp', 'fsdp'))
- grad_tokens: float32 [65536, 512], P(('dp', 'fsdp'))
- grad_weights: float32 [2097152], P(('dp', 'fsdp'))
- grad_vectors: float32 [5120], P(('dp', 'fsdp'))
Inputs may be any that keep to these rules, and one draw needn't show every extreme that they name: The datasets that assignment gives one device have lengths adding up to exactly 2048; some dataset has 2048 samples. `assignment`: every device holds exactly 8 datasets.
All inputs are finite; a program needn't handle non-finite values.
Results may differ from a plain program's by a relative error of at most 0.012.
The roundings to bfloat16 on the way count: a program that leaves them out, or rounds other values in their place, can miss the bound.
Values may be sent and summed in bfloat16 or wider, within the bound.
No kernel may reach another device: no remote copies, remote signals or barrier semaphores. Data moves between devices by JAX's collectives and lax.ppermute only.
A program may use at most 256 MiB of HBM per device.

v0:
```python
import functools
import math

import jax
import jax.numpy as jnp
from jax import lax
from jax.experimental import pallas as pl
from jax.experimental.pallas import tpu as pltpu
from jax.sharding import PartitionSpec as P

HEADS = 4
HEAD_DIM = 128
FF = 1024
AXES = ("dp", "fsdp")
NORM_EPS = 1e-05
BLOCKS = 32
QKV_ROWS = 48
Q_ROWS = 4 * QKV_ROWS + 16
R_ROWS = 320
FAR = -1e30
f32 = jnp.float32
bf16 = jnp.bfloat16
NT = (((1,), (1,)), ((), ()))
NN = (((1,), (0,)), ((), ()))
TN = (((0,), (0,)), ((), ()))
TT = (((0,), (1,)), ((), ()))
VMEM_MIB = {"pack": 2, "project": 14, "attend": 18, "middle": 26, "attend_back": 28, "input_grad": 14, "unpack": 3}


def dot(a, b, dims):
    return lax.dot_general(a, b, dims, preferred_element_type=f32)


def params(name):
    return pltpu.CompilerParams(vmem_limit_bytes=VMEM_MIB[name] << 20)


def cost(flops, moved, special=0):
    return pl.CostEstimate(flops=int(flops), bytes_accessed=int(moved), transcendentals=int(special))


def whole(shape):
    return pl.BlockSpec(shape, lambda *_: (0,) * len(shape))


def scalar_spec():
    return pl.BlockSpec(memory_space=pltpu.SMEM)


def owner_of(place, me, order):
    mask = 0
    for bit, step in enumerate(order):
        mask = mask + ((place >> bit) & 1) * step
    return jnp.bitwise_xor(me, mask)


def split3(value):
    high = value.astype(bf16)
    rest = value - high.astype(f32)
    middle = rest.astype(bf16)
    low = (rest - middle.astype(f32)).astype(bf16)
    return high, middle, low


PANELS = ((0, 48, 4), (192, 16, 4), (256, 16, 8), (384, 32, 4))


def pack_kernel(vec_width, me_ref, flat, vec, q_out, r_out, wide, line):
    wide[...] = flat[...].astype(f32)
    line[...] = jnp.zeros_like(line)
    line[0:1, 0:vec_width] = vec[...].astype(f32)
    shifted = pltpu.roll(line[...], (me_ref[0] * vec_width) % 128, 1)
    parts = []
    for start, rows, count in PANELS:
        for j in range(count):
            parts.append(wide[pl.ds(start + j, rows, stride=count), :].astype(bf16))
    q_out[0:192, :] = jnp.concatenate(parts[:4], axis=0)
    placed = jnp.concatenate([shifted[0:1, 0:128], shifted[0:1, 128:256], jnp.zeros((14, 128), f32)], axis=0)
    q_out[192:208, :] = placed.astype(bf16)
    r_out[...] = jnp.concatenate(parts[4:], axis=0)


def pack(me, flat, vec, vec_width):
    vmem = pl.BlockSpec(memory_space=pltpu.VMEM)
    return pl.pallas_call(
        functools.partial(pack_kernel, vec_width),
        in_specs=[scalar_spec(), vmem, vmem],
        out_shape=[
            jax.ShapeDtypeStruct((Q_ROWS, 128), bf16),
            jax.ShapeDtypeStruct((R_ROWS, 128), bf16),
        ],
        scratch_shapes=[pltpu.VMEM((512, 128), f32), pltpu.VMEM((8, 256), f32)],
        compiler_params=params("pack"),
        name="pack",
    )(me, flat, vec)


def project_kernel(masks, order, vec_width, me_ref, ends, tokens, *refs):
    pieces = refs[: len(masks)]
    qkv, keys_extra, query_extra, vec_out, weight, vec = refs[len(masks) :]
    step = pl.program_id(0)
    rows = tokens.shape[0]
    me = me_ref[0]

    @pl.when(step == 0)
    def _():
        vec[...] = jnp.zeros_like(vec)
        for mask, ref in zip(masks, pieces):
            for i in range(1 << len(order)):
                d = owner_of(i, jnp.bitwise_xor(me, mask), order)
                row = pl.multiple_of(d * QKV_ROWS, 16)
                for j in range(4):
                    at = i * Q_ROWS + QKV_ROWS * j
                    weight[pl.ds(row, QKV_ROWS), 128 * j : 128 * (j + 1)] = ref[at : at + QKV_ROWS, :]
                row = (d * vec_width) // 128
                at = i * Q_ROWS + 4 * QKV_ROWS
                vec[pl.ds(row, 2), :] = vec[pl.ds(row, 2), :] + ref[at : at + 16, :].astype(f32)[0:2, :]
        vec_out[...] = vec[...]

    x = tokens[...]
    scale = 1.0 / math.sqrt(HEAD_DIM)
    query_bias = jnp.concatenate([vec[j : j + 1, :] for j in range(4)], axis=1)
    value_bias = jnp.concatenate([vec[4 + j : 5 + j, :] for j in range(4)], axis=1)
    queries = ((dot(x, weight[0:512, :], NN) + query_bias) * scale).astype(bf16)
    key_heads = dot(x, weight[512:1024, :], NN).astype(bf16)
    values = (dot(x, weight[1024:1536, :], NN) + value_bias).astype(bf16)
    qkv[:, 0:512] = queries
    qkv[:, 512:1024] = key_heads
    qkv[:, 1024:1536] = values
    places = step * rows + lax.broadcasted_iota(jnp.int32, (rows, ends.shape[1]), 0)
    label = jnp.sum((ends[...] <= places).astype(f32), axis=1, keepdims=True)
    lane = lax.broadcasted_iota(jnp.int32, (rows, 128), 1)
    same = lane.astype(f32) == label
    keys_extra[...] = jnp.where(lane < 8, jnp.where(same, 1.0, 0.0), jnp.where(lane < 32, 1.0, 0.0)).astype(bf16)
    apart = jnp.where((lane < 8) & jnp.logical_not(same), FAR, 0.0)
    product = queries.astype(f32) * key_heads.astype(f32)
    extra = apart
    for h in range(HEADS):
        own = jnp.sum(product[:, 128 * h : 128 * (h + 1)], axis=1, keepdims=True)
        extra = jnp.where(lane == 8 + h, -own, extra)
    query_extra[...] = extra.astype(bf16)


def project(me, ends, tokens, pieces, masks, order, vec_width, rows=512):
    count = tokens.shape[0]
    sets = ends.shape[1]
    return pl.pallas_call(
        functools.partial(project_kernel, masks, order, vec_width),
        grid=(count // rows,),
        in_specs=[
            scalar_spec(),
            whole((1, sets)),
            pl.BlockSpec((rows, 512), lambda i: (i, 0)),
        ]
        + [whole(piece.shape) for piece in pieces],
        out_specs=[
            pl.BlockSpec((rows, 1536), lambda i: (i, 0)),
            pl.BlockSpec((rows, 128), lambda i: (i, 0)),
            pl.BlockSpec((rows, 128), lambda i: (i, 0)),
            whole((48, 128)),
            whole((1536, 512)),
        ],
        out_shape=[
            jax.ShapeDtypeStruct((count, 1536), bf16),
            jax.ShapeDtypeStruct((count, 128), bf16),
            jax.ShapeDtypeStruct((count, 128), bf16),
            jax.ShapeDtypeStruct((48, 128), f32),
            jax.ShapeDtypeStruct((1536, 512), bf16),
        ],
        scratch_shapes=[pltpu.VMEM((48, 128), f32)],
        compiler_params=params("project"),
        cost_estimate=cost(2 * count * 512 * 1536, 12e6),
        name="project",
    )(me, ends, tokens, *pieces)


def own_lanes(lane, head):
    return (lane < 8) | (lane == 8 + head) | ((lane >= 16 + 4 * head) & (lane < 19 + 4 * head))


def attend_kernel(base, q, k, v, query_extra, keys_extra, *refs):
    attended, offset_out, total, mixed, peak = refs[-5:]
    rows = q.shape[0]
    head = base + pl.program_id(0)
    lane = lax.broadcasted_iota(jnp.int32, (rows, 128), 1)
    extra = jnp.where(own_lanes(lane, head), query_extra[...].astype(f32), 0.0).astype(bf16)
    left = jnp.concatenate([k[...], keys_extra[...]], axis=1)
    right = jnp.concatenate([q[...], extra], axis=1)
    weights = jnp.exp(dot(left, right, NT))
    total[...] = jnp.sum(weights, axis=0, keepdims=True)
    mixed[...] = dot(v[...], weights.astype(bf16), TN)
    peak[...] = jnp.zeros_like(peak)
    good = (total[...] > 1e-20) & (total[...] < 1e30)

    @pl.when(jnp.sum(jnp.where(good, 0.0, 1.0)) > 0.0)
    def _():
        def part(j, _):
            place = pl.ds(pl.multiple_of(j * 128, 128), 128)
            lane = lax.broadcasted_iota(jnp.int32, (128, 128), 1)
            extra = jnp.where(own_lanes(lane, head), query_extra[place, :].astype(f32), 0.0).astype(bf16)
            again = dot(left, jnp.concatenate([q[place, :], extra], axis=1), NT)
            top = jnp.max(again, axis=0, keepdims=True)
            safe = jnp.exp(again - top)
            total[:, place] = jnp.sum(safe, axis=0, keepdims=True)
            mixed[:, place] = dot(v[...], safe.astype(bf16), TN)
            peak[:, place] = top
            return 0

        lax.fori_loop(0, rows // 128, part, 0)

    attended[...] = (mixed[...] * (1.0 / total[...])).T.astype(bf16)
    offset_out[0] = peak[...] + jnp.log(total[...])


def attend(qkv, query_extra, keys_extra, base, heads, prior, rows=1024):
    count = qkv.shape[0]
    return pl.pallas_call(
        functools.partial(attend_kernel, base),
        grid=(heads, count // rows),
        in_specs=[
            pl.BlockSpec((rows, 128), lambda h, i: (i, base + h)),
            pl.BlockSpec((count, 128), lambda h, i: (0, HEADS + base + h)),
            pl.BlockSpec((count, 128), lambda h, i: (0, 2 * HEADS + base + h)),
            pl.BlockSpec((rows, 128), lambda h, i: (i, 0)),
            pl.BlockSpec((count, 128), lambda h, i: (0, 0)),
        ]
        + [pl.BlockSpec(memory_space=pl.ANY) for _ in prior],
        out_specs=[
            pl.BlockSpec((rows, 128), lambda h, i: (i, base + h)),
            pl.BlockSpec((1, 1, rows), lambda h, i: (base + h, 0, i)),
        ],
        out_shape=[
            jax.ShapeDtypeStruct((count, 128 * HEADS), bf16),
            jax.ShapeDtypeStruct((HEADS, 1, count), f32),
        ],
        scratch_shapes=[pltpu.VMEM((1, rows), f32), pltpu.VMEM((128, rows), f32), pltpu.VMEM((1, rows), f32)],
        input_output_aliases={5: 0, 6: 1} if prior else {},
        compiler_params=params("attend"),
        cost_estimate=cost(heads * 8 * count * count * 128, 6e6, heads * count * count),
        name="attend",
    )(qkv, qkv, qkv, query_extra, keys_extra, *prior)


def mean_row(value):
    return jnp.sum(value, axis=1, keepdims=True) * (1.0 / value.shape[1])


def norm_rows(summed):
    centered = summed - mean_row(summed)
    inverse = lax.rsqrt(mean_row(centered * centered) + NORM_EPS)
    return centered * inverse, inverse


def norm_back(grad, normed, inverse):
    return inverse * (grad - mean_row(grad) - normed * mean_row(grad * normed))


def fold8(value):
    return jnp.sum(value.reshape(value.shape[0] // 8, 8, value.shape[1]), axis=0)


def middle_kernel(masks, order_in, order_out, sub, me_ref, tokens, attended, offset, query_extra, cotangent, vec, *refs):
    pieces = refs[: len(masks)]
    layer_output, grad_branch_out, grad_attended_out, grad_extra, query_extra_out, keep, send, vec_out = refs[
        len(masks) : -8
    ]
    attn_weight, in_weight, out_weight, grad_attn, grad_in, grad_out, sums, hidden_sum = refs[-8:]
    step = pl.program_id(0)
    me = me_ref[0]
    half = BLOCKS // 2

    @pl.when(step == 0)
    def _():
        for mask, ref in zip(masks, pieces):

            def place(i, _, mask=mask, ref=ref):
                d = owner_of(i, jnp.bitwise_xor(me, mask), order_in)
                start = i * R_ROWS
                a_row = pl.multiple_of(d * 16, 16)
                o_row = pl.multiple_of(d * 32, 16)
                for j in range(4):
                    attn_weight[pl.ds(a_row, 16), 128 * j : 128 * (j + 1)] = ref[
                        pl.ds(pl.multiple_of(start + 16 * j, 16), 16), :
                    ]
                for j in range(8):
                    in_weight[pl.ds(a_row, 16), 128 * j : 128 * (j + 1)] = ref[
                        pl.ds(pl.multiple_of(start + 64 + 16 * j, 16), 16), :
                    ]
                for j in range(4):
                    out_weight[pl.ds(o_row, 32), 128 * j : 128 * (j + 1)] = ref[
                        pl.ds(pl.multiple_of(start + 192 + 32 * j, 16), 32), :
                    ]
                return 0

            lax.fori_loop(0, 1 << len(order_in), place, 0, unroll=True)
        grad_attn[...] = jnp.zeros_like(grad_attn)
        grad_in[...] = jnp.zeros_like(grad_in)
        grad_out[...] = jnp.zeros_like(grad_out)
        sums[...] = jnp.zeros_like(sums)
        hidden_sum[...] = jnp.zeros_like(hidden_sum)

    def row_of(index):
        return jnp.concatenate([vec[4 * index + j : 4 * index + j + 1, :] for j in range(4)], axis=1)

    attn_bias, ffn_bias, gain_one, shift_one, gain_two, shift_two = [row_of(i) for i in range(2, 8)]
    hidden_bias = jnp.concatenate([vec[32 + j : 33 + j, :] for j in range(8)], axis=1)

    offset_rows = jnp.concatenate([offset[h] for h in range(HEADS)] + [jnp.zeros((4, tokens.shape[0]), f32)], axis=0)
    offsets = offset_rows.T
    lane = lax.broadcasted_iota(jnp.int32, (tokens.shape[0], 128), 1)
    extra = query_extra[...].astype(f32)
    for h in range(HEADS):
        for i, part in enumerate(split3(-offsets[:, h : h + 1])):
            extra = jnp.where(lane == 16 + 4 * h + i, part.astype(f32), extra)
    query_extra_out[...] = extra.astype(bf16)

    kept = [{} for _ in range(tokens.shape[0] // sub)]

    def chain(s):
        sl = slice(s * sub, (s + 1) * sub)
        att = attended[sl, :]
        branch = dot(att, attn_weight[...], NN) + attn_bias
        yield
        normed_one, inverse_one = norm_rows(tokens[sl, :].astype(f32) + branch)
        hidden = normed_one * gain_one + shift_one
        hidden_low = hidden.astype(bf16)
        yield
        pre_act = dot(hidden_low, in_weight[...], NN) + hidden_bias
        yield
        cdf = 0.5 * (1.0 + lax.erf(pre_act * 0.7071067811865476))
        density = jnp.exp(-0.5 * pre_act * pre_act) * 0.3989422804014327
        activated = (pre_act * cdf).astype(bf16)
        slope = cdf + pre_act * density
        yield
        ffn_result = dot(activated, out_weight[...], NN) + ffn_bias
        yield
        normed_two, inverse_two = norm_rows(hidden + ffn_result)
        layer_output[sl, :] = (normed_two * gain_two + shift_two).astype(bf16)
        grad_result = cotangent[sl, :].astype(f32)
        sums[4] += fold8(grad_result * normed_two)
        sums[5] += fold8(grad_result)
        grad_second = norm_back(grad_result * gain_two, normed_two, inverse_two)
        grad_ffn = grad_second.astype(bf16)
        sums[1] += fold8(grad_ffn.astype(f32))
        yield
        grad_activated = dot(grad_ffn, out_weight[...], NT)
        kept[s][0] = (activated, grad_ffn)
        yield
        grad_pre = (grad_activated * slope).astype(bf16)
        hidden_sum[...] += fold8(grad_pre.astype(f32))
        yield
        grad_hidden = grad_second + dot(grad_pre, in_weight[...], NT)
        kept[s][1] = (hidden_low, grad_pre)
        yield
        sums[2] += fold8(grad_hidden * normed_one)
        sums[3] += fold8(grad_hidden)
        grad_first = norm_back(grad_hidden * gain_one, normed_one, inverse_one)
        grad_branch = grad_first.astype(bf16)
        grad_branch_out[sl, :] = grad_branch
        sums[0] += fold8(grad_branch.astype(f32))
        yield
        grad_attended = dot(grad_branch, attn_weight[...], NT)
        kept[s][2] = (att, grad_branch)
        yield
        low = grad_attended.astype(bf16)
        grad_attended_out[sl, :] = low
        lane = lax.broadcasted_iota(jnp.int32, (sub, 128), 1)
        extra = jnp.zeros((sub, 128), f32)
        for h in range(HEADS):
            cols = slice(128 * h, 128 * (h + 1))
            low_cols = low[:, cols].astype(f32)
            centre = jnp.sum(low_cols * att[:, cols].astype(f32), axis=1, keepdims=True)
            for i, part in enumerate(split3(-centre)):
                extra = jnp.where(lane == 4 * h + i, part.astype(f32), extra)
        grad_extra[sl, :] = extra.astype(bf16)
        yield

    chains = [chain(s) for s in range(tokens.shape[0] // sub)]
    started = 0
    live = []
    while started < len(chains) or live:
        if started < len(chains):
            live.append(chains[started])
            started += 1
        remaining = []
        for c in live:
            try:
                next(c)
                remaining.append(c)
            except StopIteration:
                pass
        live = remaining
        for i, ref in enumerate((grad_out, grad_in, grad_attn)):
            if all(i in k for k in kept):
                left = jnp.concatenate([k[i][0] for k in kept], axis=0)
                right = jnp.concatenate([k.pop(i)[1] for k in kept], axis=0)
                ref[...] += dot(left, right, TN)

    @pl.when(step == pl.num_programs(0) - 1)
    def _():
        for base, ref in ((0, keep), (half, send)):

            def place(i, _, base=base, ref=ref):
                d = owner_of(base + i, me, order_out)
                start = i * R_ROWS
                a_row = pl.multiple_of(d * 16, 16)
                o_row = pl.multiple_of(d * 32, 16)
                for j in range(4):
                    ref[pl.ds(pl.multiple_of(start + 16 * j, 16), 16), :] = grad_attn[
                        pl.ds(a_row, 16), 128 * j : 128 * (j + 1)
                    ].astype(bf16)
                for j in range(8):
                    ref[pl.ds(pl.multiple_of(start + 64 + 16 * j, 16), 16), :] = grad_in[
                        pl.ds(a_row, 16), 128 * j : 128 * (j + 1)
                    ].astype(bf16)
                for j in range(4):
                    ref[pl.ds(pl.multiple_of(start + 192 + 32 * j, 16), 32), :] = grad_out[
                        pl.ds(o_row, 32), 128 * j : 128 * (j + 1)
                    ].astype(bf16)
                return 0

            lax.fori_loop(0, half, place, 0, unroll=4)
        vec_out[...] = jnp.zeros_like(vec_out)
        for i in range(6):
            row = jnp.sum(sums[i], axis=0, keepdims=True)
            for j in range(4):
                vec_out[8 + 4 * i + j : 9 + 4 * i + j, :] = row[:, 128 * j : 128 * (j + 1)]
        row = jnp.sum(hidden_sum[...], axis=0, keepdims=True)
        for j in range(8):
            vec_out[32 + j : 33 + j, :] = row[:, 128 * j : 128 * (j + 1)]


def middle(
    me, tokens, attended, offset, query_extra, cotangent, vec, pieces, masks, order_in, order_out, rows=512, sub=256
):
    count = tokens.shape[0]
    by_row = pl.BlockSpec((rows, 512), lambda i: (i, 0))
    half_rows = BLOCKS // 2 * R_ROWS
    return pl.pallas_call(
        functools.partial(middle_kernel, masks, order_in, order_out, sub),
        grid=(count // rows,),
        in_specs=[
            scalar_spec(),
            by_row,
            by_row,
            pl.BlockSpec((HEADS, 1, rows), lambda i: (0, 0, i)),
            pl.BlockSpec((rows, 128), lambda i: (i, 0)),
            by_row,
            whole((48, 128)),
        ]
        + [whole(piece.shape) for piece in pieces],
        out_specs=[
            by_row,
            by_row,
            by_row,
            pl.BlockSpec((rows, 128), lambda i: (i, 0)),
            pl.BlockSpec((rows, 128), lambda i: (i, 0)),
            whole((half_rows, 128)),
            whole((half_rows, 128)),
            whole((48, 128)),
        ],
        out_shape=[
            jax.ShapeDtypeStruct((count, 512), bf16),
            jax.ShapeDtypeStruct((count, 512), bf16),
            jax.ShapeDtypeStruct((count, 512), bf16),
            jax.ShapeDtypeStruct((count, 128), bf16),
            jax.ShapeDtypeStruct((count, 128), bf16),
            jax.ShapeDtypeStruct((half_rows, 128), bf16),
            jax.ShapeDtypeStruct((half_rows, 128), bf16),
            jax.ShapeDtypeStruct((48, 128), f32),
        ],
        scratch_shapes=[
            pltpu.VMEM((512, 512), bf16),
            pltpu.VMEM((512, FF), bf16),
            pltpu.VMEM((FF, 512), bf16),
            pltpu.VMEM((512, 512), f32),
            pltpu.VMEM((512, FF), f32),
            pltpu.VMEM((FF, 512), f32),
            pltpu.VMEM((6, 8, 512), f32),
            pltpu.VMEM((8, FF), f32),
        ],
        compiler_params=params("middle"),
        cost_estimate=cost(6 * count * 1310720, 22e6, 3 * count * FF),
        name="middle",
    )(me, tokens, attended, offset, query_extra, cotangent, vec, *pieces)


def attend_back_kernel(
    base,
    heads,
    order,
    vec_width,
    me_ref,
    tokens,
    q,
    k,
    v,
    grad,
    query_extra,
    keys_extra,
    grad_extra,
    vec_in,
    grad_query,
    grad_keys,
    grad_values,
    keep,
    send,
    vec,
    acc,
    all_keys,
    all_values,
    grad_weight,
    held,
    sem,
):
    local = pl.program_id(0)
    step = pl.program_id(1)
    steps = pl.num_programs(1)
    width = k.shape[0]
    last = base + heads == HEADS
    copy = pltpu.make_async_copy(tokens, held, sem)

    @pl.when((local == 0) & (step == 0))
    def _():
        copy.start()
        vec[...] = vec_in[...]

    head = base + local
    lane = lax.broadcasted_iota(jnp.int32, (width, 128), 1)
    ones = jnp.where((lane >= 4 * head) & (lane < 4 * head + 3), 1.0, 0.0).astype(bf16)
    extra = jnp.where(own_lanes(lane, head), keys_extra[...].astype(f32), 0.0).astype(bf16)
    scores = dot(
        jnp.concatenate([q[...], query_extra[...]], axis=1), jnp.concatenate([k[...], extra], axis=1), NT
    )
    centred = dot(
        jnp.concatenate([grad[...], grad_extra[...]], axis=1), jnp.concatenate([v[...], ones], axis=1), NT
    )
    probs = jnp.exp(scores)
    probs_low = probs.astype(bf16)
    grad_scores = (probs * centred).astype(bf16)
    gv = dot(grad[...], probs_low, TN).astype(bf16)
    gk = dot(q[...], grad_scores, TN).astype(bf16)
    grad_values[...] = gv
    grad_keys[...] = gk
    all_values[step] = gv
    all_keys[step] = gk
    part = dot(grad_scores, k[...], NN)

    @pl.when(step == 0)
    def _():
        acc[...] = part

    @pl.when(step > 0)
    def _():
        acc[...] += part

    @pl.when((local == 0) & (step == steps - 1))
    def _():
        copy.wait()

    @pl.when(step == steps - 1)
    def _():
        me = me_ref[0]
        scale = 1.0 / math.sqrt(HEAD_DIM)
        x = held[...]
        gq_all = acc[...].astype(bf16)
        grad_query[...] = gq_all
        gk_all = jnp.concatenate([all_keys[i] for i in range(all_keys.shape[0])], axis=1)
        gv_all = jnp.concatenate([all_values[i] for i in range(all_values.shape[0])], axis=1)
        grad_weight[0:512, :] = dot(gq_all, x, TN).T * scale
        grad_weight[512:1024, :] = dot(gk_all, x, NN).T
        grad_weight[1024:1536, :] = dot(gv_all, x, NN).T
        row_ones = jnp.ones((8, x.shape[0]), bf16)
        vec[pl.ds(base + local, 1), :] = dot(row_ones, gq_all, NN)[0:1] * scale
        vec[pl.ds(4 + base + local, 1), :] = dot(row_ones, gv_all, NT)[0:1]
        half = BLOCKS // 2
        block = heads * QKV_ROWS + (16 if last else 0)
        for start, ref in ((0, keep), (half, send)):

            def place(i, _, start=start, ref=ref):
                d = owner_of(start + i, me, order)
                ref[pl.ds(pl.multiple_of(i * block + local * QKV_ROWS, 16), QKV_ROWS), :] = grad_weight[
                    pl.ds(pl.multiple_of(d * QKV_ROWS, 16), QKV_ROWS), :
                ].astype(bf16)
                if last:
                    pair = vec[pl.ds((d * vec_width) // 128, 2), :]
                    pair = jnp.concatenate([pair, jnp.zeros((14, 128), f32)], axis=0)
                    ref[pl.ds(pl.multiple_of(i * block + heads * QKV_ROWS, 16), 16), :] = pair.astype(bf16)
                return 0

            lax.fori_loop(0, half, place, 0, unroll=4)


def attend_back(
    me, tokens, qkv, grad_attended, query_extra, keys_extra, grad_extra, vec, order, vec_width, base, heads, width=512
):
    count = qkv.shape[0]
    half_rows = BLOCKS // 2 * (heads * QKV_ROWS + (16 if base + heads == HEADS else 0))
    return pl.pallas_call(
        functools.partial(attend_back_kernel, base, heads, order, vec_width),
        grid=(heads, count // width),
        in_specs=[
            scalar_spec(),
            pl.BlockSpec(memory_space=pl.ANY),
            pl.BlockSpec((count, 128), lambda h, i: (0, base + h)),
            pl.BlockSpec((width, 128), lambda h, i: (i, HEADS + base + h)),
            pl.BlockSpec((width, 128), lambda h, i: (i, 2 * HEADS + base + h)),
            pl.BlockSpec((count, 128), lambda h, i: (0, base + h)),
            whole((count, 128)),
            pl.BlockSpec((width, 128), lambda h, i: (i, 0)),
            whole((count, 128)),
            whole((48, 128)),
        ],
        out_specs=[
            pl.BlockSpec((count, 128), lambda h, i: (0, h)),
            pl.BlockSpec((128, width), lambda h, i: (h, i)),
            pl.BlockSpec((128, width), lambda h, i: (h, i)),
            whole((half_rows, 128)),
            whole((half_rows, 128)),
            whole((48, 128)),
        ],
        out_shape=[
            jax.ShapeDtypeStruct((count, 128 * heads), bf16),
            jax.ShapeDtypeStruct((128 * heads, count), bf16),
            jax.ShapeDtypeStruct((128 * heads, count), bf16),
            jax.ShapeDtypeStruct((half_rows, 128), bf16),
            jax.ShapeDtypeStruct((half_rows, 128), bf16),
            jax.ShapeDtypeStruct((48, 128), f32),
        ],
        scratch_shapes=[
            pltpu.VMEM((count, 128), f32),
            pltpu.VMEM((count // width, 128, width), bf16),
            pltpu.VMEM((count // width, 128, width), bf16),
            pltpu.VMEM((1536, 128), f32),
            pltpu.VMEM((count, 512), bf16),
            pltpu.SemaphoreType.DMA,
        ],
        compiler_params=params("attend_back"),
        cost_estimate=cost(heads * 20 * count * count * 128, heads * 12e6, heads * count * count),
        name="attend_back",
    )(me, tokens, qkv, qkv, qkv, grad_attended, query_extra, keys_extra, grad_extra, vec)


def input_grad_kernel(groups, *refs):
    grad_branch = refs[0]
    queries, keys, values = [refs[1 + i * groups : 1 + (i + 1) * groups] for i in range(3)]
    weight, out = refs[-2], refs[-1]
    scale = 1.0 / math.sqrt(HEAD_DIM)
    gq = jnp.concatenate([r[...] for r in queries], axis=1)
    gk = jnp.concatenate([r[...] for r in keys], axis=0)
    gv = jnp.concatenate([r[...] for r in values], axis=0)
    total = grad_branch[...].astype(f32) + scale * dot(gq, weight[0:512, :], NT)
    total = total + dot(gk, weight[512:1024, :], TT)
    out[...] = total + dot(gv, weight[1024:1536, :], TT)


def input_grad(grad_branch, queries, keys, values, weight, rows=512):
    count = grad_branch.shape[0]
    by_row = pl.BlockSpec((rows, 512), lambda i: (i, 0))
    return pl.pallas_call(
        functools.partial(input_grad_kernel, len(queries)),
        grid=(count // rows,),
        in_specs=[by_row]
        + [pl.BlockSpec((rows, a.shape[1]), lambda i: (i, 0)) for a in queries]
        + [pl.BlockSpec((a.shape[0], rows), lambda i: (0, i)) for a in keys + values]
        + [whole((1536, 512))],
        out_specs=by_row,
        out_shape=jax.ShapeDtypeStruct((count, 512), f32),
        compiler_params=params("input_grad"),
        cost_estimate=cost(2 * count * 512 * 1536, 16e6),
        name="input_grad",
    )(grad_branch, *queries, *keys, *values, weight)


def unpack_kernel(vec_width, me_ref, *refs):
    q_parts, r_parts = refs[:4], refs[4:6]
    out, vec_out, line = refs[6:]
    q_sum, r_sum = q_parts[0][...], r_parts[0][...]
    for part in q_parts[1:]:
        q_sum = q_sum + part[...].astype(f32)
    for part in r_parts[1:]:
        r_sum = r_sum + part[...].astype(f32)
    at = 0
    source = q_sum
    for index, (start, rows, count) in enumerate(PANELS):
        if index == 1:
            source, at = r_sum, 0
        for j in range(count):
            out[pl.ds(start + j, rows, stride=count), :] = source[at : at + rows, :]
            at += rows
    pair = jnp.concatenate([q_sum[192:200, :], q_sum[193:201, :]], axis=1)
    line[...] = pltpu.roll(pair, 256 - (me_ref[0] * vec_width) % 128, 1)
    vec_out[...] = line[0:1, 0:vec_width]


def unpack(me, q_parts, r_parts, vec_width):
    vmem = pl.BlockSpec(memory_space=pltpu.VMEM)
    return pl.pallas_call(
        functools.partial(unpack_kernel, vec_width),
        in_specs=[scalar_spec()] + [vmem] * 6,
        out_shape=[jax.ShapeDtypeStruct((512, 128), f32), jax.ShapeDtypeStruct((1, vec_width), f32)],
        scratch_shapes=[pltpu.VMEM((8, 256), f32)],
        compiler_params=params("unpack"),
        name="unpack",
    )(me, *q_parts, *r_parts)


def swap(array, step, count):
    return lax.ppermute(array, AXES, [(i, i ^ step) for i in range(count)])


def swap_each(parts, steps, count):
    pairs = list(zip(parts, steps))
    return [swap(part, step, count) for part, step in pairs[::-1]][::-1]


def after(value, *others):
    return lax.optimization_barrier((value, *others))[0]


def quarters(groups):
    parts = []
    for keep, got in groups:
        keep, got = keep.reshape(4, 4, -1, 128), got.reshape(4, 4, -1, 128)
        parts.append([keep[i].astype(f32) + got[i].astype(f32) for i in range(4)])
    totals = [jnp.concatenate(same, axis=1) if len(same) > 1 else same[0] for same in zip(*parts)]
    return totals[0], [total.astype(bf16).reshape(-1, 128) for total in totals[1:]]


def halves(keep, gots):
    total = keep
    for got in gots:
        total = total + got.astype(f32).reshape(keep.shape)
    half = total.shape[0] // 2
    return total[:half], total[half:].astype(bf16).reshape(-1, 128)


def fourths(keep, gots):
    total = keep
    for got in gots:
        total = total + got.astype(f32).reshape(keep.shape)
    return [total[0]] + [total[i].astype(bf16) for i in range(1, 4)]


def fast_layout(dp, fsdp):
    return dp == 4 and fsdp == 8


def gather_line(block, steps, count):
    return jnp.concatenate([block] + [swap(block, step, count) for step in steps], axis=0)


def body(dp, fsdp, tokens, lengths, assignment, weights, vectors, cotangent):
    count = dp * fsdp
    fast = fast_layout(dp, fsdp)
    owner = lax.axis_index(AXES).astype(jnp.int32)
    owned = assignment == owner
    ends = jnp.cumsum(jnp.where(owned, lengths, 0), dtype=jnp.int32)
    ends = jnp.where(owned, ends, 1 << 30)[None, :]
    if fast:
        vec_width = vectors.shape[0]
        core, x_step, y_step, z_near, z_far = fsdp, 1, 2 * fsdp, 2, 4
        planes = [x_step, y_step, x_step + y_step]
        spread = [x_step + y_step, y_step, x_step]
        line = [z_near, z_far, z_near + z_far]
        order_in, order_rest = [z_near, z_far], [z_far, z_near]
        order_out = [z_near, z_far, x_step, y_step, core]
        order_rest_out = order_rest + order_out[2:]
        masks = [0] + spread
        masks = masks + [m + core for m in masks]
        me = owner[None]
        q_block, r_block = pack(me, pltpu.with_memory_space_constraint(weights.reshape(512, 128), pltpu.HBM), vectors.reshape(1, vec_width), vec_width)
        lines = [swap(q_block, step, count) for step in line[::-1]][::-1]
        q_far = jnp.concatenate([q_block, lines[0], lines[1], after(lines[2], ends)], axis=0)
        q_core = swap(q_far, core, count)
        q_pieces = [q_far] + [swap(q_far, step, count) for step in spread]
        r_far = gather_line(after(r_block, q_core), [z_far], count)
        r_far = gather_line(r_far, [z_near], count)
        q_pieces = q_pieces + [q_core] + [swap(piece, core, count) for piece in q_pieces[1:]]
        r_pieces = [swap(after(r_far, *q_pieces), step, count) for step in spread]
    else:
        vec_width = 160
        order_in, order_rest, order_out = [1, 2], [1, 2], [1, 2, 4, 8, 16]
        order_rest_out = order_out
        masks = [4 * i for i in range(8)]
        me = jnp.zeros((1,), jnp.int32)
        blocks = lax.all_gather(weights, AXES, axis=0, tiled=True).reshape(count, -1)
        flat = lax.all_gather(vectors, AXES, axis=0, tiled=True).reshape(40, 128)
        square = 512 * 512 // count
        cuts = [0, 3 * square, 4 * square, 6 * square, 8 * square]
        panels = []
        for index, (start, rows, width) in enumerate(PANELS):
            piece = blocks[:, cuts[index] : cuts[index + 1]].reshape(BLOCKS, rows, width, 128)
            panels.append(piece.transpose(0, 2, 1, 3).reshape(BLOCKS, rows * width, 128))
        spots = [(d * vec_width) // 128 for d in range(BLOCKS)]
        lanes = jnp.arange(256)
        vec_blocks = []
        for d in range(BLOCKS):
            pair = jnp.concatenate([flat, jnp.zeros((8, 128), bf16)], axis=0)[spots[d] : spots[d] + 2].reshape(256)
            offset = d * vec_width - 128 * spots[d]
            pair = jnp.where((lanes >= offset) & (lanes < offset + vec_width), pair, 0)
            vec_blocks.append(jnp.concatenate([pair.reshape(2, 128), jnp.zeros((14, 128), bf16)], axis=0))
        q_all = jnp.concatenate([panels[0], jnp.stack(vec_blocks)], axis=1)
        r_all = jnp.concatenate(panels[1:], axis=1)
        q_pieces = [q_all[4 * i : 4 * i + 4].reshape(-1, 128) for i in range(8)]
        r_pieces = [r_all[4 * i : 4 * i + 4].reshape(-1, 128) for i in range(8)]
    qkv, keys_extra, query_extra, vec, weight = project(
        me, ends, pltpu.with_memory_space_constraint(tokens, pltpu.HBM), q_pieces, masks, order_in, vec_width
    )
    prior = attend(qkv, query_extra, keys_extra, 0, 3, [])
    if fast:
        r_pieces = [r_far] + [after(piece, prior[0]) for piece in r_pieces]
        keys_extra = after(keys_extra, *r_pieces)
        r_pieces = r_pieces + [swap(piece, core, count) for piece in r_pieces]
    attended, offset = attend(qkv, query_extra, keys_extra, 3, 1, prior)
    layer_output, grad_branch, grad_attended, grad_extra, query_extra, r_keep, r_send, vec_grad = middle(
        me, tokens, attended, offset, query_extra, cotangent, vec, r_pieces, masks, order_rest, order_rest_out
    )
    queries, keys, values, keeps, sends, gots = [], [], [], [], [], []
    if fast:
        r_got = swap(r_send, core, count)
    for base, heads in ((0, 1), (1, 2), (3, 1)):
        gq, gk, gv, keep, send, vec_grad = attend_back(
            me,
            tokens,
            qkv,
            grad_attended,
            query_extra,
            keys_extra,
            grad_extra,
            vec_grad,
            order_out,
            vec_width,
            base,
            heads,
        )
        queries.append(gq)
        keys.append(gk)
        values.append(gv)
        keeps.append(keep)
        sends.append(send)
        if not fast:
            continue
        gots.append(swap(send, core, count))
        if base == 0:
            r_keep, r_sends = quarters([(r_keep, after(r_got, gq))])
            vec_grad = after(vec_grad, *r_sends)
            r_gots = swap_each(r_sends, planes, count)
        elif base == 1:
            r_gots = [after(part, gq) for part in r_gots]
            r_keep, r_send = halves(r_keep, r_gots)
            vec_grad = after(vec_grad, r_send)
            r_got = swap(r_send, z_near, count)
    if fast:
        r_keep, r_send = halves(r_keep, [after(r_got, gq)])
        gots = [after(got, gq) for got in gots]
        q_keep, q_sends = quarters(list(zip(keeps, gots)))
        grad_branch = after(grad_branch, *q_sends)
        q_gots = swap_each(q_sends, planes, count)
    grad_tokens = input_grad(grad_branch, queries, keys, values, weight)
    if fast:
        r_parts = [r_keep.reshape(-1, 128), swap(after(r_send, grad_tokens), z_far, count)]
        q_gots = [after(part, grad_tokens) for part in q_gots]
        q_parts = fourths(q_keep, q_gots)
        q_parts = q_parts[:1] + swap_each(q_parts[1:], line, count)
        own_weights, own_vectors = unpack(me, q_parts, r_parts, vec_width)
        own_weights = own_weights.reshape(-1)
        own_vectors = own_vectors.reshape(-1)
    else:
        heads = [jnp.concatenate([k, g], axis=0).astype(f32).reshape(BLOCKS, -1, 128) for k, g in zip(keeps, sends)]
        q_all = jnp.concatenate(heads, axis=1)
        r_all = jnp.concatenate([r_keep, r_send], axis=0).astype(f32).reshape(BLOCKS, R_ROWS, 128)
        sources = (q_all[:, : 4 * QKV_ROWS], r_all[:, :64], r_all[:, 64:192], r_all[:, 192:])
        pieces = []
        for source, (start, rows, width) in zip(sources, PANELS):
            piece = source.reshape(BLOCKS, width, rows, 128).transpose(0, 2, 1, 3)
            pieces.append(piece.reshape(count, -1))
        own_weights = lax.psum_scatter(
            jnp.concatenate(pieces, axis=1).reshape(-1), AXES, scatter_dimension=0, tiled=True
        )
        pairs = q_all[:, 4 * QKV_ROWS : 4 * QKV_ROWS + 2].reshape(BLOCKS, 256)
        rows = [
            pairs[d, (d * vec_width) % 128 : (d * vec_width) % 128 + vec_width] for d in range(BLOCKS)
        ]
        own_vectors = lax.psum_scatter(jnp.concatenate(rows), AXES, scatter_dimension=0, tiled=True)
    return (layer_output, grad_tokens, own_weights, own_vectors)


def solution(mesh):
    dp, fsdp = mesh.shape["dp"], mesh.shape["fsdp"]
    in_specs = (
        P(AXES, None),
        P(),
        P(),
        P(AXES),
        P(AXES),
        P(AXES, None),
    )
    out_specs = (
        P(AXES, None),
        P(AXES, None),
        P(AXES),
        P(AXES),
    )
    return jax.shard_map(
        functools.partial(body, dp, fsdp), mesh=mesh, in_specs=in_specs, out_specs=out_specs, check_vma=False
    )
```

profile of v0, /device:TPU:0, one launch (start us, length us, event | category | flops | bytes accessed | tf_op | source)
XLA Modules:
  0.0 161.9 jit_solution(5639682488143572290)
XLA Ops:
  0.6 0.7 reshape.215.vec
  1.3 1.0 pack.1
  2.3 5.1 %collective-permute-start.2 = (bf16[208,128]{1,0:T(8,128)(2,1)S(1)}, bf16[208,128]{1,0:T(8,128)(2,1)S(1)}, u32[]{:S(2)}, u32[]{:S(2)}) collective-permute-start(bf16[208,128]{1,0:T(8,128)(2,1)S(1)} %get-tuple-element.64), channel_id=1, source_target_pairs={{0,6},{1,7},{2,4},{3,5},{4,2},{5,3},{6,0},{7,1},{8,14},{9,15},{10,... | collective-permute-start | bytes 159752 | tf_op jit(solution)/shard_map/ppermute | solution.py:709
  7.4 0.6 collective-permute-start
  8.0 0.7 select_bitcast_fusion
  8.7 0.3 reduce-window.9
  9.2 0.8 bitcast_select_fusion
  10.0 1.5 collective-permute-done
  11.5 0.9 collective-permute-done.1
  12.5 1.6 collective-permute-start.5
  14.1 1.5 collective-permute-start.4
  15.6 0.5 collective-permute-start.3
  16.1 2.1 %collective-permute-start.10 = (bf16[320,128]{1,0:T(8,128)(2,1)S(1)}, bf16[320,128]{1,0:T(8,128)(2,1)S(1)}, u32[]{:S(2)}, u32[]{:S(2)}) collective-permute-start(bf16[320,128]{1,0:T(8,128)(2,1)S(1)} %get-tuple-element.70), channel_id=1, source_target_pairs={{0,4},{1,5},{2,6},{3,7},{4,0},{5,1},{6,2},{7,3},{8,12},{9,13},{10,... | collective-permute-start | bytes 245768 | tf_op jit(solution)/shard_map/ppermute | solution.py:709
  18.1 2.5 %collective-permute-done.5.refs_3_ = bf16[832,128]{1,0:T(8,128)(2,1)S(1)} collective-permute-done((bf16[832,128]{1,0:T(8,128)(2,1)S(1)}, bf16[832,128]{1,0:T(8,128)(2,1)S(1)}, u32[]{:S(2)}, u32[]{:S(2)}) %collective-permute-start.5) | collective-permute-done | bytes 213024 | tf_op jit(solution)/shard_map/ppermute | solution.py:709
  20.6 5.3 %collective-permute-done.4.refs_2_ = bf16[832,128]{1,0:T(8,128)(2,1)S(1)} collective-permute-done((bf16[832,128]{1,0:T(8,128)(2,1)S(1)}, bf16[832,128]{1,0:T(8,128)(2,1)S(1)}, u32[]{:S(2)}, u32[]{:S(2)}) %collective-permute-start.4) | collective-permute-done | bytes 213024 | tf_op jit(solution)/shard_map/ppermute | solution.py:709
  26.0 0.5 collective-permute-start.7
  26.5 1.0 collective-permute-start.11
  27.7 5.7 %project.1 = (bf16[2048,1536]{1,0:T(8,128)(2,1)S(1)}, bf16[2048,128]{1,0:T(8,128)(2,1)S(1)}, bf16[2048,128]{1,0:T(8,128)(2,1)S(1)}, f32[48,128]{1,0:T(8,128)S(1)}, bf16[1536,512]{1,0:T(8,128)(2,1)S(1)}) custom-call(s32[1]{0:T(128)} %bitcast.me_ref, s32[1,256]{1,0:T(1,128)S(1)} %bitcast.38, bf16[2048,512]{1,0:T(8,128)(2,1)} %tokens.9, ...), custom_call_target="tpu_custom_call" | custom-call | flops 3221225472 | bytes 12000000 | tf_op jit(solution)/shard_map/project/pallas_call | solution.py:147
  33.5 1.0 collective-permute-start.14
  34.5 1.1 collective-permute-start.13
  35.6 1.4 collective-permute-start.12
  37.0 13.3 %attend.2 = (bf16[2048,512]{1,0:T(8,128)(2,1)S(1)}, f32[4,1,2048]{2,1,0:T(1,128)S(1)}) custom-call(bf16[2048,1536]{1,0:T(8,128)(2,1)S(1)} %get-tuple-element.66.q.k.v, bf16[2048,1536]{1,0:T(8,128)(2,1)S(1)} %get-tuple-element.66.q.k.v, bf16[2048,1536]{1,0:T(8,128)(2,1)S(1)} %get-tuple-element.66.q.k.v, bf16[2048,128]{1,0:T(8,128)(2,1)S(1)} %get-tuple-element.67.query_extra, ...), custom_call_target="tpu_custom_call" | custom-call | flops 12884901888 | bytes 6000000 | tf_op jit(solution)/shard_map/attend/pallas_call | solution.py:217
  50.5 0.9 collective-permute-done.12.refs_1_
  51.3 0.5 collective-permute-start.17
  51.8 4.5 %attend.3 = (bf16[2048,512]{1,0:T(8,128)(2,1)S(1)}, f32[4,1,2048]{2,1,0:T(1,128)S(1)}) custom-call(bf16[2048,1536]{1,0:T(8,128)(2,1)S(1)} %get-tuple-element.66.q.k.v, bf16[2048,1536]{1,0:T(8,128)(2,1)S(1)} %get-tuple-element.66.q.k.v, bf16[2048,1536]{1,0:T(8,128)(2,1)S(1)} %get-tuple-element.66.q.k.v, ...), custom_call_target="tpu_custom_call", output_to_operand_aliasing={{0}: (5, {}), {1}: (6, {})} | custom-call | flops 4294967296 | bytes 6000000 | tf_op jit(solution)/shard_map/attend/pallas_call | solution.py:217
  56.4 26.0 %middle.1 = (bf16[2048,512]{1,0:T(8,128)(2,1)}, bf16[2048,512]{1,0:T(8,128)(2,1)S(1)}, bf16[2048,512]{1,0:T(8,128)(2,1)S(1)}, bf16[2048,128]{1,0:T(8,128)(2,1)S(...) custom-call(s32[1]{0:T(128)} %bitcast.me_ref, ...), custom_call_target="tpu_custom_call" | custom-call | flops 16106127360 | bytes 22000000 | tf_op jit(solution)/shard_map/middle/pallas_call | solution.py:439
  82.3 0.5 collective-permute-start.20
  82.8 12.4 %attend_back.3 = (bf16[2048,128]{1,0:T(8,128)(2,1)S(1)}, bf16[128,2048]{1,0:T(8,128)(2,1)S(1)}, bf16[128,2048]{1,0:T(8,128)(2,1)S(1)}, bf16[768,128]{1,0:T(8,128...) custom-call(s32[1]{0:T(128)} %bitcast.me_ref, bf16[2048,512]{1,0:T(8,128)(2,1)S(1)} %copy-done.1, ...), custom_call_target="tpu_custom_call" | custom-call | flops 10737418240 | bytes 12000000 | tf_op jit(solution)/shard_map/attend_back/pallas_call | solution.py:599
  95.6 1.8 %collective-permute-start.23 = (bf16[1280,128]{1,0:T(8,128)(2,1)S(1)}, bf16[1280,128]{1,0:T(8,128)(2,1)S(1)}, u32[]{:S(2)}, u32[]{:S(2)}) collective-permute-start(bf16[1280,128]{1,0:T(8,128)(2,1)S(1)} %get-tuple-element.126), channel_id=1, source_target_pairs={{0,17},{1,16},{2,19},{3,18},{4,21},{5,20},{6,23},{7,22},{8,25},{9,... | collective-permute-start | bytes 983048 | tf_op jit(solution)/shard_map/ppermute | solution.py:709
  97.4 0.5 collective-permute-start.22
  97.9 1.3 collective-permute-start.21
  99.2 24.9 %attend_back.4 = (bf16[2048,256]{1,0:T(8,128)(2,1)S(1)}, bf16[256,2048]{1,0:T(8,128)(2,1)S(1)}, bf16[256,2048]{1,0:T(8,128)(2,1)S(1)}, bf16[1536,128]{1,0:T(8,12...) custom-call(s32[1]{0:T(128)} %bitcast.me_ref, bf16[2048,512]{1,0:T(8,128)(2,1)S(1)} %copy-done.1, ...), custom_call_target="tpu_custom_call" | custom-call | flops 21474836480 | bytes 24000000 | tf_op jit(solution)/shard_map/attend_back/pallas_call | solution.py:599
  124.5 1.0 collective-permute-start.32
  125.4 13.2 %attend_back.5 = (bf16[2048,128]{1,0:T(8,128)(2,1)S(1)}, bf16[128,2048]{1,0:T(8,128)(2,1)S(1)}, bf16[128,2048]{1,0:T(8,128)(2,1)S(1)}, bf16[1024,128]{1,0:T(8,12...) custom-call(s32[1]{0:T(128)} %bitcast.me_ref, bf16[2048,512]{1,0:T(8,128)(2,1)S(1)} %copy-done.1, ...), custom_call_target="tpu_custom_call" | custom-call | flops 10737418240 | bytes 12000000 | tf_op jit(solution)/shard_map/attend_back/pallas_call | solution.py:599
  138.7 0.3 collective-permute-start.25
  139.2 1.1 collective-permute-done.25
  140.4 0.8 collective-permute-start.26
  141.2 1.6 collective-permute-start.27
  142.8 1.3 collective-permute-start.28
  144.1 5.5 %input_grad.1 = f32[2048,512]{1,0:T(8,128)} custom-call(bf16[2048,512]{1,0:T(8,128)(2,1)S(1)} %get-tuple-element.109.refs_0_, bf16[2048,128]{1,0:T(8,128)(2,1)S(1)} %get-tuple-element.92.refs_1_, bf16[2048,256]{1,0:T(8,128)(2,1)S(1)} %get-tuple-element.96.refs_2_, bf16[2048,128]{1,0:T(8,128)(2,1)S(1)} %get-tuple-element.101.refs_3_, ...), custom_call_target="tpu_custom_call" | custom-call | flops 3221225472 | bytes 16000000 | tf_op jit(solution)/shard_map/input_grad/pallas_call | solution.py:660
  149.5 2.0 %collective-permute-start.33 = (bf16[320,128]{1,0:T(8,128)(2,1)S(1)}, bf16[320,128]{1,0:T(8,128)(2,1)S(1)}, u32[]{:S(2)}, u32[]{:S(2)}) collective-permute-start(bf16[320,128]{1,0:T(8,128)(2,1)S(1)} %slice.259), channel_id=1, source_target_pairs={{0,4},{1,5},{2,6},{3,7},{4,0},{5,1},{6,2},{7,3},{8,12},{9,13},{10,... | collective-permute-start | bytes 245768 | tf_op jit(solution)/shard_map/ppermute | solution.py:709
  151.6 0.4 collective-permute-done.27
  152.0 1.0 collective-permute-done.28
  153.1 2.7 %collective-permute-start.31 = (bf16[208,128]{1,0:T(8,128)(2,1)S(1)}, bf16[208,128]{1,0:T(8,128)(2,1)S(1)}, u32[]{:S(2)}, u32[]{:S(2)}) collective-permute-start(bf16[208,128]{1,0:T(8,128)(2,1)S(1)} %get-tuple-element.141), channel_id=1, source_target_pairs={{0,6},{1,7},{2,4},{3,5},{4,2},{5,3},{6,0},{7,1},{8,14},{9,15},{10,... | collective-permute-start | bytes 159752 | tf_op jit(solution)/shard_map/ppermute | solution.py:709
  155.8 1.8 %collective-permute-start.29 = (bf16[208,128]{1,0:T(8,128)(2,1)S(1)}, bf16[208,128]{1,0:T(8,128)(2,1)S(1)}, u32[]{:S(2)}, u32[]{:S(2)}) collective-permute-start(bf16[208,128]{1,0:T(8,128)(2,1)S(1)} %get-tuple-element.143), channel_id=1, source_target_pairs={{0,2},{1,3},{2,0},{3,1},{4,6},{5,7},{6,4},{7,5},{8,10},{9,11},{10,... | collective-permute-start | bytes 159752 | tf_op jit(solution)/shard_map/ppermute | solution.py:709
  157.6 1.5 collective-permute-done.31.refs_3_
  159.1 2.0 %collective-permute-done.30.refs_2_ = bf16[208,128]{1,0:T(8,128)(2,1)S(1)} collective-permute-done((bf16[208,128]{1,0:T(8,128)(2,1)S(1)}, bf16[208,128]{1,0:T(8,128)(2,1)S(1)}, u32[]{:S(2)}, u32[]{:S(2)}) %collective-permute-start.30) | collective-permute-done | bytes 53280 | tf_op jit(solution)/shard_map/ppermute | solution.py:709
  161.1 0.8 unpack.1
  (64 shorter events, 1.8 us)
Async XLA Ops:
  2.3 9.2 %collective-permute-start.2 = (bf16[208,128]{1,0:T(8,128)(2,1)S(1)}, bf16[208,128]{1,0:T(8,128)(2,1)S(1)}, u32[]{:S(2)}, u32[]{:S(2)}) collective-permute-start(bf16[208,128]{1,0:T(8,128)(2,1)S(1)} %get-tuple-element.64), channel_id=1, source_target_pairs={{0,6},{1,7},{2,4},{3,5},{4,2},{5,3},{6,0},{7,1},{8,14},{9,15},{10,... | collective-permute-start | bytes 159752 | tf_op jit(solution)/shard_map/ppermute | solution.py:709
  7.4 5.0 %collective-permute-start.1 = (bf16[208,128]{1,0:T(8,128)(2,1)S(1)}, bf16[208,128]{1,0:T(8,128)(2,1)S(1)}, u32[]{:S(2)}, u32[]{:S(2)}) collective-permute-start(bf16[208,128]{1,0:T(8,128)(2,1)S(1)} %get-tuple-element.64), channel_id=1, source_target_pairs={{0,4},{1,5},{2,6},{3,7},{4,0},{5,1},{6,2},{7,3},{8,12},{9,13},{10,... | collective-permute-start | bytes 159752 | tf_op jit(solution)/shard_map/ppermute | solution.py:709
  7.4 4.1 %collective-permute-start = (bf16[208,128]{1,0:T(8,128)(2,1)S(1)}, bf16[208,128]{1,0:T(8,128)(2,1)S(1)}, u32[]{:S(2)}, u32[]{:S(2)}) collective-permute-start(bf16[208,128]{1,0:T(8,128)(2,1)S(1)} %get-tuple-element.64), channel_id=1, source_target_pairs={{0,2},{1,3},{2,0},{3,1},{4,6},{5,7},{6,4},{7,5},{8,10},{9,11},{10,... | collective-permute-start | bytes 159752 | tf_op jit(solution)/shard_map/ppermute | solution.py:709
  12.4 3.6 %collective-permute-start.6 = (bf16[832,128]{1,0:T(8,128)(2,1)S(1)}, bf16[832,128]{1,0:T(8,128)(2,1)S(1)}, u32[]{:S(2)}, u32[]{:S(2)}) collective-permute-start(bf16[832,128]{1,0:T(8,128)(2,1)S(1)} %constant_dynamic-update-slice_fusion.refs_0_), channel_id=1, source_target_pairs={{0,8},{1,9},{2,10},{3,11},{4,12},{5,13},{6,14},{7,15},{8,0},{9,1},... | collective-permute-start | bytes 638984 | tf_op jit(solution)/shard_map/ppermute | solution.py:709
  12.5 8.1 %collective-permute-start.5 = (bf16[832,128]{1,0:T(8,128)(2,1)S(1)}, bf16[832,128]{1,0:T(8,128)(2,1)S(1)}, u32[]{:S(2)}, u32[]{:S(2)}) collective-permute-start(bf16[832,128]{1,0:T(8,128)(2,1)S(1)} %constant_dynamic-update-slice_fusion.refs_0_), channel_id=1, source_target_pairs={{0,1},{1,0},{2,3},{3,2},{4,5},{5,4},{6,7},{7,6},{8,9},{9,8},{10,11... | collective-permute-start | bytes 638984 | tf_op jit(solution)/shard_map/ppermute | solution.py:709
  14.1 11.9 %collective-permute-start.4 = (bf16[832,128]{1,0:T(8,128)(2,1)S(1)}, bf16[832,128]{1,0:T(8,128)(2,1)S(1)}, u32[]{:S(2)}, u32[]{:S(2)}) collective-permute-start(bf16[832,128]{1,0:T(8,128)(2,1)S(1)} %constant_dynamic-update-slice_fusion.refs_0_), channel_id=1, source_target_pairs={{0,16},{1,17},{2,18},{3,19},{4,20},{5,21},{6,22},{7,23},{8,24},{9,... | collective-permute-start | bytes 638984 | tf_op jit(solution)/shard_map/ppermute | solution.py:709
  15.6 10.4 %collective-permute-start.3 = (bf16[832,128]{1,0:T(8,128)(2,1)S(1)}, bf16[832,128]{1,0:T(8,128)(2,1)S(1)}, u32[]{:S(2)}, u32[]{:S(2)}) collective-permute-start(bf16[832,128]{1,0:T(8,128)(2,1)S(1)} %constant_dynamic-update-slice_fusion.refs_0_), channel_id=1, source_target_pairs={{0,17},{1,16},{2,19},{3,18},{4,21},{5,20},{6,23},{7,22},{8,25},{9,... | collective-permute-start | bytes 638984 | tf_op jit(solution)/shard_map/ppermute | solution.py:709
  16.1 10.4 %collective-permute-start.10 = (bf16[320,128]{1,0:T(8,128)(2,1)S(1)}, bf16[320,128]{1,0:T(8,128)(2,1)S(1)}, u32[]{:S(2)}, u32[]{:S(2)}) collective-permute-start(bf16[320,128]{1,0:T(8,128)(2,1)S(1)} %get-tuple-element.70), channel_id=1, source_target_pairs={{0,4},{1,5},{2,6},{3,7},{4,0},{5,1},{6,2},{7,3},{8,12},{9,13},{10,... | collective-permute-start | bytes 245768 | tf_op jit(solution)/shard_map/ppermute | solution.py:709
  20.6 6.9 %collective-permute-start.9 = (bf16[832,128]{1,0:T(8,128)(2,1)S(1)}, bf16[832,128]{1,0:T(8,128)(2,1)S(1)}, u32[]{:S(2)}, u32[]{:S(2)}) collective-permute-start(bf16[832,128]{1,0:T(8,128)(2,1)S(1)} %collective-permute-done.5.refs_3_), channel_id=1, source_target_pairs={{0,8},{1,9},{2,10},{3,11},{4,12},{5,13},{6,14},{7,15},{8,0},{9,1},... | collective-permute-start | bytes 638984 | tf_op jit(solution)/shard_map/ppermute | solution.py:709
  25.9 1.5 collective-permute-start.8
  26.0 1.8 %collective-permute-start.7 = (bf16[832,128]{1,0:T(8,128)(2,1)S(1)}, bf16[832,128]{1,0:T(8,128)(2,1)S(1)}, u32[]{:S(2)}, u32[]{:S(2)}) collective-permute-start(bf16[832,128]{1,0:T(8,128)(2,1)S(1)} %collective-permute-done.3.refs_1_), channel_id=1, source_target_pairs={{0,8},{1,9},{2,10},{3,11},{4,12},{5,13},{6,14},{7,15},{8,0},{9,1},... | collective-permute-start | bytes 638984 | tf_op jit(solution)/shard_map/ppermute | solution.py:709
  26.5 6.9 %collective-permute-start.11 = (bf16[640,128]{1,0:T(8,128)(2,1)S(1)}, bf16[640,128]{1,0:T(8,128)(2,1)S(1)}, u32[]{:S(2)}, u32[]{:S(2)}) collective-permute-start(bf16[640,128]{1,0:T(8,128)(2,1)S(1)} %pad_maximum_fusion.3), channel_id=1, source_target_pairs={{0,2},{1,3},{2,0},{3,1},{4,6},{5,7},{6,4},{7,5},{8,10},{9,11},{10,... | collective-permute-start | bytes 491528 | tf_op jit(solution)/shard_map/ppermute | solution.py:709
  33.5 17.0 %collective-permute-start.14 = (bf16[1280,128]{1,0:T(8,128)(2,1)S(1)}, bf16[1280,128]{1,0:T(8,128)(2,1)S(1)}, u32[]{:S(2)}, u32[]{:S(2)}) collective-permute-start(bf16[1280,128]{1,0:T(8,128)(2,1)S(1)} %constant_dynamic-update-slice_fusion.4.refs_0_), channel_id=1, source_target_pairs={{0,1},{1,0},{2,3},{3,2},{4,5},{5,4},{6,7},{7,6},{8,9},{9,8},{10,11... | collective-permute-start | bytes 983048 | tf_op jit(solution)/shard_map/ppermute | solution.py:709
  34.5 16.0 %collective-permute-start.13 = (bf16[1280,128]{1,0:T(8,128)(2,1)S(1)}, bf16[1280,128]{1,0:T(8,128)(2,1)S(1)}, u32[]{:S(2)}, u32[]{:S(2)}) collective-permute-start(bf16[1280,128]{1,0:T(8,128)(2,1)S(1)} %constant_dynamic-update-slice_fusion.4.refs_0_), channel_id=1, source_target_pairs={{0,16},{1,17},{2,18},{3,19},{4,20},{5,21},{6,22},{7,23},{8,24},{9,... | collective-permute-start | bytes 983048 | tf_op jit(solution)/shard_map/ppermute | solution.py:709
  35.6 15.7 %collective-permute-start.12 = (bf16[1280,128]{1,0:T(8,128)(2,1)S(1)}, bf16[1280,128]{1,0:T(8,128)(2,1)S(1)}, u32[]{:S(2)}, u32[]{:S(2)}) collective-permute-start(bf16[1280,128]{1,0:T(8,128)(2,1)S(1)} %constant_dynamic-update-slice_fusion.4.refs_0_), channel_id=1, source_target_pairs={{0,17},{1,16},{2,19},{3,18},{4,21},{5,20},{6,23},{7,22},{8,25},{9,... | collective-permute-start | bytes 983048 | tf_op jit(solution)/shard_map/ppermute | solution.py:709
  50.4 5.9 %collective-permute-start.15 = (bf16[1280,128]{1,0:T(8,128)(2,1)S(1)}, bf16[1280,128]{1,0:T(8,128)(2,1)S(1)}, u32[]{:S(2)}, u32[]{:S(2)}) collective-permute-start(bf16[1280,128]{1,0:T(8,128)(2,1)S(1)} %constant_dynamic-update-slice_fusion.4.refs_0_), channel_id=1, source_target_pairs={{0,8},{1,9},{2,10},{3,11},{4,12},{5,13},{6,14},{7,15},{8,0},{9,1},... | collective-permute-start | bytes 983048 | tf_op jit(solution)/shard_map/ppermute | solution.py:709
  51.3 5.0 %collective-permute-start.16 = (bf16[1280,128]{1,0:T(8,128)(2,1)S(1)}, bf16[1280,128]{1,0:T(8,128)(2,1)S(1)}, u32[]{:S(2)}, u32[]{:S(2)}) collective-permute-start(bf16[1280,128]{1,0:T(8,128)(2,1)S(1)} %collective-permute-done.12.refs_1_), channel_id=1, source_target_pairs={{0,8},{1,9},{2,10},{3,11},{4,12},{5,13},{6,14},{7,15},{8,0},{9,1},... | collective-permute-start | bytes 983048 | tf_op jit(solution)/shard_map/ppermute | solution.py:709
  51.3 5.0 %collective-permute-start.17 = (bf16[1280,128]{1,0:T(8,128)(2,1)S(1)}, bf16[1280,128]{1,0:T(8,128)(2,1)S(1)}, u32[]{:S(2)}, u32[]{:S(2)}) collective-permute-start(bf16[1280,128]{1,0:T(8,128)(2,1)S(1)} %collective-permute-done.13.refs_2_), channel_id=1, source_target_pairs={{0,8},{1,9},{2,10},{3,11},{4,12},{5,13},{6,14},{7,15},{8,0},{9,1},... | collective-permute-start | bytes 983048 | tf_op jit(solution)/shard_map/ppermute | solution.py:709
  51.8 4.5 %collective-permute-start.18 = (bf16[1280,128]{1,0:T(8,128)(2,1)S(1)}, bf16[1280,128]{1,0:T(8,128)(2,1)S(1)}, u32[]{:S(2)}, u32[]{:S(2)}) collective-permute-start(bf16[1280,128]{1,0:T(8,128)(2,1)S(1)} %collective-permute-done.14.refs_3_), channel_id=1, source_target_pairs={{0,8},{1,9},{2,10},{3,11},{4,12},{5,13},{6,14},{7,15},{8,0},{9,1},... | collective-permute-start | bytes 983048 | tf_op jit(solution)/shard_map/ppermute | solution.py:709
  51.8 4.5 %copy-start = (bf16[2048,512]{1,0:T(8,128)(2,1)S(1)}, bf16[2048,512]{1,0:T(8,128)(2,1)}, u32[]{:S(2)}) copy-start(bf16[2048,512]{1,0:T(8,128)(2,1)} %cotangent.1) | copy-start | bytes 6291460
  51.8 4.5 %copy-start.1 = (bf16[2048,512]{1,0:T(8,128)(2,1)S(1)}, bf16[2048,512]{1,0:T(8,128)(2,1)}, u32[]{:S(2)}) copy-start(bf16[2048,512]{1,0:T(8,128)(2,1)} %tokens.9) | copy-start | bytes 6291460
  82.3 13.0 %collective-permute-start.20 = (bf16[5120,128]{1,0:T(8,128)(2,1)S(1)}, bf16[5120,128]{1,0:T(8,128)(2,1)S(1)}, u32[]{:S(2)}, u32[]{:S(2)}) collective-permute-start(bf16[5120,128]{1,0:T(8,128)(2,1)S(1)} %get-tuple-element.91), channel_id=1, source_target_pairs={{0,8},{1,9},{2,10},{3,11},{4,12},{5,13},{6,14},{7,15},{8,0},{9,1},... | collective-permute-start | bytes 3932168 | tf_op jit(solution)/shard_map/ppermute | solution.py:709
  95.3 43.4 %collective-permute-start.19 = (bf16[768,128]{1,0:T(8,128)(2,1)S(1)}, bf16[768,128]{1,0:T(8,128)(2,1)S(1)}, u32[]{:S(2)}, u32[]{:S(2)}) collective-permute-start(bf16[768,128]{1,0:T(8,128)(2,1)S(1)} %get-tuple-element.88), channel_id=1, source_target_pairs={{0,8},{1,9},{2,10},{3,11},{4,12},{5,13},{6,14},{7,15},{8,0},{9,1},... | collective-permute-start | bytes 589832 | tf_op jit(solution)/shard_map/ppermute | solution.py:709
  95.6 28.6 %collective-permute-start.23 = (bf16[1280,128]{1,0:T(8,128)(2,1)S(1)}, bf16[1280,128]{1,0:T(8,128)(2,1)S(1)}, u32[]{:S(2)}, u32[]{:S(2)}) collective-permute-start(bf16[1280,128]{1,0:T(8,128)(2,1)S(1)} %get-tuple-element.126), channel_id=1, source_target_pairs={{0,17},{1,16},{2,19},{3,18},{4,21},{5,20},{6,23},{7,22},{8,25},{9,... | collective-permute-start | bytes 983048 | tf_op jit(solution)/shard_map/ppermute | solution.py:709
  97.4 26.8 %collective-permute-start.22 = (bf16[1280,128]{1,0:T(8,128)(2,1)S(1)}, bf16[1280,128]{1,0:T(8,128)(2,1)S(1)}, u32[]{:S(2)}, u32[]{:S(2)}) collective-permute-start(bf16[1280,128]{1,0:T(8,128)(2,1)S(1)} %get-tuple-element.127), channel_id=1, source_target_pairs={{0,16},{1,17},{2,18},{3,19},{4,20},{5,21},{6,22},{7,23},{8,24},{9,... | collective-permute-start | bytes 983048 | tf_op jit(solution)/shard_map/ppermute | solution.py:709
  97.9 26.3 %collective-permute-start.21 = (bf16[1280,128]{1,0:T(8,128)(2,1)S(1)}, bf16[1280,128]{1,0:T(8,128)(2,1)S(1)}, u32[]{:S(2)}, u32[]{:S(2)}) collective-permute-start(bf16[1280,128]{1,0:T(8,128)(2,1)S(1)} %get-tuple-element.128), channel_id=1, source_target_pairs={{0,1},{1,0},{2,3},{3,2},{4,5},{5,4},{6,7},{7,6},{8,9},{9,8},{10,11... | collective-permute-start | bytes 983048 | tf_op jit(solution)/shard_map/ppermute | solution.py:709
  124.1 14.9 %collective-permute-start.24 = (bf16[1536,128]{1,0:T(8,128)(2,1)S(1)}, bf16[1536,128]{1,0:T(8,128)(2,1)S(1)}, u32[]{:S(2)}, u32[]{:S(2)}) collective-permute-start(bf16[1536,128]{1,0:T(8,128)(2,1)S(1)} %get-tuple-element.104), channel_id=1, source_target_pairs={{0,8},{1,9},{2,10},{3,11},{4,12},{5,13},{6,14},{7,15},{8,0},{9,1},... | collective-permute-start | bytes 1179656 | tf_op jit(solution)/shard_map/ppermute | solution.py:709
  124.5 14.6 %collective-permute-start.32 = (bf16[640,128]{1,0:T(8,128)(2,1)S(1)}, bf16[640,128]{1,0:T(8,128)(2,1)S(1)}, u32[]{:S(2)}, u32[]{:S(2)}) collective-permute-start(bf16[640,128]{1,0:T(8,128)(2,1)S(1)} %slice.258), channel_id=1, source_target_pairs={{0,2},{1,3},{2,0},{3,1},{4,6},{5,7},{6,4},{7,5},{8,10},{9,11},{10,... | collective-permute-start | bytes 491528 | tf_op jit(solution)/shard_map/ppermute | solution.py:709
  138.7 1.6 collective-permute-start.25
  140.4 11.2 %collective-permute-start.26 = (bf16[832,128]{1,0:T(8,128)(2,1)S(1)}, bf16[832,128]{1,0:T(8,128)(2,1)S(1)}, u32[]{:S(2)}, u32[]{:S(2)}) collective-permute-start(bf16[832,128]{1,0:T(8,128)(2,1)S(1)} %bitcast.50), channel_id=1, source_target_pairs={{0,1},{1,0},{2,3},{3,2},{4,5},{5,4},{6,7},{7,6},{8,9},{9,8},{10,11... | collective-permute-start | bytes 638984 | tf_op jit(solution)/shard_map/ppermute | solution.py:709
  141.2 10.8 %collective-permute-start.27 = (bf16[832,128]{1,0:T(8,128)(2,1)S(1)}, bf16[832,128]{1,0:T(8,128)(2,1)S(1)}, u32[]{:S(2)}, u32[]{:S(2)}) collective-permute-start(bf16[832,128]{1,0:T(8,128)(2,1)S(1)} %bitcast.52), channel_id=1, source_target_pairs={{0,16},{1,17},{2,18},{3,19},{4,20},{5,21},{6,22},{7,23},{8,24},{9,... | collective-permute-start | bytes 638984 | tf_op jit(solution)/shard_map/ppermute | solution.py:709
  142.8 10.2 %collective-permute-start.28 = (bf16[832,128]{1,0:T(8,128)(2,1)S(1)}, bf16[832,128]{1,0:T(8,128)(2,1)S(1)}, u32[]{:S(2)}, u32[]{:S(2)}) collective-permute-start(bf16[832,128]{1,0:T(8,128)(2,1)S(1)} %bitcast.53), channel_id=1, source_target_pairs={{0,17},{1,16},{2,19},{3,18},{4,21},{5,20},{6,23},{7,22},{8,25},{9,... | collective-permute-start | bytes 638984 | tf_op jit(solution)/shard_map/ppermute | solution.py:709
  149.5 8.1 %collective-permute-start.33 = (bf16[320,128]{1,0:T(8,128)(2,1)S(1)}, bf16[320,128]{1,0:T(8,128)(2,1)S(1)}, u32[]{:S(2)}, u32[]{:S(2)}) collective-permute-start(bf16[320,128]{1,0:T(8,128)(2,1)S(1)} %slice.259), channel_id=1, source_target_pairs={{0,4},{1,5},{2,6},{3,7},{4,0},{5,1},{6,2},{7,3},{8,12},{9,13},{10,... | collective-permute-start | bytes 245768 | tf_op jit(solution)/shard_map/ppermute | solution.py:709
  153.1 6.0 %collective-permute-start.31 = (bf16[208,128]{1,0:T(8,128)(2,1)S(1)}, bf16[208,128]{1,0:T(8,128)(2,1)S(1)}, u32[]{:S(2)}, u32[]{:S(2)}) collective-permute-start(bf16[208,128]{1,0:T(8,128)(2,1)S(1)} %get-tuple-element.141), channel_id=1, source_target_pairs={{0,6},{1,7},{2,4},{3,5},{4,2},{5,3},{6,0},{7,1},{8,14},{9,15},{10,... | collective-permute-start | bytes 159752 | tf_op jit(solution)/shard_map/ppermute | solution.py:709
  155.8 5.3 %collective-permute-start.30 = (bf16[208,128]{1,0:T(8,128)(2,1)S(1)}, bf16[208,128]{1,0:T(8,128)(2,1)S(1)}, u32[]{:S(2)}, u32[]{:S(2)}) collective-permute-start(bf16[208,128]{1,0:T(8,128)(2,1)S(1)} %get-tuple-element.142), channel_id=1, source_target_pairs={{0,4},{1,5},{2,6},{3,7},{4,0},{5,1},{6,2},{7,3},{8,12},{9,13},{10,... | collective-permute-start | bytes 159752 | tf_op jit(solution)/shard_map/ppermute | solution.py:709
  155.8 5.3 %collective-permute-start.29 = (bf16[208,128]{1,0:T(8,128)(2,1)S(1)}, bf16[208,128]{1,0:T(8,128)(2,1)S(1)}, u32[]{:S(2)}, u32[]{:S(2)}) collective-permute-start(bf16[208,128]{1,0:T(8,128)(2,1)S(1)} %get-tuple-element.143), channel_id=1, source_target_pairs={{0,2},{1,3},{2,0},{3,1},{4,6},{5,7},{6,4},{7,5},{8,10},{9,11},{10,... | collective-permute-start | bytes 159752 | tf_op jit(solution)/shard_map/ppermute | solution.py:709
where the time goes:
time: 162 us
  Pallas kernels  107 us (66%)
  starting transfers between devices  32.6 us (20%)
  waiting for transfers between devices  17.4 us (11%)
  other arithmetic  2.68 us (2%)
    pallas_call x3, Pallas kernels, attend_back(): pl.pallas_call(functools.partial(attend_back_kernel, base, heads, order,...  50.6 us
    ppermute x34, starting transfers between devices, swap(): return lax.ppermute(array, AXES, [(i, i ^ step) for i in range(count)])  32.6 us
    pallas_call x1, Pallas kernels, middle(): pl.pallas_call(functools.partial(middle_kernel, masks, order_in, order_ou...  26 us
    pallas_call x2, Pallas kernels, attend(): pl.pallas_call(functools.partial(attend_kernel, base), grid=(heads, count...  17.8 us
    ppermute x34, waiting for transfers between devices, swap(): return lax.ppermute(array, AXES, [(i, i ^ step) for i in range(count)])  17.4 us
    pallas_call x1, Pallas kernels, project(): pl.pallas_call(functools.partial(project_kernel, masks, order, vec_width)...  5.69 us
    pallas_call x1, Pallas kernels, input_grad(): pl.pallas_call(functools.partial(input_grad_kernel, len(queries)), grid=(...  5.46 us
  transfers between devices with their start and end apart: 34, of which 11 were waited for; matrix products, arithmetic and copies ran while one was open for 2% of the time, Pallas kernels for 49%

commit v1 on v0

--- a/solution.py
+++ b/solution.py
@@ -419,7 +419,7 @@
                     ].astype(bf16)
                 return 0
 
-            lax.fori_loop(0, half, place, 0, unroll=4)
+            lax.fori_loop(0, half, place, 0, unroll=True)
         vec_out[...] = jnp.zeros_like(vec_out)
         for i in range(6):
             row = jnp.sum(sums[i], axis=0, keepdims=True)
@@ -567,9 +567,10 @@
         grad_query[...] = gq_all
         gk_all = jnp.concatenate([all_keys[i] for i in range(all_keys.shape[0])], axis=1)
         gv_all = jnp.concatenate([all_values[i] for i in range(all_values.shape[0])], axis=1)
-        grad_weight[0:512, :] = dot(gq_all, x, TN).T * scale
-        grad_weight[512:1024, :] = dot(gk_all, x, NN).T
-        grad_weight[1024:1536, :] = dot(gv_all, x, NN).T
+        sums = dot(jnp.concatenate([gq_all.T, gk_all, gv_all], axis=0), x, NN)
+        grad_weight[0:512, :] = (sums[0:128].T * scale).astype(bf16)
+        grad_weight[512:1024, :] = sums[128:256].T.astype(bf16)
+        grad_weight[1024:1536, :] = sums[256:384].T.astype(bf16)
         row_ones = jnp.ones((8, x.shape[0]), bf16)
         vec[pl.ds(base + local, 1), :] = dot(row_ones, gq_all, NN)[0:1] * scale
         vec[pl.ds(4 + base + local, 1), :] = dot(row_ones, gv_all, NT)[0:1]
@@ -581,14 +582,14 @@
                 d = owner_of(start + i, me, order)
                 ref[pl.ds(pl.multiple_of(i * block + local * QKV_ROWS, 16), QKV_ROWS), :] = grad_weight[
                     pl.ds(pl.multiple_of(d * QKV_ROWS, 16), QKV_ROWS), :
-                ].astype(bf16)
+                ]
                 if last:
                     pair = vec[pl.ds((d * vec_width) // 128, 2), :]
                     pair = jnp.concatenate([pair, jnp.zeros((14, 128), f32)], axis=0)
                     ref[pl.ds(pl.multiple_of(i * block + heads * QKV_ROWS, 16), 16), :] = pair.astype(bf16)
                 return 0
 
-            lax.fori_loop(0, half, place, 0, unroll=4)
+            lax.fori_loop(0, half, place, 0, unroll=True)
 
 
 def attend_back(
@@ -631,7 +632,7 @@
             pltpu.VMEM((count, 128), f32),
             pltpu.VMEM((count // width, 128, width), bf16),
             pltpu.VMEM((count // width, 128, width), bf16),
-            pltpu.VMEM((1536, 128), f32),
+            pltpu.VMEM((1536, 128), bf16),
             pltpu.VMEM((count, 512), bf16),
             pltpu.SemaphoreType.DMA,
         ],
@@ -654,7 +655,7 @@
     out[...] = total + dot(gv, weight[1024:1536, :], TT)
 
 
-def input_grad(grad_branch, queries, keys, values, weight, rows=512):
+def input_grad(grad_branch, queries, keys, values, weight, rows=1024):
     count = grad_branch.shape[0]
     by_row = pl.BlockSpec((rows, 512), lambda i: (i, 0))
     return pl.pallas_call(

time: 162 us -> 161 us (level)
  no operation moved by 1% of the time
where the time goes in v1:
time: 161 us; the launch traced here: 160 us
  Pallas kernels  106 us (66%)
  starting transfers between devices  32.6 us (20%)
  waiting for transfers between devices  17.4 us (11%)
  other arithmetic  2.68 us (2%)
    pallas_call x3, Pallas kernels, attend_back(): pl.pallas_call(functools.partial(attend_back_kernel, base, heads, order,...  49.6 us
    ppermute x34, starting transfers between devices, swap(): return lax.ppermute(array, AXES, [(i, i ^ step) for i in range(count)])  32.6 us
    pallas_call x1, Pallas kernels, middle(): pl.pallas_call(functools.partial(middle_kernel, masks, order_in, order_ou...  25.3 us
    pallas_call x2, Pallas kernels, attend(): pl.pallas_call(functools.partial(attend_kernel, base), grid=(heads, count...  17.8 us
    ppermute x34, waiting for transfers between devices, swap(): return lax.ppermute(array, AXES, [(i, i ^ step) for i in range(count)])  17.4 us
    pallas_call x1, Pallas kernels, project(): pl.pallas_call(functools.partial(project_kernel, masks, order, vec_width)...  5.69 us
    pallas_call x1, Pallas kernels, input_grad(): pl.pallas_call(functools.partial(input_grad_kernel, len(queries)), grid=(...  5.42 us
  transfers between devices with their start and end apart: 34, of which 11 were waited for; matrix products, arithmetic and copies ran while one was open for 2% of the time, Pallas kernels for 49%

profile of v1, /device:TPU:0, one launch (start us, length us, event | category | flops | bytes accessed | tf_op | source)
XLA Modules:
  0.0 160.3 jit_solution(14735899339657544637)
XLA Ops:
  0.6 0.7 reshape.215.vec
  1.3 1.0 pack.1
  2.3 5.1 %collective-permute-start.2 = (bf16[208,128]{1,0:T(8,128)(2,1)S(1)}, bf16[208,128]{1,0:T(8,128)(2,1)S(1)}, u32[]{:S(2)}, u32[]{:S(2)}) collective-permute-start(bf16[208,128]{1,0:T(8,128)(2,1)S(1)} %get-tuple-element.64), channel_id=1, source_target_pairs={{0,6},{1,7},{2,4},{3,5},{4,2},{5,3},{6,0},{7,1},{8,14},{9,15},{10,... | collective-permute-start | bytes 159752 | tf_op jit(solution)/shard_map/ppermute | solution.py:710
  7.4 0.6 collective-permute-start
  8.0 0.7 select_bitcast_fusion
  8.7 0.3 reduce-window.9
  9.2 0.8 bitcast_select_fusion
  10.0 1.5 collective-permute-done
  11.5 0.9 collective-permute-done.1
  12.5 1.6 collective-permute-start.5
  14.1 1.5 collective-permute-start.4
  15.6 0.5 collective-permute-start.3
  16.1 2.1 %collective-permute-start.10 = (bf16[320,128]{1,0:T(8,128)(2,1)S(1)}, bf16[320,128]{1,0:T(8,128)(2,1)S(1)}, u32[]{:S(2)}, u32[]{:S(2)}) collective-permute-start(bf16[320,128]{1,0:T(8,128)(2,1)S(1)} %get-tuple-element.70), channel_id=1, source_target_pairs={{0,4},{1,5},{2,6},{3,7},{4,0},{5,1},{6,2},{7,3},{8,12},{9,13},{10,... | collective-permute-start | bytes 245768 | tf_op jit(solution)/shard_map/ppermute | solution.py:710
  18.1 2.5 %collective-permute-done.5.refs_3_ = bf16[832,128]{1,0:T(8,128)(2,1)S(1)} collective-permute-done((bf16[832,128]{1,0:T(8,128)(2,1)S(1)}, bf16[832,128]{1,0:T(8,128)(2,1)S(1)}, u32[]{:S(2)}, u32[]{:S(2)}) %collective-permute-start.5) | collective-permute-done | bytes 213024 | tf_op jit(solution)/shard_map/ppermute | solution.py:710
  20.6 5.3 %collective-permute-done.4.refs_2_ = bf16[832,128]{1,0:T(8,128)(2,1)S(1)} collective-permute-done((bf16[832,128]{1,0:T(8,128)(2,1)S(1)}, bf16[832,128]{1,0:T(8,128)(2,1)S(1)}, u32[]{:S(2)}, u32[]{:S(2)}) %collective-permute-start.4) | collective-permute-done | bytes 213024 | tf_op jit(solution)/shard_map/ppermute | solution.py:710
  26.0 0.5 collective-permute-start.7
  26.5 1.0 collective-permute-start.11
  27.7 5.7 %project.1 = (bf16[2048,1536]{1,0:T(8,128)(2,1)S(1)}, bf16[2048,128]{1,0:T(8,128)(2,1)S(1)}, bf16[2048,128]{1,0:T(8,128)(2,1)S(1)}, f32[48,128]{1,0:T(8,128)S(1)}, bf16[1536,512]{1,0:T(8,128)(2,1)S(1)}) custom-call(s32[1]{0:T(128)} %bitcast.me_ref, s32[1,256]{1,0:T(1,128)S(1)} %bitcast.38, bf16[2048,512]{1,0:T(8,128)(2,1)} %tokens.9, ...), custom_call_target="tpu_custom_call" | custom-call | flops 3221225472 | bytes 12000000 | tf_op jit(solution)/shard_map/project/pallas_call | solution.py:147
  33.5 1.0 collective-permute-start.14
  34.5 1.1 collective-permute-start.13
  35.6 1.4 collective-permute-start.12
  37.0 13.3 %attend.2 = (bf16[2048,512]{1,0:T(8,128)(2,1)S(1)}, f32[4,1,2048]{2,1,0:T(1,128)S(1)}) custom-call(bf16[2048,1536]{1,0:T(8,128)(2,1)S(1)} %get-tuple-element.66.q.k.v, bf16[2048,1536]{1,0:T(8,128)(2,1)S(1)} %get-tuple-element.66.q.k.v, bf16[2048,1536]{1,0:T(8,128)(2,1)S(1)} %get-tuple-element.66.q.k.v, bf16[2048,128]{1,0:T(8,128)(2,1)S(1)} %get-tuple-element.67.query_extra, ...), custom_call_target="tpu_custom_call" | custom-call | flops 12884901888 | bytes 6000000 | tf_op jit(solution)/shard_map/attend/pallas_call | solution.py:217
  50.5 0.9 collective-permute-done.12.refs_1_
  51.3 0.5 collective-permute-start.17
  51.8 4.5 %attend.3 = (bf16[2048,512]{1,0:T(8,128)(2,1)S(1)}, f32[4,1,2048]{2,1,0:T(1,128)S(1)}) custom-call(bf16[2048,1536]{1,0:T(8,128)(2,1)S(1)} %get-tuple-element.66.q.k.v, bf16[2048,1536]{1,0:T(8,128)(2,1)S(1)} %get-tuple-element.66.q.k.v, bf16[2048,1536]{1,0:T(8,128)(2,1)S(1)} %get-tuple-element.66.q.k.v, ...), custom_call_target="tpu_custom_call", output_to_operand_aliasing={{0}: (5, {}), {1}: (6, {})} | custom-call | flops 4294967296 | bytes 6000000 | tf_op jit(solution)/shard_map/attend/pallas_call | solution.py:217
  56.4 25.3 %middle.1 = (bf16[2048,512]{1,0:T(8,128)(2,1)}, bf16[2048,512]{1,0:T(8,128)(2,1)S(1)}, bf16[2048,512]{1,0:T(8,128)(2,1)S(1)}, bf16[2048,128]{1,0:T(8,128)(2,1)S(...) custom-call(s32[1]{0:T(128)} %bitcast.me_ref, ...), custom_call_target="tpu_custom_call" | custom-call | flops 16106127360 | bytes 22000000 | tf_op jit(solution)/shard_map/middle/pallas_call | solution.py:439
  81.7 0.5 collective-permute-start.20
  82.2 12.2 %attend_back.3 = (bf16[2048,128]{1,0:T(8,128)(2,1)S(1)}, bf16[128,2048]{1,0:T(8,128)(2,1)S(1)}, bf16[128,2048]{1,0:T(8,128)(2,1)S(1)}, bf16[768,128]{1,0:T(8,128...) custom-call(s32[1]{0:T(128)} %bitcast.me_ref, bf16[2048,512]{1,0:T(8,128)(2,1)S(1)} %copy-done.1, ...), custom_call_target="tpu_custom_call" | custom-call | flops 10737418240 | bytes 12000000 | tf_op jit(solution)/shard_map/attend_back/pallas_call | solution.py:600
  94.7 1.8 %collective-permute-start.23 = (bf16[1280,128]{1,0:T(8,128)(2,1)S(1)}, bf16[1280,128]{1,0:T(8,128)(2,1)S(1)}, u32[]{:S(2)}, u32[]{:S(2)}) collective-permute-start(bf16[1280,128]{1,0:T(8,128)(2,1)S(1)} %get-tuple-element.126), channel_id=1, source_target_pairs={{0,17},{1,16},{2,19},{3,18},{4,21},{5,20},{6,23},{7,22},{8,25},{9,... | collective-permute-start | bytes 983048 | tf_op jit(solution)/shard_map/ppermute | solution.py:710
  96.6 0.5 collective-permute-start.22
  97.1 1.2 collective-permute-start.21
  98.3 24.5 %attend_back.4 = (bf16[2048,256]{1,0:T(8,128)(2,1)S(1)}, bf16[256,2048]{1,0:T(8,128)(2,1)S(1)}, bf16[256,2048]{1,0:T(8,128)(2,1)S(1)}, bf16[1536,128]{1,0:T(8,12...) custom-call(s32[1]{0:T(128)} %bitcast.me_ref, bf16[2048,512]{1,0:T(8,128)(2,1)S(1)} %copy-done.1, ...), custom_call_target="tpu_custom_call" | custom-call | flops 21474836480 | bytes 24000000 | tf_op jit(solution)/shard_map/attend_back/pallas_call | solution.py:600
  123.1 1.0 collective-permute-start.32
  124.1 12.9 %attend_back.5 = (bf16[2048,128]{1,0:T(8,128)(2,1)S(1)}, bf16[128,2048]{1,0:T(8,128)(2,1)S(1)}, bf16[128,2048]{1,0:T(8,128)(2,1)S(1)}, bf16[1024,128]{1,0:T(8,12...) custom-call(s32[1]{0:T(128)} %bitcast.me_ref, bf16[2048,512]{1,0:T(8,128)(2,1)S(1)} %copy-done.1, ...), custom_call_target="tpu_custom_call" | custom-call | flops 10737418240 | bytes 12000000 | tf_op jit(solution)/shard_map/attend_back/pallas_call | solution.py:600
  137.0 0.3 collective-permute-start.25
  137.5 1.1 collective-permute-done.25
  138.7 0.9 collective-permute-start.26
  139.6 1.6 collective-permute-start.27
  141.2 1.2 collective-permute-start.28
  142.4 5.4 %input_grad.1 = f32[2048,512]{1,0:T(8,128)} custom-call(bf16[2048,512]{1,0:T(8,128)(2,1)S(1)} %get-tuple-element.109.refs_0_, bf16[2048,128]{1,0:T(8,128)(2,1)S(1)} %get-tuple-element.92.refs_1_, bf16[2048,256]{1,0:T(8,128)(2,1)S(1)} %get-tuple-element.96.refs_2_, bf16[2048,128]{1,0:T(8,128)(2,1)S(1)} %get-tuple-element.101.refs_3_, ...), custom_call_target="tpu_custom_call" | custom-call | flops 3221225472 | bytes 16000000 | tf_op jit(solution)/shard_map/input_grad/pallas_call | solution.py:661
  147.8 2.0 %collective-permute-start.33 = (bf16[320,128]{1,0:T(8,128)(2,1)S(1)}, bf16[320,128]{1,0:T(8,128)(2,1)S(1)}, u32[]{:S(2)}, u32[]{:S(2)}) collective-permute-start(bf16[320,128]{1,0:T(8,128)(2,1)S(1)} %slice.259), channel_id=1, source_target_pairs={{0,4},{1,5},{2,6},{3,7},{4,0},{5,1},{6,2},{7,3},{8,12},{9,13},{10,... | collective-permute-start | bytes 245768 | tf_op jit(solution)/shard_map/ppermute | solution.py:710
  149.9 0.5 collective-permute-done.27
  150.4 1.0 collective-permute-done.28
  151.5 2.7 %collective-permute-start.31 = (bf16[208,128]{1,0:T(8,128)(2,1)S(1)}, bf16[208,128]{1,0:T(8,128)(2,1)S(1)}, u32[]{:S(2)}, u32[]{:S(2)}) collective-permute-start(bf16[208,128]{1,0:T(8,128)(2,1)S(1)} %get-tuple-element.141), channel_id=1, source_target_pairs={{0,6},{1,7},{2,4},{3,5},{4,2},{5,3},{6,0},{7,1},{8,14},{9,15},{10,... | collective-permute-start | bytes 159752 | tf_op jit(solution)/shard_map/ppermute | solution.py:710
  154.2 1.8 %collective-permute-start.29 = (bf16[208,128]{1,0:T(8,128)(2,1)S(1)}, bf16[208,128]{1,0:T(8,128)(2,1)S(1)}, u32[]{:S(2)}, u32[]{:S(2)}) collective-permute-start(bf16[208,128]{1,0:T(8,128)(2,1)S(1)} %get-tuple-element.143), channel_id=1, source_target_pairs={{0,2},{1,3},{2,0},{3,1},{4,6},{5,7},{6,4},{7,5},{8,10},{9,11},{10,... | collective-permute-start | bytes 159752 | tf_op jit(solution)/shard_map/ppermute | solution.py:710
  156.0 1.5 collective-permute-done.31.refs_3_
  157.5 2.0 %collective-permute-done.30.refs_2_ = bf16[208,128]{1,0:T(8,128)(2,1)S(1)} collective-permute-done((bf16[208,128]{1,0:T(8,128)(2,1)S(1)}, bf16[208,128]{1,0:T(8,128)(2,1)S(1)}, u32[]{:S(2)}, u32[]{:S(2)}) %collective-permute-start.30) | collective-permute-done | bytes 53280 | tf_op jit(solution)/shard_map/ppermute | solution.py:710
  159.5 0.8 unpack.1
  (64 shorter events, 1.9 us)
Async XLA Ops:
  2.3 9.2 %collective-permute-start.2 = (bf16[208,128]{1,0:T(8,128)(2,1)S(1)}, bf16[208,128]{1,0:T(8,128)(2,1)S(1)}, u32[]{:S(2)}, u32[]{:S(2)}) collective-permute-start(bf16[208,128]{1,0:T(8,128)(2,1)S(1)} %get-tuple-element.64), channel_id=1, source_target_pairs={{0,6},{1,7},{2,4},{3,5},{4,2},{5,3},{6,0},{7,1},{8,14},{9,15},{10,... | collective-permute-start | bytes 159752 | tf_op jit(solution)/shard_map/ppermute | solution.py:710
  7.4 5.0 %collective-permute-start.1 = (bf16[208,128]{1,0:T(8,128)(2,1)S(1)}, bf16[208,128]{1,0:T(8,128)(2,1)S(1)}, u32[]{:S(2)}, u32[]{:S(2)}) collective-permute-start(bf16[208,128]{1,0:T(8,128)(2,1)S(1)} %get-tuple-element.64), channel_id=1, source_target_pairs={{0,4},{1,5},{2,6},{3,7},{4,0},{5,1},{6,2},{7,3},{8,12},{9,13},{10,... | collective-permute-start | bytes 159752 | tf_op jit(solution)/shard_map/ppermute | solution.py:710
  7.4 4.1 %collective-permute-start = (bf16[208,128]{1,0:T(8,128)(2,1)S(1)}, bf16[208,128]{1,0:T(8,128)(2,1)S(1)}, u32[]{:S(2)}, u32[]{:S(2)}) collective-permute-start(bf16[208,128]{1,0:T(8,128)(2,1)S(1)} %get-tuple-element.64), channel_id=1, source_target_pairs={{0,2},{1,3},{2,0},{3,1},{4,6},{5,7},{6,4},{7,5},{8,10},{9,11},{10,... | collective-permute-start | bytes 159752 | tf_op jit(solution)/shard_map/ppermute | solution.py:710
  12.4 3.6 %collective-permute-start.6 = (bf16[832,128]{1,0:T(8,128)(2,1)S(1)}, bf16[832,128]{1,0:T(8,128)(2,1)S(1)}, u32[]{:S(2)}, u32[]{:S(2)}) collective-permute-start(bf16[832,128]{1,0:T(8,128)(2,1)S(1)} %constant_dynamic-update-slice_fusion.refs_0_), channel_id=1, source_target_pairs={{0,8},{1,9},{2,10},{3,11},{4,12},{5,13},{6,14},{7,15},{8,0},{9,1},... | collective-permute-start | bytes 638984 | tf_op jit(solution)/shard_map/ppermute | solution.py:710
  12.5 8.1 %collective-permute-start.5 = (bf16[832,128]{1,0:T(8,128)(2,1)S(1)}, bf16[832,128]{1,0:T(8,128)(2,1)S(1)}, u32[]{:S(2)}, u32[]{:S(2)}) collective-permute-start(bf16[832,128]{1,0:T(8,128)(2,1)S(1)} %constant_dynamic-update-slice_fusion.refs_0_), channel_id=1, source_target_pairs={{0,1},{1,0},{2,3},{3,2},{4,5},{5,4},{6,7},{7,6},{8,9},{9,8},{10,11... | collective-permute-start | bytes 638984 | tf_op jit(solution)/shard_map/ppermute | solution.py:710
  14.1 11.9 %collective-permute-start.4 = (bf16[832,128]{1,0:T(8,128)(2,1)S(1)}, bf16[832,128]{1,0:T(8,128)(2,1)S(1)}, u32[]{:S(2)}, u32[]{:S(2)}) collective-permute-start(bf16[832,128]{1,0:T(8,128)(2,1)S(1)} %constant_dynamic-update-slice_fusion.refs_0_), channel_id=1, source_target_pairs={{0,16},{1,17},{2,18},{3,19},{4,20},{5,21},{6,22},{7,23},{8,24},{9,... | collective-permute-start | bytes 638984 | tf_op jit(solution)/shard_map/ppermute | solution.py:710
  15.6 10.4 %collective-permute-start.3 = (bf16[832,128]{1,0:T(8,128)(2,1)S(1)}, bf16[832,128]{1,0:T(8,128)(2,1)S(1)}, u32[]{:S(2)}, u32[]{:S(2)}) collective-permute-start(bf16[832,128]{1,0:T(8,128)(2,1)S(1)} %constant_dynamic-update-slice_fusion.refs_0_), channel_id=1, source_target_pairs={{0,17},{1,16},{2,19},{3,18},{4,21},{5,20},{6,23},{7,22},{8,25},{9,... | collective-permute-start | bytes 638984 | tf_op jit(solution)/shard_map/ppermute | solution.py:710
  16.1 10.4 %collective-permute-start.10 = (bf16[320,128]{1,0:T(8,128)(2,1)S(1)}, bf16[320,128]{1,0:T(8,128)(2,1)S(1)}, u32[]{:S(2)}, u32[]{:S(2)}) collective-permute-start(bf16[320,128]{1,0:T(8,128)(2,1)S(1)} %get-tuple-element.70), channel_id=1, source_target_pairs={{0,4},{1,5},{2,6},{3,7},{4,0},{5,1},{6,2},{7,3},{8,12},{9,13},{10,... | collective-permute-start | bytes 245768 | tf_op jit(solution)/shard_map/ppermute | solution.py:710
  20.6 6.9 %collective-permute-start.9 = (bf16[832,128]{1,0:T(8,128)(2,1)S(1)}, bf16[832,128]{1,0:T(8,128)(2,1)S(1)}, u32[]{:S(2)}, u32[]{:S(2)}) collective-permute-start(bf16[832,128]{1,0:T(8,128)(2,1)S(1)} %collective-permute-done.5.refs_3_), channel_id=1, source_target_pairs={{0,8},{1,9},{2,10},{3,11},{4,12},{5,13},{6,14},{7,15},{8,0},{9,1},... | collective-permute-start | bytes 638984 | tf_op jit(solution)/shard_map/ppermute | solution.py:710
  25.9 1.5 collective-permute-start.8
  26.0 1.8 %collective-permute-start.7 = (bf16[832,128]{1,0:T(8,128)(2,1)S(1)}, bf16[832,128]{1,0:T(8,128)(2,1)S(1)}, u32[]{:S(2)}, u32[]{:S(2)}) collective-permute-start(bf16[832,128]{1,0:T(8,128)(2,1)S(1)} %collective-permute-done.3.refs_1_), channel_id=1, source_target_pairs={{0,8},{1,9},{2,10},{3,11},{4,12},{5,13},{6,14},{7,15},{8,0},{9,1},... | collective-permute-start | bytes 638984 | tf_op jit(solution)/shard_map/ppermute | solution.py:710
  26.5 6.9 %collective-permute-start.11 = (bf16[640,128]{1,0:T(8,128)(2,1)S(1)}, bf16[640,128]{1,0:T(8,128)(2,1)S(1)}, u32[]{:S(2)}, u32[]{:S(2)}) collective-permute-start(bf16[640,128]{1,0:T(8,128)(2,1)S(1)} %pad_maximum_fusion.3), channel_id=1, source_target_pairs={{0,2},{1,3},{2,0},{3,1},{4,6},{5,7},{6,4},{7,5},{8,10},{9,11},{10,... | collective-permute-start | bytes 491528 | tf_op jit(solution)/shard_map/ppermute | solution.py:710
  33.5 17.0 %collective-permute-start.14 = (bf16[1280,128]{1,0:T(8,128)(2,1)S(1)}, bf16[1280,128]{1,0:T(8,128)(2,1)S(1)}, u32[]{:S(2)}, u32[]{:S(2)}) collective-permute-start(bf16[1280,128]{1,0:T(8,128)(2,1)S(1)} %constant_dynamic-update-slice_fusion.4.refs_0_), channel_id=1, source_target_pairs={{0,1},{1,0},{2,3},{3,2},{4,5},{5,4},{6,7},{7,6},{8,9},{9,8},{10,11... | collective-permute-start | bytes 983048 | tf_op jit(solution)/shard_map/ppermute | solution.py:710
  34.5 16.0 %collective-permute-start.13 = (bf16[1280,128]{1,0:T(8,128)(2,1)S(1)}, bf16[1280,128]{1,0:T(8,128)(2,1)S(1)}, u32[]{:S(2)}, u32[]{:S(2)}) collective-permute-start(bf16[1280,128]{1,0:T(8,128)(2,1)S(1)} %constant_dynamic-update-slice_fusion.4.refs_0_), channel_id=1, source_target_pairs={{0,16},{1,17},{2,18},{3,19},{4,20},{5,21},{6,22},{7,23},{8,24},{9,... | collective-permute-start | bytes 983048 | tf_op jit(solution)/shard_map/ppermute | solution.py:710
  35.6 15.7 %collective-permute-start.12 = (bf16[1280,128]{1,0:T(8,128)(2,1)S(1)}, bf16[1280,128]{1,0:T(8,128)(2,1)S(1)}, u32[]{:S(2)}, u32[]{:S(2)}) collective-permute-start(bf16[1280,128]{1,0:T(8,128)(2,1)S(1)} %constant_dynamic-update-slice_fusion.4.refs_0_), channel_id=1, source_target_pairs={{0,17},{1,16},{2,19},{3,18},{4,21},{5,20},{6,23},{7,22},{8,25},{9,... | collective-permute-start | bytes 983048 | tf_op jit(solution)/shard_map/ppermute | solution.py:710
  50.4 5.9 %collective-permute-start.15 = (bf16[1280,128]{1,0:T(8,128)(2,1)S(1)}, bf16[1280,128]{1,0:T(8,128)(2,1)S(1)}, u32[]{:S(2)}, u32[]{:S(2)}) collective-permute-start(bf16[1280,128]{1,0:T(8,128)(2,1)S(1)} %constant_dynamic-update-slice_fusion.4.refs_0_), channel_id=1, source_target_pairs={{0,8},{1,9},{2,10},{3,11},{4,12},{5,13},{6,14},{7,15},{8,0},{9,1},... | collective-permute-start | bytes 983048 | tf_op jit(solution)/shard_map/ppermute | solution.py:710
  51.3 5.0 %collective-permute-start.16 = (bf16[1280,128]{1,0:T(8,128)(2,1)S(1)}, bf16[1280,128]{1,0:T(8,128)(2,1)S(1)}, u32[]{:S(2)}, u32[]{:S(2)}) collective-permute-start(bf16[1280,128]{1,0:T(8,128)(2,1)S(1)} %collective-permute-done.12.refs_1_), channel_id=1, source_target_pairs={{0,8},{1,9},{2,10},{3,11},{4,12},{5,13},{6,14},{7,15},{8,0},{9,1},... | collective-permute-start | bytes 983048 | tf_op jit(solution)/shard_map/ppermute | solution.py:710
  51.3 5.0 %collective-permute-start.17 = (bf16[1280,128]{1,0:T(8,128)(2,1)S(1)}, bf16[1280,128]{1,0:T(8,128)(2,1)S(1)}, u32[]{:S(2)}, u32[]{:S(2)}) collective-permute-start(bf16[1280,128]{1,0:T(8,128)(2,1)S(1)} %collective-permute-done.13.refs_2_), channel_id=1, source_target_pairs={{0,8},{1,9},{2,10},{3,11},{4,12},{5,13},{6,14},{7,15},{8,0},{9,1},... | collective-permute-start | bytes 983048 | tf_op jit(solution)/shard_map/ppermute | solution.py:710
  51.8 4.5 %collective-permute-start.18 = (bf16[1280,128]{1,0:T(8,128)(2,1)S(1)}, bf16[1280,128]{1,0:T(8,128)(2,1)S(1)}, u32[]{:S(2)}, u32[]{:S(2)}) collective-permute-start(bf16[1280,128]{1,0:T(8,128)(2,1)S(1)} %collective-permute-done.14.refs_3_), channel_id=1, source_target_pairs={{0,8},{1,9},{2,10},{3,11},{4,12},{5,13},{6,14},{7,15},{8,0},{9,1},... | collective-permute-start | bytes 983048 | tf_op jit(solution)/shard_map/ppermute | solution.py:710
  51.8 4.5 %copy-start = (bf16[2048,512]{1,0:T(8,128)(2,1)S(1)}, bf16[2048,512]{1,0:T(8,128)(2,1)}, u32[]{:S(2)}) copy-start(bf16[2048,512]{1,0:T(8,128)(2,1)} %cotangent.1) | copy-start | bytes 6291460
  51.8 4.5 %copy-start.1 = (bf16[2048,512]{1,0:T(8,128)(2,1)S(1)}, bf16[2048,512]{1,0:T(8,128)(2,1)}, u32[]{:S(2)}) copy-start(bf16[2048,512]{1,0:T(8,128)(2,1)} %tokens.9) | copy-start | bytes 6291460
  81.7 12.8 %collective-permute-start.20 = (bf16[5120,128]{1,0:T(8,128)(2,1)S(1)}, bf16[5120,128]{1,0:T(8,128)(2,1)S(1)}, u32[]{:S(2)}, u32[]{:S(2)}) collective-permute-start(bf16[5120,128]{1,0:T(8,128)(2,1)S(1)} %get-tuple-element.91), channel_id=1, source_target_pairs={{0,8},{1,9},{2,10},{3,11},{4,12},{5,13},{6,14},{7,15},{8,0},{9,1},... | collective-permute-start | bytes 3932168 | tf_op jit(solution)/shard_map/ppermute | solution.py:710
  94.4 42.6 %collective-permute-start.19 = (bf16[768,128]{1,0:T(8,128)(2,1)S(1)}, bf16[768,128]{1,0:T(8,128)(2,1)S(1)}, u32[]{:S(2)}, u32[]{:S(2)}) collective-permute-start(bf16[768,128]{1,0:T(8,128)(2,1)S(1)} %get-tuple-element.88), channel_id=1, source_target_pairs={{0,8},{1,9},{2,10},{3,11},{4,12},{5,13},{6,14},{7,15},{8,0},{9,1},... | collective-permute-start | bytes 589832 | tf_op jit(solution)/shard_map/ppermute | solution.py:710
  94.7 28.1 %collective-permute-start.23 = (bf16[1280,128]{1,0:T(8,128)(2,1)S(1)}, bf16[1280,128]{1,0:T(8,128)(2,1)S(1)}, u32[]{:S(2)}, u32[]{:S(2)}) collective-permute-start(bf16[1280,128]{1,0:T(8,128)(2,1)S(1)} %get-tuple-element.126), channel_id=1, source_target_pairs={{0,17},{1,16},{2,19},{3,18},{4,21},{5,20},{6,23},{7,22},{8,25},{9,... | collective-permute-start | bytes 983048 | tf_op jit(solution)/shard_map/ppermute | solution.py:710
  96.6 26.3 %collective-permute-start.22 = (bf16[1280,128]{1,0:T(8,128)(2,1)S(1)}, bf16[1280,128]{1,0:T(8,128)(2,1)S(1)}, u32[]{:S(2)}, u32[]{:S(2)}) collective-permute-start(bf16[1280,128]{1,0:T(8,128)(2,1)S(1)} %get-tuple-element.127), channel_id=1, source_target_pairs={{0,16},{1,17},{2,18},{3,19},{4,20},{5,21},{6,22},{7,23},{8,24},{9,... | collective-permute-start | bytes 983048 | tf_op jit(solution)/shard_map/ppermute | solution.py:710
  97.1 25.8 %collective-permute-start.21 = (bf16[1280,128]{1,0:T(8,128)(2,1)S(1)}, bf16[1280,128]{1,0:T(8,128)(2,1)S(1)}, u32[]{:S(2)}, u32[]{:S(2)}) collective-permute-start(bf16[1280,128]{1,0:T(8,128)(2,1)S(1)} %get-tuple-element.128), channel_id=1, source_target_pairs={{0,1},{1,0},{2,3},{3,2},{4,5},{5,4},{6,7},{7,6},{8,9},{9,8},{10,11... | collective-permute-start | bytes 983048 | tf_op jit(solution)/shard_map/ppermute | solution.py:710
  122.8 14.5 %collective-permute-start.24 = (bf16[1536,128]{1,0:T(8,128)(2,1)S(1)}, bf16[1536,128]{1,0:T(8,128)(2,1)S(1)}, u32[]{:S(2)}, u32[]{:S(2)}) collective-permute-start(bf16[1536,128]{1,0:T(8,128)(2,1)S(1)} %get-tuple-element.104), channel_id=1, source_target_pairs={{0,8},{1,9},{2,10},{3,11},{4,12},{5,13},{6,14},{7,15},{8,0},{9,1},... | collective-permute-start | bytes 1179656 | tf_op jit(solution)/shard_map/ppermute | solution.py:710
  123.1 14.3 %collective-permute-start.32 = (bf16[640,128]{1,0:T(8,128)(2,1)S(1)}, bf16[640,128]{1,0:T(8,128)(2,1)S(1)}, u32[]{:S(2)}, u32[]{:S(2)}) collective-permute-start(bf16[640,128]{1,0:T(8,128)(2,1)S(1)} %slice.258), channel_id=1, source_target_pairs={{0,2},{1,3},{2,0},{3,1},{4,6},{5,7},{6,4},{7,5},{8,10},{9,11},{10,... | collective-permute-start | bytes 491528 | tf_op jit(solution)/shard_map/ppermute | solution.py:710
  137.0 1.6 collective-permute-start.25
  138.7 11.2 %collective-permute-start.26 = (bf16[832,128]{1,0:T(8,128)(2,1)S(1)}, bf16[832,128]{1,0:T(8,128)(2,1)S(1)}, u32[]{:S(2)}, u32[]{:S(2)}) collective-permute-start(bf16[832,128]{1,0:T(8,128)(2,1)S(1)} %bitcast.50), channel_id=1, source_target_pairs={{0,1},{1,0},{2,3},{3,2},{4,5},{5,4},{6,7},{7,6},{8,9},{9,8},{10,11... | collective-permute-start | bytes 638984 | tf_op jit(solution)/shard_map/ppermute | solution.py:710
  139.6 10.8 %collective-permute-start.27 = (bf16[832,128]{1,0:T(8,128)(2,1)S(1)}, bf16[832,128]{1,0:T(8,128)(2,1)S(1)}, u32[]{:S(2)}, u32[]{:S(2)}) collective-permute-start(bf16[832,128]{1,0:T(8,128)(2,1)S(1)} %bitcast.52), channel_id=1, source_target_pairs={{0,16},{1,17},{2,18},{3,19},{4,20},{5,21},{6,22},{7,23},{8,24},{9,... | collective-permute-start | bytes 638984 | tf_op jit(solution)/shard_map/ppermute | solution.py:710
  141.2 10.2 %collective-permute-start.28 = (bf16[832,128]{1,0:T(8,128)(2,1)S(1)}, bf16[832,128]{1,0:T(8,128)(2,1)S(1)}, u32[]{:S(2)}, u32[]{:S(2)}) collective-permute-start(bf16[832,128]{1,0:T(8,128)(2,1)S(1)} %bitcast.53), channel_id=1, source_target_pairs={{0,17},{1,16},{2,19},{3,18},{4,21},{5,20},{6,23},{7,22},{8,25},{9,... | collective-permute-start | bytes 638984 | tf_op jit(solution)/shard_map/ppermute | solution.py:710
  147.8 8.1 %collective-permute-start.33 = (bf16[320,128]{1,0:T(8,128)(2,1)S(1)}, bf16[320,128]{1,0:T(8,128)(2,1)S(1)}, u32[]{:S(2)}, u32[]{:S(2)}) collective-permute-start(bf16[320,128]{1,0:T(8,128)(2,1)S(1)} %slice.259), channel_id=1, source_target_pairs={{0,4},{1,5},{2,6},{3,7},{4,0},{5,1},{6,2},{7,3},{8,12},{9,13},{10,... | collective-permute-start | bytes 245768 | tf_op jit(solution)/shard_map/ppermute | solution.py:710
  151.5 6.0 %collective-permute-start.31 = (bf16[208,128]{1,0:T(8,128)(2,1)S(1)}, bf16[208,128]{1,0:T(8,128)(2,1)S(1)}, u32[]{:S(2)}, u32[]{:S(2)}) collective-permute-start(bf16[208,128]{1,0:T(8,128)(2,1)S(1)} %get-tuple-element.141), channel_id=1, source_target_pairs={{0,6},{1,7},{2,4},{3,5},{4,2},{5,3},{6,0},{7,1},{8,14},{9,15},{10,... | collective-permute-start | bytes 159752 | tf_op jit(solution)/shard_map/ppermute | solution.py:710
  154.2 5.3 %collective-permute-start.30 = (bf16[208,128]{1,0:T(8,128)(2,1)S(1)}, bf16[208,128]{1,0:T(8,128)(2,1)S(1)}, u32[]{:S(2)}, u32[]{:S(2)}) collective-permute-start(bf16[208,128]{1,0:T(8,128)(2,1)S(1)} %get-tuple-element.142), channel_id=1, source_target_pairs={{0,4},{1,5},{2,6},{3,7},{4,0},{5,1},{6,2},{7,3},{8,12},{9,13},{10,... | collective-permute-start | bytes 159752 | tf_op jit(solution)/shard_map/ppermute | solution.py:710
  154.2 5.3 %collective-permute-start.29 = (bf16[208,128]{1,0:T(8,128)(2,1)S(1)}, bf16[208,128]{1,0:T(8,128)(2,1)S(1)}, u32[]{:S(2)}, u32[]{:S(2)}) collective-permute-start(bf16[208,128]{1,0:T(8,128)(2,1)S(1)} %get-tuple-element.143), channel_id=1, source_target_pairs={{0,2},{1,3},{2,0},{3,1},{4,6},{5,7},{6,4},{7,5},{8,10},{9,11},{10,... | collective-permute-start | bytes 159752 | tf_op jit(solution)/shard_map/ppermute | solution.py:710

commit v2 on v1

--- a/solution.py
+++ b/solution.py
@@ -24,7 +24,7 @@
 NN = (((1,), (0,)), ((), ()))
 TN = (((0,), (0,)), ((), ()))
 TT = (((0,), (1,)), ((), ()))
-VMEM_MIB = {"pack": 2, "project": 14, "attend": 18, "middle": 26, "attend_back": 28, "input_grad": 14, "unpack": 3}
+VMEM_MIB = {"pack": 2, "project": 22, "attend": 18, "middle": 26, "attend_back": 28, "input_grad": 14, "unpack": 3}
 
 
 def dot(a, b, dims):
@@ -41,6 +41,10 @@
 
 def whole(shape):
     return pl.BlockSpec(shape, lambda *_: (0,) * len(shape))
+
+
+def resident():
+    return pl.BlockSpec(memory_space=pltpu.VMEM)
 
 
 def scalar_spec():
@@ -124,24 +128,25 @@
     queries = ((dot(x, weight[0:512, :], NN) + query_bias) * scale).astype(bf16)
     key_heads = dot(x, weight[512:1024, :], NN).astype(bf16)
     values = (dot(x, weight[1024:1536, :], NN) + value_bias).astype(bf16)
-    qkv[:, 0:512] = queries
-    qkv[:, 512:1024] = key_heads
-    qkv[:, 1024:1536] = values
+    here = pl.ds(pl.multiple_of(step * rows, rows), rows)
+    qkv[here, 0:512] = queries
+    qkv[here, 512:1024] = key_heads
+    qkv[here, 1024:1536] = values
     places = step * rows + lax.broadcasted_iota(jnp.int32, (rows, ends.shape[1]), 0)
     label = jnp.sum((ends[...] <= places).astype(f32), axis=1, keepdims=True)
     lane = lax.broadcasted_iota(jnp.int32, (rows, 128), 1)
     same = lane.astype(f32) == label
-    keys_extra[...] = jnp.where(lane < 8, jnp.where(same, 1.0, 0.0), jnp.where(lane < 32, 1.0, 0.0)).astype(bf16)
+    keys_extra[here, :] = jnp.where(lane < 8, jnp.where(same, 1.0, 0.0), jnp.where(lane < 32, 1.0, 0.0)).astype(bf16)
     apart = jnp.where((lane < 8) & jnp.logical_not(same), FAR, 0.0)
     product = queries.astype(f32) * key_heads.astype(f32)
     extra = apart
     for h in range(HEADS):
         own = jnp.sum(product[:, 128 * h : 128 * (h + 1)], axis=1, keepdims=True)
         extra = jnp.where(lane == 8 + h, -own, extra)
-    query_extra[...] = extra.astype(bf16)
-
-
-def project(me, ends, tokens, pieces, masks, order, vec_width, rows=512):
+    query_extra[here, :] = extra.astype(bf16)
+
+
+def project(me, ends, tokens, pieces, masks, order, vec_width, rows=1024):
     count = tokens.shape[0]
     sets = ends.shape[1]
     return pl.pallas_call(
@@ -152,14 +157,8 @@
             whole((1, sets)),
             pl.BlockSpec((rows, 512), lambda i: (i, 0)),
         ]
-        + [whole(piece.shape) for piece in pieces],
-        out_specs=[
-            pl.BlockSpec((rows, 1536), lambda i: (i, 0)),
-            pl.BlockSpec((rows, 128), lambda i: (i, 0)),
-            pl.BlockSpec((rows, 128), lambda i: (i, 0)),
-            whole((48, 128)),
-            whole((1536, 512)),
-        ],
+        + [resident() for _ in pieces],
+        out_specs=[resident() for _ in range(5)],
         out_shape=[
             jax.ShapeDtypeStruct((count, 1536), bf16),
             jax.ShapeDtypeStruct((count, 128), bf16),
@@ -178,17 +177,23 @@
     return (lane < 8) | (lane == 8 + head) | ((lane >= 16 + 4 * head) & (lane < 19 + 4 * head))
 
 
-def attend_kernel(base, q, k, v, query_extra, keys_extra, *refs):
-    attended, offset_out, total, mixed, peak = refs[-5:]
-    rows = q.shape[0]
-    head = base + pl.program_id(0)
+def attend_kernel(base, rows, qkv, query_extra, keys_extra, attended, offset_out, total, mixed, peak):
+    local = pl.program_id(0)
+    head = base + local
+    start = pl.program_id(1) * rows
+    here = pl.ds(pl.multiple_of(start, rows), rows)
+
+    def columns(first):
+        return pl.ds(pl.multiple_of(128 * (first + head), 128), 128)
+
+    v = qkv[:, columns(2 * HEADS)]
     lane = lax.broadcasted_iota(jnp.int32, (rows, 128), 1)
-    extra = jnp.where(own_lanes(lane, head), query_extra[...].astype(f32), 0.0).astype(bf16)
-    left = jnp.concatenate([k[...], keys_extra[...]], axis=1)
-    right = jnp.concatenate([q[...], extra], axis=1)
+    extra = jnp.where(own_lanes(lane, head), query_extra[here, :].astype(f32), 0.0).astype(bf16)
+    left = jnp.concatenate([qkv[:, columns(HEADS)], keys_extra[...]], axis=1)
+    right = jnp.concatenate([qkv[here, columns(0)], extra], axis=1)
     weights = jnp.exp(dot(left, right, NT))
     total[...] = jnp.sum(weights, axis=0, keepdims=True)
-    mixed[...] = dot(v[...], weights.astype(bf16), TN)
+    mixed[...] = dot(v, weights.astype(bf16), TN)
     peak[...] = jnp.zeros_like(peak)
     good = (total[...] > 1e-20) & (total[...] < 1e30)
 
@@ -196,49 +201,40 @@
     def _():
         def part(j, _):
             place = pl.ds(pl.multiple_of(j * 128, 128), 128)
+            some = pl.ds(pl.multiple_of(start + j * 128, 128), 128)
             lane = lax.broadcasted_iota(jnp.int32, (128, 128), 1)
-            extra = jnp.where(own_lanes(lane, head), query_extra[place, :].astype(f32), 0.0).astype(bf16)
-            again = dot(left, jnp.concatenate([q[place, :], extra], axis=1), NT)
+            extra = jnp.where(own_lanes(lane, head), query_extra[some, :].astype(f32), 0.0).astype(bf16)
+            again = dot(left, jnp.concatenate([qkv[some, columns(0)], extra], axis=1), NT)
             top = jnp.max(again, axis=0, keepdims=True)
             safe = jnp.exp(again - top)
             total[:, place] = jnp.sum(safe, axis=0, keepdims=True)
-            mixed[:, place] = dot(v[...], safe.astype(bf16), TN)
+            mixed[:, place] = dot(v, safe.astype(bf16), TN)
             peak[:, place] = top
             return 0
 
         lax.fori_loop(0, rows // 128, part, 0)
 
-    attended[...] = (mixed[...] * (1.0 / total[...])).T.astype(bf16)
-    offset_out[0] = peak[...] + jnp.log(total[...])
-
-
-def attend(qkv, query_extra, keys_extra, base, heads, prior, rows=1024):
+    own = pl.ds(pl.multiple_of(128 * local, 128), 128)
+    attended[here, own] = (mixed[...] * (1.0 / total[...])).T.astype(bf16)
+    offset_out[local, :, here] = peak[...] + jnp.log(total[...])
+
+
+def attend(qkv, query_extra, keys_extra, base, heads, rows=1024):
     count = qkv.shape[0]
     return pl.pallas_call(
-        functools.partial(attend_kernel, base),
+        functools.partial(attend_kernel, base, rows),
         grid=(heads, count // rows),
-        in_specs=[
-            pl.BlockSpec((rows, 128), lambda h, i: (i, base + h)),
-            pl.BlockSpec((count, 128), lambda h, i: (0, HEADS + base + h)),
-            pl.BlockSpec((count, 128), lambda h, i: (0, 2 * HEADS + base + h)),
-            pl.BlockSpec((rows, 128), lambda h, i: (i, 0)),
-            pl.BlockSpec((count, 128), lambda h, i: (0, 0)),
-        ]
-        + [pl.BlockSpec(memory_space=pl.ANY) for _ in prior],
-        out_specs=[
-            pl.BlockSpec((rows, 128), lambda h, i: (i, base + h)),
-            pl.BlockSpec((1, 1, rows), lambda h, i: (base + h, 0, i)),
-        ],
+        in_specs=[resident() for _ in range(3)],
+        out_specs=[resident() for _ in range(2)],
         out_shape=[
-            jax.ShapeDtypeStruct((count, 128 * HEADS), bf16),
-            jax.ShapeDtypeStruct((HEADS, 1, count), f32),
+            jax.ShapeDtypeStruct((count, 128 * heads), bf16),
+            jax.ShapeDtypeStruct((heads, 1, count), f32),
         ],
         scratch_shapes=[pltpu.VMEM((1, rows), f32), pltpu.VMEM((128, rows), f32), pltpu.VMEM((1, rows), f32)],
-        input_output_aliases={5: 0, 6: 1} if prior else {},
         compiler_params=params("attend"),
         cost_estimate=cost(heads * 8 * count * count * 128, 6e6, heads * count * count),
         name="attend",
-    )(qkv, qkv, qkv, query_extra, keys_extra, *prior)
+    )(qkv, query_extra, keys_extra)
 
 
 def mean_row(value):
@@ -259,7 +255,23 @@
     return jnp.sum(value.reshape(value.shape[0] // 8, 8, value.shape[1]), axis=0)
 
 
-def middle_kernel(masks, order_in, order_out, sub, me_ref, tokens, attended, offset, query_extra, cotangent, vec, *refs):
+def middle_kernel(
+    masks,
+    order_in,
+    order_out,
+    rows,
+    sub,
+    me_ref,
+    tokens,
+    attended_a,
+    attended_b,
+    offset_a,
+    offset_b,
+    query_extra,
+    cotangent,
+    vec,
+    *refs,
+):
     pieces = refs[: len(masks)]
     layer_output, grad_branch_out, grad_attended_out, grad_extra, query_extra_out, keep, send, vec_out = refs[
         len(masks) : -8
@@ -305,20 +317,23 @@
     attn_bias, ffn_bias, gain_one, shift_one, gain_two, shift_two = [row_of(i) for i in range(2, 8)]
     hidden_bias = jnp.concatenate([vec[32 + j : 33 + j, :] for j in range(8)], axis=1)
 
-    offset_rows = jnp.concatenate([offset[h] for h in range(HEADS)] + [jnp.zeros((4, tokens.shape[0]), f32)], axis=0)
-    offsets = offset_rows.T
-    lane = lax.broadcasted_iota(jnp.int32, (tokens.shape[0], 128), 1)
-    extra = query_extra[...].astype(f32)
+    first_row = pl.multiple_of(step * rows, rows)
+    here = pl.ds(first_row, rows)
+    parts = [offset_a[h, :, here] for h in range(3)] + [offset_b[0, :, here], jnp.zeros((4, rows), f32)]
+    offsets = jnp.concatenate(parts, axis=0).T
+    lane = lax.broadcasted_iota(jnp.int32, (rows, 128), 1)
+    extra = query_extra[here, :].astype(f32)
     for h in range(HEADS):
         for i, part in enumerate(split3(-offsets[:, h : h + 1])):
             extra = jnp.where(lane == 16 + 4 * h + i, part.astype(f32), extra)
-    query_extra_out[...] = extra.astype(bf16)
-
-    kept = [{} for _ in range(tokens.shape[0] // sub)]
+    query_extra_out[here, :] = extra.astype(bf16)
+
+    kept = [{} for _ in range(rows // sub)]
 
     def chain(s):
-        sl = slice(s * sub, (s + 1) * sub)
-        att = attended[sl, :]
+        out = slice(s * sub, (s + 1) * sub)
+        sl = pl.ds(pl.multiple_of(step * rows + s * sub, sub), sub)
+        att = jnp.concatenate([attended_a[sl, :], attended_b[sl, :]], axis=1)
         branch = dot(att, attn_weight[...], NN) + attn_bias
         yield
         normed_one, inverse_one = norm_rows(tokens[sl, :].astype(f32) + branch)
@@ -335,7 +350,7 @@
         ffn_result = dot(activated, out_weight[...], NN) + ffn_bias
         yield
         normed_two, inverse_two = norm_rows(hidden + ffn_result)
-        layer_output[sl, :] = (normed_two * gain_two + shift_two).astype(bf16)
+        layer_output[out, :] = (normed_two * gain_two + shift_two).astype(bf16)
         grad_result = cotangent[sl, :].astype(f32)
         sums[4] += fold8(grad_result * normed_two)
         sums[5] += fold8(grad_result)
@@ -375,7 +390,7 @@
         grad_extra[sl, :] = extra.astype(bf16)
         yield
 
-    chains = [chain(s) for s in range(tokens.shape[0] // sub)]
+    chains = [chain(s) for s in range(rows // sub)]
     started = 0
     live = []
     while started < len(chains) or live:
@@ -430,35 +445,14 @@
             vec_out[32 + j : 33 + j, :] = row[:, 128 * j : 128 * (j + 1)]
 
 
-def middle(
-    me, tokens, attended, offset, query_extra, cotangent, vec, pieces, masks, order_in, order_out, rows=512, sub=256
-):
+def middle(me, tokens, attended, offset, query_extra, cotangent, vec, pieces, masks, order_in, order_out, rows=512, sub=256):
     count = tokens.shape[0]
-    by_row = pl.BlockSpec((rows, 512), lambda i: (i, 0))
     half_rows = BLOCKS // 2 * R_ROWS
     return pl.pallas_call(
-        functools.partial(middle_kernel, masks, order_in, order_out, sub),
+        functools.partial(middle_kernel, masks, order_in, order_out, rows, sub),
         grid=(count // rows,),
-        in_specs=[
-            scalar_spec(),
-            by_row,
-            by_row,
-            pl.BlockSpec((HEADS, 1, rows), lambda i: (0, 0, i)),
-            pl.BlockSpec((rows, 128), lambda i: (i, 0)),
-            by_row,
-            whole((48, 128)),
-        ]
-        + [whole(piece.shape) for piece in pieces],
-        out_specs=[
-            by_row,
-            by_row,
-            by_row,
-            pl.BlockSpec((rows, 128), lambda i: (i, 0)),
-            pl.BlockSpec((rows, 128), lambda i: (i, 0)),
-            whole((half_rows, 128)),
-            whole((half_rows, 128)),
-            whole((48, 128)),
-        ],
+        in_specs=[scalar_spec()] + [resident() for _ in range(8 + len(pieces))],
+        out_specs=[pl.BlockSpec((rows, 512), lambda i: (i, 0))] + [resident() for _ in range(7)],
         out_shape=[
             jax.ShapeDtypeStruct((count, 512), bf16),
             jax.ShapeDtypeStruct((count, 512), bf16),
@@ -482,20 +476,19 @@
         compiler_params=params("middle"),
         cost_estimate=cost(6 * count * 1310720, 22e6, 3 * count * FF),
         name="middle",
-    )(me, tokens, attended, offset, query_extra, cotangent, vec, *pieces)
+    )(me, tokens, *attended, *offset, query_extra, cotangent, vec, *pieces)
 
 
 def attend_back_kernel(
     base,
     heads,
+    width,
     order,
     vec_width,
     me_ref,
     tokens,
-    q,
-    k,
-    v,
-    grad,
+    qkv,
+    grad_all,
     query_extra,
     keys_extra,
     grad_extra,
@@ -510,41 +503,42 @@
     all_keys,
     all_values,
     grad_weight,
-    held,
-    sem,
 ):
     local = pl.program_id(0)
     step = pl.program_id(1)
     steps = pl.num_programs(1)
-    width = k.shape[0]
     last = base + heads == HEADS
-    copy = pltpu.make_async_copy(tokens, held, sem)
 
     @pl.when((local == 0) & (step == 0))
     def _():
-        copy.start()
         vec[...] = vec_in[...]
 
     head = base + local
+    keys = pl.ds(pl.multiple_of(step * width, width), width)
+
+    def columns(first):
+        return pl.ds(pl.multiple_of(128 * (first + head), 128), 128)
+
+    q = qkv[:, columns(0)]
+    k = qkv[keys, columns(HEADS)]
+    v = qkv[keys, columns(2 * HEADS)]
+    grad = grad_all[:, columns(0)]
     lane = lax.broadcasted_iota(jnp.int32, (width, 128), 1)
     ones = jnp.where((lane >= 4 * head) & (lane < 4 * head + 3), 1.0, 0.0).astype(bf16)
-    extra = jnp.where(own_lanes(lane, head), keys_extra[...].astype(f32), 0.0).astype(bf16)
-    scores = dot(
-        jnp.concatenate([q[...], query_extra[...]], axis=1), jnp.concatenate([k[...], extra], axis=1), NT
-    )
-    centred = dot(
-        jnp.concatenate([grad[...], grad_extra[...]], axis=1), jnp.concatenate([v[...], ones], axis=1), NT
-    )
+    extra = jnp.where(own_lanes(lane, head), keys_extra[keys, :].astype(f32), 0.0).astype(bf16)
+    scores = dot(jnp.concatenate([q, query_extra[...]], axis=1), jnp.concatenate([k, extra], axis=1), NT)
+    centred = dot(jnp.concatenate([grad, grad_extra[...]], axis=1), jnp.concatenate([v, ones], axis=1), NT)
     probs = jnp.exp(scores)
     probs_low = probs.astype(bf16)
     grad_scores = (probs * centred).astype(bf16)
-    gv = dot(grad[...], probs_low, TN).astype(bf16)
-    gk = dot(q[...], grad_scores, TN).astype(bf16)
-    grad_values[...] = gv
-    grad_keys[...] = gk
+    gv = dot(grad, probs_low, TN).astype(bf16)
+    gk = dot(q, grad_scores, TN).astype(bf16)
+    own_rows = pl.ds(pl.multiple_of(local * 128, 128), 128)
+    grad_values[own_rows, keys] = gv
+    grad_keys[own_rows, keys] = gk
     all_values[step] = gv
     all_keys[step] = gk
-    part = dot(grad_scores, k[...], NN)
+    part = dot(grad_scores, k, NN)
 
     @pl.when(step == 0)
     def _():
@@ -553,18 +547,14 @@
     @pl.when(step > 0)
     def _():
         acc[...] += part
-
-    @pl.when((local == 0) & (step == steps - 1))
-    def _():
-        copy.wait()
 
     @pl.when(step == steps - 1)
     def _():
         me = me_ref[0]
         scale = 1.0 / math.sqrt(HEAD_DIM)
-        x = held[...]
+        x = tokens[...]
         gq_all = acc[...].astype(bf16)
-        grad_query[...] = gq_all
+        grad_query[:, pl.ds(pl.multiple_of(local * 128, 128), 128)] = gq_all
         gk_all = jnp.concatenate([all_keys[i] for i in range(all_keys.shape[0])], axis=1)
         gv_all = jnp.concatenate([all_values[i] for i in range(all_values.shape[0])], axis=1)
         sums = dot(jnp.concatenate([gq_all.T, gk_all, gv_all], axis=0), x, NN)
@@ -598,28 +588,10 @@
     count = qkv.shape[0]
     half_rows = BLOCKS // 2 * (heads * QKV_ROWS + (16 if base + heads == HEADS else 0))
     return pl.pallas_call(
-        functools.partial(attend_back_kernel, base, heads, order, vec_width),
+        functools.partial(attend_back_kernel, base, heads, width, order, vec_width),
         grid=(heads, count // width),
-        in_specs=[
-            scalar_spec(),
-            pl.BlockSpec(memory_space=pl.ANY),
-            pl.BlockSpec((count, 128), lambda h, i: (0, base + h)),
-            pl.BlockSpec((width, 128), lambda h, i: (i, HEADS + base + h)),
-            pl.BlockSpec((width, 128), lambda h, i: (i, 2 * HEADS + base + h)),
-            pl.BlockSpec((count, 128), lambda h, i: (0, base + h)),
-            whole((count, 128)),
-            pl.BlockSpec((width, 128), lambda h, i: (i, 0)),
-            whole((count, 128)),
-            whole((48, 128)),
-        ],
-        out_specs=[
-            pl.BlockSpec((count, 128), lambda h, i: (0, h)),
-            pl.BlockSpec((128, width), lambda h, i: (h, i)),
-            pl.BlockSpec((128, width), lambda h, i: (h, i)),
-            whole((half_rows, 128)),
-            whole((half_rows, 128)),
-            whole((48, 128)),
-        ],
+        in_specs=[scalar_spec()] + [resident() for _ in range(7)],
+        out_specs=[resident() for _ in range(6)],
         out_shape=[
             jax.ShapeDtypeStruct((count, 128 * heads), bf16),
             jax.ShapeDtypeStruct((128 * heads, count), bf16),
@@ -633,24 +605,23 @@
             pltpu.VMEM((count // width, 128, width), bf16),
             pltpu.VMEM((count // width, 128, width), bf16),
             pltpu.VMEM((1536, 128), bf16),
-            pltpu.VMEM((count, 512), bf16),
-            pltpu.SemaphoreType.DMA,
         ],
         compiler_params=params("attend_back"),
         cost_estimate=cost(heads * 20 * count * count * 128, heads * 12e6, heads * count * count),
         name="attend_back",
-    )(me, tokens, qkv, qkv, qkv, grad_attended, query_extra, keys_extra, grad_extra, vec)
-
-
-def input_grad_kernel(groups, *refs):
+    )(me, tokens, qkv, grad_attended, query_extra, keys_extra, grad_extra, vec)
+
+
+def input_grad_kernel(groups, rows, *refs):
     grad_branch = refs[0]
     queries, keys, values = [refs[1 + i * groups : 1 + (i + 1) * groups] for i in range(3)]
     weight, out = refs[-2], refs[-1]
     scale = 1.0 / math.sqrt(HEAD_DIM)
-    gq = jnp.concatenate([r[...] for r in queries], axis=1)
-    gk = jnp.concatenate([r[...] for r in keys], axis=0)
-    gv = jnp.concatenate([r[...] for r in values], axis=0)
-    total = grad_branch[...].astype(f32) + scale * dot(gq, weight[0:512, :], NT)
+    here = pl.ds(pl.multiple_of(pl.program_id(0) * rows, rows), rows)
+    gq = jnp.concatenate([r[here, :] for r in queries], axis=1)
+    gk = jnp.concatenate([r[:, here] for r in keys], axis=0)
+    gv = jnp.concatenate([r[:, here] for r in values], axis=0)
+    total = grad_branch[here, :].astype(f32) + scale * dot(gq, weight[0:512, :], NT)
     total = total + dot(gk, weight[512:1024, :], TT)
     out[...] = total + dot(gv, weight[1024:1536, :], TT)
 
@@ -659,12 +630,9 @@
     count = grad_branch.shape[0]
     by_row = pl.BlockSpec((rows, 512), lambda i: (i, 0))
     return pl.pallas_call(
-        functools.partial(input_grad_kernel, len(queries)),
+        functools.partial(input_grad_kernel, len(queries), rows),
         grid=(count // rows,),
-        in_specs=[by_row]
-        + [pl.BlockSpec((rows, a.shape[1]), lambda i: (i, 0)) for a in queries]
-        + [pl.BlockSpec((a.shape[0], rows), lambda i: (0, i)) for a in keys + values]
-        + [whole((1536, 512))],
+        in_specs=[resident() for _ in range(2 + 3 * len(queries))],
         out_specs=by_row,
         out_shape=jax.ShapeDtypeStruct((count, 512), f32),
         compiler_params=params("input_grad"),
@@ -808,14 +776,14 @@
     qkv, keys_extra, query_extra, vec, weight = project(
         me, ends, pltpu.with_memory_space_constraint(tokens, pltpu.HBM), q_pieces, masks, order_in, vec_width
     )
-    prior = attend(qkv, query_extra, keys_extra, 0, 3, [])
+    attended_a, offset_a = attend(qkv, query_extra, keys_extra, 0, 3)
     if fast:
-        r_pieces = [r_far] + [after(piece, prior[0]) for piece in r_pieces]
+        r_pieces = [r_far] + [after(piece, attended_a) for piece in r_pieces]
         keys_extra = after(keys_extra, *r_pieces)
         r_pieces = r_pieces + [swap(piece, core, count) for piece in r_pieces]
-    attended, offset = attend(qkv, query_extra, keys_extra, 3, 1, prior)
+    attended_b, offset_b = attend(qkv, query_extra, keys_extra, 3, 1)
     layer_output, grad_branch, grad_attended, grad_extra, query_extra, r_keep, r_send, vec_grad = middle(
-        me, tokens, attended, offset, query_extra, cotangent, vec, r_pieces, masks, order_rest, order_rest_out
+        me, tokens, (attended_a, attended_b), (offset_a, offset_b), query_extra, cotangent, vec, r_pieces, masks, order_rest, order_rest_out
     )
     queries, keys, values, keeps, sends, gots = [], [], [], [], [], []
     if fast:

time: 161 us -> 157 us (0.975)
  Pallas kernels: 106 us -> 101 us
    pallas_call x6, Pallas kernels: 72.8 us -> 68.2 us  [the longest x3 46.7 us: attend_back(): pl.pallas_call(functools.partial(attend_back_kernel, base, heads, width,...]
  transfers between devices with their start and end apart: 34 -> 34, of which waited for: 11 -> 11; matrix products, arithmetic and copies ran while one was open for 2% -> 2% of each run, Pallas kernels for 49% -> 47%
where the time goes in v2:
time: 157 us
  Pallas kernels  101 us (64%)
  starting transfers between devices  32.6 us (21%)
  waiting for transfers between devices  18.6 us (12%)
  other arithmetic  2.68 us (2%)
    pallas_call x3, Pallas kernels, attend_back(): pl.pallas_call(functools.partial(attend_back_kernel, base, heads, width,...  46.7 us
    ppermute x34, starting transfers between devices, swap(): return lax.ppermute(array, AXES, [(i, i ^ step) for i in range(count)])  32.6 us
    pallas_call x1, Pallas kernels, middle(): pl.pallas_call(functools.partial(middle_kernel, masks, order_in, order_ou...  25.3 us
    ppermute x34, waiting for transfers between devices, swap(): return lax.ppermute(array, AXES, [(i, i ^ step) for i in range(count)])  18.6 us
    pallas_call x2, Pallas kernels, attend(): pl.pallas_call(functools.partial(attend_kernel, base, rows), grid=(heads,...  16.4 us
    pallas_call x1, Pallas kernels, project(): pl.pallas_call(functools.partial(project_kernel, masks, order, vec_width)...  5.47 us
    pallas_call x1, Pallas kernels, input_grad(): pl.pallas_call(functools.partial(input_grad_kernel, len(queries), rows),...  5.07 us
  transfers between devices with their start and end apart: 34, of which 11 were waited for; matrix products, arithmetic and copies ran while one was open for 2% of the time, Pallas kernels for 47%

profile of v2, /device:TPU:0, one launch (start us, length us, event | category | flops | bytes accessed | tf_op | source)
XLA Modules:
  0.0 156.5 jit_solution(8201020814280757826)
XLA Ops:
  0.6 0.7 reshape.215.vec
  1.3 1.0 pack.1
  2.3 5.1 %collective-permute-start.2 = (bf16[208,128]{1,0:T(8,128)(2,1)S(1)}, bf16[208,128]{1,0:T(8,128)(2,1)S(1)}, u32[]{:S(2)}, u32[]{:S(2)}) collective-permute-start(bf16[208,128]{1,0:T(8,128)(2,1)S(1)} %get-tuple-element.64), channel_id=1, source_target_pairs={{0,6},{1,7},{2,4},{3,5},{4,2},{5,3},{6,0},{7,1},{8,14},{9,15},{10,... | collective-permute-start | bytes 159752 | tf_op jit(solution)/shard_map/ppermute | solution.py:678
  7.4 0.6 collective-permute-start
  8.0 0.7 select_bitcast_fusion
  8.7 0.3 reduce-window.9
  9.2 0.8 bitcast_select_fusion
  10.0 1.5 collective-permute-done
  11.5 0.9 collective-permute-done.1
  12.5 1.6 collective-permute-start.5
  14.1 1.5 collective-permute-start.4
  15.6 0.5 collective-permute-start.3
  16.1 2.1 %collective-permute-start.10 = (bf16[320,128]{1,0:T(8,128)(2,1)S(1)}, bf16[320,128]{1,0:T(8,128)(2,1)S(1)}, u32[]{:S(2)}, u32[]{:S(2)}) collective-permute-start(bf16[320,128]{1,0:T(8,128)(2,1)S(1)} %get-tuple-element.71), channel_id=1, source_target_pairs={{0,4},{1,5},{2,6},{3,7},{4,0},{5,1},{6,2},{7,3},{8,12},{9,13},{10,... | collective-permute-start | bytes 245768 | tf_op jit(solution)/shard_map/ppermute | solution.py:678
  18.1 2.5 %collective-permute-done.5.refs_3_ = bf16[832,128]{1,0:T(8,128)(2,1)S(1)} collective-permute-done((bf16[832,128]{1,0:T(8,128)(2,1)S(1)}, bf16[832,128]{1,0:T(8,128)(2,1)S(1)}, u32[]{:S(2)}, u32[]{:S(2)}) %collective-permute-start.5) | collective-permute-done | bytes 213024 | tf_op jit(solution)/shard_map/ppermute | solution.py:678
  20.6 5.3 %collective-permute-done.4.refs_2_ = bf16[832,128]{1,0:T(8,128)(2,1)S(1)} collective-permute-done((bf16[832,128]{1,0:T(8,128)(2,1)S(1)}, bf16[832,128]{1,0:T(8,128)(2,1)S(1)}, u32[]{:S(2)}, u32[]{:S(2)}) %collective-permute-start.4) | collective-permute-done | bytes 213024 | tf_op jit(solution)/shard_map/ppermute | solution.py:678
  26.0 0.5 collective-permute-start.7
  26.5 1.0 collective-permute-start.11
  27.7 5.5 %project.1 = (bf16[2048,1536]{1,0:T(8,128)(2,1)S(1)}, bf16[2048,128]{1,0:T(8,128)(2,1)S(1)}, bf16[2048,128]{1,0:T(8,128)(2,1)S(1)}, f32[48,128]{1,0:T(8,128)S(1)}, bf16[1536,512]{1,0:T(8,128)(2,1)S(1)}) custom-call(s32[1]{0:T(128)} %bitcast.me_ref, s32[1,256]{1,0:T(1,128)S(1)} %bitcast.38, bf16[2048,512]{1,0:T(8,128)(2,1)} %tokens.9, ...), custom_call_target="tpu_custom_call" | custom-call | flops 3221225472 | bytes 12000000 | tf_op jit(solution)/shard_map/project/pallas_call | solution.py:152
  33.2 1.0 collective-permute-start.14
  34.2 1.1 collective-permute-start.13
  35.3 1.4 collective-permute-start.12
  36.8 12.3 %attend.2 = (bf16[2048,384]{1,0:T(8,128)(2,1)S(1)}, f32[3,1,2048]{2,1,0:T(1,128)S(1)}) custom-call(bf16[2048,1536]{1,0:T(8,128)(2,1)S(1)} %get-tuple-element.66.qkv, bf16[2048,128]{1,0:T(8,128)(2,1)S(1)} %get-tuple-element.67.query_extra, bf16[2048,128]{1,0:T(8,128)(2,1)S(1)} %get-tuple-element.76.keys_extra), custom_call_target="tpu_custom_call" | custom-call | flops 12884901888 | bytes 6000000 | tf_op jit(solution)/shard_map/attend/pallas_call | solution.py:224
  49.2 0.3 collective-permute-done.13.refs_2_
  49.5 1.6 %collective-permute-done.12.refs_1_ = bf16[1280,128]{1,0:T(8,128)(2,1)S(1)} collective-permute-done((bf16[1280,128]{1,0:T(8,128)(2,1)S(1)}, bf16[1280,128]{1,0:T(8,128)(2,1)S(1)}, u32[]{:S(2)}, u32[]{:S(2)}) %collective-permute-start.12) | collective-permute-done | bytes 327712 | tf_op jit(solution)/shard_map/ppermute | solution.py:678
  51.1 0.5 collective-permute-start.17
  51.6 4.2 %attend.3 = (bf16[2048,128]{1,0:T(8,128)(2,1)S(1)}, f32[1,1,2048]{2,1,0:T(1,128)S(1)}) custom-call(bf16[2048,1536]{1,0:T(8,128)(2,1)S(1)} %get-tuple-element.66.qkv, bf16[2048,128]{1,0:T(8,128)(2,1)S(1)} %get-tuple-element.67.query_extra, bf16[2048,128]{1,0:T(8,128)(2,1)S(1)} %get-tuple-element.76.keys_extra), custom_call_target="tpu_custom_call" | custom-call | flops 4294967296 | bytes 6000000 | tf_op jit(solution)/shard_map/attend/pallas_call | solution.py:224
  55.8 25.3 %middle.1 = (bf16[2048,512]{1,0:T(8,128)(2,1)}, bf16[2048,512]{1,0:T(8,128)(2,1)S(1)}, bf16[2048,512]{1,0:T(8,128)(2,1)S(1)}, bf16[2048,128]{1,0:T(8,128)(2,1)S(...) custom-call(s32[1]{0:T(128)} %bitcast.me_ref, ...), custom_call_target="tpu_custom_call" | custom-call | flops 16106127360 | bytes 22000000 | tf_op jit(solution)/shard_map/middle/pallas_call | solution.py:451
  81.1 0.5 collective-permute-start.20
  81.6 11.5 %attend_back.3 = (bf16[2048,128]{1,0:T(8,128)(2,1)S(1)}, bf16[128,2048]{1,0:T(8,128)(2,1)S(1)}, bf16[128,2048]{1,0:T(8,128)(2,1)S(1)}, bf16[768,128]{1,0:T(8,128...) custom-call(s32[1]{0:T(128)} %bitcast.me_ref, bf16[2048,512]{1,0:T(8,128)(2,1)S(1)} %copy-done.1, ...), custom_call_target="tpu_custom_call" | custom-call | flops 10737418240 | bytes 12000000 | tf_op jit(solution)/shard_map/attend_back/pallas_call | solution.py:590
  93.2 0.3 add_convert_fusion
  93.5 1.8 %collective-permute-start.23 = (bf16[1280,128]{1,0:T(8,128)(2,1)S(1)}, bf16[1280,128]{1,0:T(8,128)(2,1)S(1)}, u32[]{:S(2)}, u32[]{:S(2)}) collective-permute-start(bf16[1280,128]{1,0:T(8,128)(2,1)S(1)} %get-tuple-element.126), channel_id=1, source_target_pairs={{0,17},{1,16},{2,19},{3,18},{4,21},{5,20},{6,23},{7,22},{8,25},{9,... | collective-permute-start | bytes 983048 | tf_op jit(solution)/shard_map/ppermute | solution.py:678
  95.3 0.5 collective-permute-start.22
  95.8 1.2 collective-permute-start.21
  97.1 23.0 %attend_back.4 = (bf16[2048,256]{1,0:T(8,128)(2,1)S(1)}, bf16[256,2048]{1,0:T(8,128)(2,1)S(1)}, bf16[256,2048]{1,0:T(8,128)(2,1)S(1)}, bf16[1536,128]{1,0:T(8,12...) custom-call(s32[1]{0:T(128)} %bitcast.me_ref, bf16[2048,512]{1,0:T(8,128)(2,1)S(1)} %copy-done.1, ...), custom_call_target="tpu_custom_call" | custom-call | flops 21474836480 | bytes 24000000 | tf_op jit(solution)/shard_map/attend_back/pallas_call | solution.py:590
  120.4 1.0 collective-permute-start.32
  121.3 12.2 %attend_back.5 = (bf16[2048,128]{1,0:T(8,128)(2,1)S(1)}, bf16[128,2048]{1,0:T(8,128)(2,1)S(1)}, bf16[128,2048]{1,0:T(8,128)(2,1)S(1)}, bf16[1024,128]{1,0:T(8,12...) custom-call(s32[1]{0:T(128)} %bitcast.me_ref, bf16[2048,512]{1,0:T(8,128)(2,1)S(1)} %copy-done.1, ...), custom_call_target="tpu_custom_call" | custom-call | flops 10737418240 | bytes 12000000 | tf_op jit(solution)/shard_map/attend_back/pallas_call | solution.py:590
  134.0 1.1 collective-permute-done.25
  135.2 0.9 collective-permute-start.26
  136.0 1.6 %collective-permute-start.27 = (bf16[832,128]{1,0:T(8,128)(2,1)S(1)}, bf16[832,128]{1,0:T(8,128)(2,1)S(1)}, u32[]{:S(2)}, u32[]{:S(2)}) collective-permute-start(bf16[832,128]{1,0:T(8,128)(2,1)S(1)} %bitcast.52), channel_id=1, source_target_pairs={{0,16},{1,17},{2,18},{3,19},{4,20},{5,21},{6,22},{7,23},{8,24},{9,... | collective-permute-start | bytes 638984 | tf_op jit(solution)/shard_map/ppermute | solution.py:678
  137.6 1.2 collective-permute-start.28
  138.9 5.1 %input_grad.1 = f32[2048,512]{1,0:T(8,128)} custom-call(bf16[2048,512]{1,0:T(8,128)(2,1)S(1)} %get-tuple-element.109.refs_0_, bf16[2048,128]{1,0:T(8,128)(2,1)S(1)} %get-tuple-element.92.refs_1_, bf16[2048,256]{1,0:T(8,128)(2,1)S(1)} %get-tuple-element.96.refs_2_, bf16[2048,128]{1,0:T(8,128)(2,1)S(1)} %get-tuple-element.101.refs_3_, ...), custom_call_target="tpu_custom_call" | custom-call | flops 3221225472 | bytes 16000000 | tf_op jit(solution)/shard_map/input_grad/pallas_call | solution.py:632
  143.9 2.0 %collective-permute-start.33 = (bf16[320,128]{1,0:T(8,128)(2,1)S(1)}, bf16[320,128]{1,0:T(8,128)(2,1)S(1)}, u32[]{:S(2)}, u32[]{:S(2)}) collective-permute-start(bf16[320,128]{1,0:T(8,128)(2,1)S(1)} %slice.259), channel_id=1, source_target_pairs={{0,4},{1,5},{2,6},{3,7},{4,0},{5,1},{6,2},{7,3},{8,12},{9,13},{10,... | collective-permute-start | bytes 245768 | tf_op jit(solution)/shard_map/ppermute | solution.py:678
  146.0 1.8 %collective-permute-done.27 = bf16[832,128]{1,0:T(8,128)(2,1)S(1)} collective-permute-done((bf16[832,128]{1,0:T(8,128)(2,1)S(1)}, bf16[832,128]{1,0:T(8,128)(2,1)S(1)}, u32[]{:S(2)}, u32[]{:S(2)}) %collective-permute-start.27) | collective-permute-done | bytes 213024 | tf_op jit(solution)/shard_map/ppermute | solution.py:678
  147.9 2.7 %collective-permute-start.31 = (bf16[208,128]{1,0:T(8,128)(2,1)S(1)}, bf16[208,128]{1,0:T(8,128)(2,1)S(1)}, u32[]{:S(2)}, u32[]{:S(2)}) collective-permute-start(bf16[208,128]{1,0:T(8,128)(2,1)S(1)} %get-tuple-element.141), channel_id=1, source_target_pairs={{0,6},{1,7},{2,4},{3,5},{4,2},{5,3},{6,0},{7,1},{8,14},{9,15},{10,... | collective-permute-start | bytes 159752 | tf_op jit(solution)/shard_map/ppermute | solution.py:678
  150.6 1.8 %collective-permute-start.29 = (bf16[208,128]{1,0:T(8,128)(2,1)S(1)}, bf16[208,128]{1,0:T(8,128)(2,1)S(1)}, u32[]{:S(2)}, u32[]{:S(2)}) collective-permute-start(bf16[208,128]{1,0:T(8,128)(2,1)S(1)} %get-tuple-element.143), channel_id=1, source_target_pairs={{0,2},{1,3},{2,0},{3,1},{4,6},{5,7},{6,4},{7,5},{8,10},{9,11},{10,... | collective-permute-start | bytes 159752 | tf_op jit(solution)/shard_map/ppermute | solution.py:678
  152.4 1.5 collective-permute-done.31.refs_3_
  153.9 1.9 %collective-permute-done.30.refs_2_ = bf16[208,128]{1,0:T(8,128)(2,1)S(1)} collective-permute-done((bf16[208,128]{1,0:T(8,128)(2,1)S(1)}, bf16[208,128]{1,0:T(8,128)(2,1)S(1)}, u32[]{:S(2)}, u32[]{:S(2)}) %collective-permute-start.30) | collective-permute-done | bytes 53280 | tf_op jit(solution)/shard_map/ppermute | solution.py:678
  155.8 0.8 unpack.1
  (64 shorter events, 1.8 us)
Async XLA Ops:
  2.3 9.2 %collective-permute-start.2 = (bf16[208,128]{1,0:T(8,128)(2,1)S(1)}, bf16[208,128]{1,0:T(8,128)(2,1)S(1)}, u32[]{:S(2)}, u32[]{:S(2)}) collective-permute-start(bf16[208,128]{1,0:T(8,128)(2,1)S(1)} %get-tuple-element.64), channel_id=1, source_target_pairs={{0,6},{1,7},{2,4},{3,5},{4,2},{5,3},{6,0},{7,1},{8,14},{9,15},{10,... | collective-permute-start | bytes 159752 | tf_op jit(solution)/shard_map/ppermute | solution.py:678
  7.4 5.0 %collective-permute-start.1 = (bf16[208,128]{1,0:T(8,128)(2,1)S(1)}, bf16[208,128]{1,0:T(8,128)(2,1)S(1)}, u32[]{:S(2)}, u32[]{:S(2)}) collective-permute-start(bf16[208,128]{1,0:T(8,128)(2,1)S(1)} %get-tuple-element.64), channel_id=1, source_target_pairs={{0,4},{1,5},{2,6},{3,7},{4,0},{5,1},{6,2},{7,3},{8,12},{9,13},{10,... | collective-permute-start | bytes 159752 | tf_op jit(solution)/shard_map/ppermute | solution.py:678
  7.4 4.1 %collective-permute-start = (bf16[208,128]{1,0:T(8,128)(2,1)S(1)}, bf16[208,128]{1,0:T(8,128)(2,1)S(1)}, u32[]{:S(2)}, u32[]{:S(2)}) collective-permute-start(bf16[208,128]{1,0:T(8,128)(2,1)S(1)} %get-tuple-element.64), channel_id=1, source_target_pairs={{0,2},{1,3},{2,0},{3,1},{4,6},{5,7},{6,4},{7,5},{8,10},{9,11},{10,... | collective-permute-start | bytes 159752 | tf_op jit(solution)/shard_map/ppermute | solution.py:678
  12.4 3.6 %collective-permute-start.6 = (bf16[832,128]{1,0:T(8,128)(2,1)S(1)}, bf16[832,128]{1,0:T(8,128)(2,1)S(1)}, u32[]{:S(2)}, u32[]{:S(2)}) collective-permute-start(bf16[832,128]{1,0:T(8,128)(2,1)S(1)} %constant_dynamic-update-slice_fusion.refs_0_), channel_id=1, source_target_pairs={{0,8},{1,9},{2,10},{3,11},{4,12},{5,13},{6,14},{7,15},{8,0},{9,1},... | collective-permute-start | bytes 638984 | tf_op jit(solution)/shard_map/ppermute | solution.py:678
  12.5 8.1 %collective-permute-start.5 = (bf16[832,128]{1,0:T(8,128)(2,1)S(1)}, bf16[832,128]{1,0:T(8,128)(2,1)S(1)}, u32[]{:S(2)}, u32[]{:S(2)}) collective-permute-start(bf16[832,128]{1,0:T(8,128)(2,1)S(1)} %constant_dynamic-update-slice_fusion.refs_0_), channel_id=1, source_target_pairs={{0,1},{1,0},{2,3},{3,2},{4,5},{5,4},{6,7},{7,6},{8,9},{9,8},{10,11... | collective-permute-start | bytes 638984 | tf_op jit(solution)/shard_map/ppermute | solution.py:678
  14.1 11.9 %collective-permute-start.4 = (bf16[832,128]{1,0:T(8,128)(2,1)S(1)}, bf16[832,128]{1,0:T(8,128)(2,1)S(1)}, u32[]{:S(2)}, u32[]{:S(2)}) collective-permute-start(bf16[832,128]{1,0:T(8,128)(2,1)S(1)} %constant_dynamic-update-slice_fusion.refs_0_), channel_id=1, source_target_pairs={{0,16},{1,17},{2,18},{3,19},{4,20},{5,21},{6,22},{7,23},{8,24},{9,... | collective-permute-start | bytes 638984 | tf_op jit(solution)/shard_map/ppermute | solution.py:678
  15.6 10.4 %collective-permute-start.3 = (bf16[832,128]{1,0:T(8,128)(2,1)S(1)}, bf16[832,128]{1,0:T(8,128)(2,1)S(1)}, u32[]{:S(2)}, u32[]{:S(2)}) collective-permute-start(bf16[832,128]{1,0:T(8,128)(2,1)S(1)} %constant_dynamic-update-slice_fusion.refs_0_), channel_id=1, source_target_pairs={{0,17},{1,16},{2,19},{3,18},{4,21},{5,20},{6,23},{7,22},{8,25},{9,... | collective-permute-start | bytes 638984 | tf_op jit(solution)/shard_map/ppermute | solution.py:678
  16.1 10.4 %collective-permute-start.10 = (bf16[320,128]{1,0:T(8,128)(2,1)S(1)}, bf16[320,128]{1,0:T(8,128)(2,1)S(1)}, u32[]{:S(2)}, u32[]{:S(2)}) collective-permute-start(bf16[320,128]{1,0:T(8,128)(2,1)S(1)} %get-tuple-element.71), channel_id=1, source_target_pairs={{0,4},{1,5},{2,6},{3,7},{4,0},{5,1},{6,2},{7,3},{8,12},{9,13},{10,... | collective-permute-start | bytes 245768 | tf_op jit(solution)/shard_map/ppermute | solution.py:678
  20.6 6.9 %collective-permute-start.9 = (bf16[832,128]{1,0:T(8,128)(2,1)S(1)}, bf16[832,128]{1,0:T(8,128)(2,1)S(1)}, u32[]{:S(2)}, u32[]{:S(2)}) collective-permute-start(bf16[832,128]{1,0:T(8,128)(2,1)S(1)} %collective-permute-done.5.refs_3_), channel_id=1, source_target_pairs={{0,8},{1,9},{2,10},{3,11},{4,12},{5,13},{6,14},{7,15},{8,0},{9,1},... | collective-permute-start | bytes 638984 | tf_op jit(solution)/shard_map/ppermute | solution.py:678
  25.9 1.5 collective-permute-start.8
  26.0 1.8 %collective-permute-start.7 = (bf16[832,128]{1,0:T(8,128)(2,1)S(1)}, bf16[832,128]{1,0:T(8,128)(2,1)S(1)}, u32[]{:S(2)}, u32[]{:S(2)}) collective-permute-start(bf16[832,128]{1,0:T(8,128)(2,1)S(1)} %collective-permute-done.3.refs_1_), channel_id=1, source_target_pairs={{0,8},{1,9},{2,10},{3,11},{4,12},{5,13},{6,14},{7,15},{8,0},{9,1},... | collective-permute-start | bytes 638984 | tf_op jit(solution)/shard_map/ppermute | solution.py:678
  26.5 6.7 %collective-permute-start.11 = (bf16[640,128]{1,0:T(8,128)(2,1)S(1)}, bf16[640,128]{1,0:T(8,128)(2,1)S(1)}, u32[]{:S(2)}, u32[]{:S(2)}) collective-permute-start(bf16[640,128]{1,0:T(8,128)(2,1)S(1)} %pad_maximum_fusion.3), channel_id=1, source_target_pairs={{0,2},{1,3},{2,0},{3,1},{4,6},{5,7},{6,4},{7,5},{8,10},{9,11},{10,... | collective-permute-start | bytes 491528 | tf_op jit(solution)/shard_map/ppermute | solution.py:678
  33.2 15.9 %collective-permute-start.14 = (bf16[1280,128]{1,0:T(8,128)(2,1)S(1)}, bf16[1280,128]{1,0:T(8,128)(2,1)S(1)}, u32[]{:S(2)}, u32[]{:S(2)}) collective-permute-start(bf16[1280,128]{1,0:T(8,128)(2,1)S(1)} %constant_dynamic-update-slice_fusion.4.refs_0_), channel_id=1, source_target_pairs={{0,1},{1,0},{2,3},{3,2},{4,5},{5,4},{6,7},{7,6},{8,9},{9,8},{10,11... | collective-permute-start | bytes 983048 | tf_op jit(solution)/shard_map/ppermute | solution.py:678
  34.2 15.2 %collective-permute-start.13 = (bf16[1280,128]{1,0:T(8,128)(2,1)S(1)}, bf16[1280,128]{1,0:T(8,128)(2,1)S(1)}, u32[]{:S(2)}, u32[]{:S(2)}) collective-permute-start(bf16[1280,128]{1,0:T(8,128)(2,1)S(1)} %constant_dynamic-update-slice_fusion.4.refs_0_), channel_id=1, source_target_pairs={{0,16},{1,17},{2,18},{3,19},{4,20},{5,21},{6,22},{7,23},{8,24},{9,... | collective-permute-start | bytes 983048 | tf_op jit(solution)/shard_map/ppermute | solution.py:678
  35.3 15.8 %collective-permute-start.12 = (bf16[1280,128]{1,0:T(8,128)(2,1)S(1)}, bf16[1280,128]{1,0:T(8,128)(2,1)S(1)}, u32[]{:S(2)}, u32[]{:S(2)}) collective-permute-start(bf16[1280,128]{1,0:T(8,128)(2,1)S(1)} %constant_dynamic-update-slice_fusion.4.refs_0_), channel_id=1, source_target_pairs={{0,17},{1,16},{2,19},{3,18},{4,21},{5,20},{6,23},{7,22},{8,25},{9,... | collective-permute-start | bytes 983048 | tf_op jit(solution)/shard_map/ppermute | solution.py:678
  49.1 6.7 %collective-permute-start.15 = (bf16[1280,128]{1,0:T(8,128)(2,1)S(1)}, bf16[1280,128]{1,0:T(8,128)(2,1)S(1)}, u32[]{:S(2)}, u32[]{:S(2)}) collective-permute-start(bf16[1280,128]{1,0:T(8,128)(2,1)S(1)} %constant_dynamic-update-slice_fusion.4.refs_0_), channel_id=1, source_target_pairs={{0,8},{1,9},{2,10},{3,11},{4,12},{5,13},{6,14},{7,15},{8,0},{9,1},... | collective-permute-start | bytes 983048 | tf_op jit(solution)/shard_map/ppermute | solution.py:678
  49.1 6.7 %copy-start = (bf16[2048,512]{1,0:T(8,128)(2,1)S(1)}, bf16[2048,512]{1,0:T(8,128)(2,1)}, u32[]{:S(2)}) copy-start(bf16[2048,512]{1,0:T(8,128)(2,1)} %cotangent.1) | copy-start | bytes 6291460
  49.2 6.7 %copy-start.1 = (bf16[2048,512]{1,0:T(8,128)(2,1)S(1)}, bf16[2048,512]{1,0:T(8,128)(2,1)}, u32[]{:S(2)}) copy-start(bf16[2048,512]{1,0:T(8,128)(2,1)} %tokens.9) | copy-start | bytes 6291460
  51.1 4.7 %collective-permute-start.16 = (bf16[1280,128]{1,0:T(8,128)(2,1)S(1)}, bf16[1280,128]{1,0:T(8,128)(2,1)S(1)}, u32[]{:S(2)}, u32[]{:S(2)}) collective-permute-start(bf16[1280,128]{1,0:T(8,128)(2,1)S(1)} %collective-permute-done.12.refs_1_), channel_id=1, source_target_pairs={{0,8},{1,9},{2,10},{3,11},{4,12},{5,13},{6,14},{7,15},{8,0},{9,1},... | collective-permute-start | bytes 983048 | tf_op jit(solution)/shard_map/ppermute | solution.py:678
  51.1 4.7 %collective-permute-start.17 = (bf16[1280,128]{1,0:T(8,128)(2,1)S(1)}, bf16[1280,128]{1,0:T(8,128)(2,1)S(1)}, u32[]{:S(2)}, u32[]{:S(2)}) collective-permute-start(bf16[1280,128]{1,0:T(8,128)(2,1)S(1)} %collective-permute-done.13.refs_2_), channel_id=1, source_target_pairs={{0,8},{1,9},{2,10},{3,11},{4,12},{5,13},{6,14},{7,15},{8,0},{9,1},... | collective-permute-start | bytes 983048 | tf_op jit(solution)/shard_map/ppermute | solution.py:678
  51.6 4.2 %collective-permute-start.18 = (bf16[1280,128]{1,0:T(8,128)(2,1)S(1)}, bf16[1280,128]{1,0:T(8,128)(2,1)S(1)}, u32[]{:S(2)}, u32[]{:S(2)}) collective-permute-start(bf16[1280,128]{1,0:T(8,128)(2,1)S(1)} %collective-permute-done.14.refs_3_), channel_id=1, source_target_pairs={{0,8},{1,9},{2,10},{3,11},{4,12},{5,13},{6,14},{7,15},{8,0},{9,1},... | collective-permute-start | bytes 983048 | tf_op jit(solution)/shard_map/ppermute | solution.py:678
  81.1 12.1 %collective-permute-start.20 = (bf16[5120,128]{1,0:T(8,128)(2,1)S(1)}, bf16[5120,128]{1,0:T(8,128)(2,1)S(1)}, u32[]{:S(2)}, u32[]{:S(2)}) collective-permute-start(bf16[5120,128]{1,0:T(8,128)(2,1)S(1)} %get-tuple-element.91), channel_id=1, source_target_pairs={{0,8},{1,9},{2,10},{3,11},{4,12},{5,13},{6,14},{7,15},{8,0},{9,1},... | collective-permute-start | bytes 3932168 | tf_op jit(solution)/shard_map/ppermute | solution.py:678
  93.1 40.4 %collective-permute-start.19 = (bf16[768,128]{1,0:T(8,128)(2,1)S(1)}, bf16[768,128]{1,0:T(8,128)(2,1)S(1)}, u32[]{:S(2)}, u32[]{:S(2)}) collective-permute-start(bf16[768,128]{1,0:T(8,128)(2,1)S(1)} %get-tuple-element.88), channel_id=1, source_target_pairs={{0,8},{1,9},{2,10},{3,11},{4,12},{5,13},{6,14},{7,15},{8,0},{9,1},... | collective-permute-start | bytes 589832 | tf_op jit(solution)/shard_map/ppermute | solution.py:678
  93.5 26.6 %collective-permute-start.23 = (bf16[1280,128]{1,0:T(8,128)(2,1)S(1)}, bf16[1280,128]{1,0:T(8,128)(2,1)S(1)}, u32[]{:S(2)}, u32[]{:S(2)}) collective-permute-start(bf16[1280,128]{1,0:T(8,128)(2,1)S(1)} %get-tuple-element.126), channel_id=1, source_target_pairs={{0,17},{1,16},{2,19},{3,18},{4,21},{5,20},{6,23},{7,22},{8,25},{9,... | collective-permute-start | bytes 983048 | tf_op jit(solution)/shard_map/ppermute | solution.py:678
  95.3 24.8 %collective-permute-start.22 = (bf16[1280,128]{1,0:T(8,128)(2,1)S(1)}, bf16[1280,128]{1,0:T(8,128)(2,1)S(1)}, u32[]{:S(2)}, u32[]{:S(2)}) collective-permute-start(bf16[1280,128]{1,0:T(8,128)(2,1)S(1)} %get-tuple-element.127), channel_id=1, source_target_pairs={{0,16},{1,17},{2,18},{3,19},{4,20},{5,21},{6,22},{7,23},{8,24},{9,... | collective-permute-start | bytes 983048 | tf_op jit(solution)/shard_map/ppermute | solution.py:678
  95.8 24.3 %collective-permute-start.21 = (bf16[1280,128]{1,0:T(8,128)(2,1)S(1)}, bf16[1280,128]{1,0:T(8,128)(2,1)S(1)}, u32[]{:S(2)}, u32[]{:S(2)}) collective-permute-start(bf16[1280,128]{1,0:T(8,128)(2,1)S(1)} %get-tuple-element.128), channel_id=1, source_target_pairs={{0,1},{1,0},{2,3},{3,2},{4,5},{5,4},{6,7},{7,6},{8,9},{9,8},{10,11... | collective-permute-start | bytes 983048 | tf_op jit(solution)/shard_map/ppermute | solution.py:678
  120.0 13.7 %collective-permute-start.24 = (bf16[1536,128]{1,0:T(8,128)(2,1)S(1)}, bf16[1536,128]{1,0:T(8,128)(2,1)S(1)}, u32[]{:S(2)}, u32[]{:S(2)}) collective-permute-start(bf16[1536,128]{1,0:T(8,128)(2,1)S(1)} %get-tuple-element.104), channel_id=1, source_target_pairs={{0,8},{1,9},{2,10},{3,11},{4,12},{5,13},{6,14},{7,15},{8,0},{9,1},... | collective-permute-start | bytes 1179656 | tf_op jit(solution)/shard_map/ppermute | solution.py:678
  120.4 13.5 %collective-permute-start.32 = (bf16[640,128]{1,0:T(8,128)(2,1)S(1)}, bf16[640,128]{1,0:T(8,128)(2,1)S(1)}, u32[]{:S(2)}, u32[]{:S(2)}) collective-permute-start(bf16[640,128]{1,0:T(8,128)(2,1)S(1)} %slice.258), channel_id=1, source_target_pairs={{0,2},{1,3},{2,0},{3,1},{4,6},{5,7},{6,4},{7,5},{8,10},{9,11},{10,... | collective-permute-start | bytes 491528 | tf_op jit(solution)/shard_map/ppermute | solution.py:678
  133.5 1.5 collective-permute-start.25
  135.2 10.8 %collective-permute-start.26 = (bf16[832,128]{1,0:T(8,128)(2,1)S(1)}, bf16[832,128]{1,0:T(8,128)(2,1)S(1)}, u32[]{:S(2)}, u32[]{:S(2)}) collective-permute-start(bf16[832,128]{1,0:T(8,128)(2,1)S(1)} %bitcast.50), channel_id=1, source_target_pairs={{0,1},{1,0},{2,3},{3,2},{4,5},{5,4},{6,7},{7,6},{8,9},{9,8},{10,11... | collective-permute-start | bytes 638984 | tf_op jit(solution)/shard_map/ppermute | solution.py:678
  136.0 11.7 %collective-permute-start.27 = (bf16[832,128]{1,0:T(8,128)(2,1)S(1)}, bf16[832,128]{1,0:T(8,128)(2,1)S(1)}, u32[]{:S(2)}, u32[]{:S(2)}) collective-permute-start(bf16[832,128]{1,0:T(8,128)(2,1)S(1)} %bitcast.52), channel_id=1, source_target_pairs={{0,16},{1,17},{2,18},{3,19},{4,20},{5,21},{6,22},{7,23},{8,24},{9,... | collective-permute-start | bytes 638984 | tf_op jit(solution)/shard_map/ppermute | solution.py:678
  137.6 10.1 %collective-permute-start.28 = (bf16[832,128]{1,0:T(8,128)(2,1)S(1)}, bf16[832,128]{1,0:T(8,128)(2,1)S(1)}, u32[]{:S(2)}, u32[]{:S(2)}) collective-permute-start(bf16[832,128]{1,0:T(8,128)(2,1)S(1)} %bitcast.53), channel_id=1, source_target_pairs={{0,17},{1,16},{2,19},{3,18},{4,21},{5,20},{6,23},{7,22},{8,25},{9,... | collective-permute-start | bytes 638984 | tf_op jit(solution)/shard_map/ppermute | solution.py:678
  143.9 8.4 %collective-permute-start.33 = (bf16[320,128]{1,0:T(8,128)(2,1)S(1)}, bf16[320,128]{1,0:T(8,128)(2,1)S(1)}, u32[]{:S(2)}, u32[]{:S(2)}) collective-permute-start(bf16[320,128]{1,0:T(8,128)(2,1)S(1)} %slice.259), channel_id=1, source_target_pairs={{0,4},{1,5},{2,6},{3,7},{4,0},{5,1},{6,2},{7,3},{8,12},{9,13},{10,... | collective-permute-start | bytes 245768 | tf_op jit(solution)/shard_map/ppermute | solution.py:678
  147.9 6.0 %collective-permute-start.31 = (bf16[208,128]{1,0:T(8,128)(2,1)S(1)}, bf16[208,128]{1,0:T(8,128)(2,1)S(1)}, u32[]{:S(2)}, u32[]{:S(2)}) collective-permute-start(bf16[208,128]{1,0:T(8,128)(2,1)S(1)} %get-tuple-element.141), channel_id=1, source_target_pairs={{0,6},{1,7},{2,4},{3,5},{4,2},{5,3},{6,0},{7,1},{8,14},{9,15},{10,... | collective-permute-start | bytes 159752 | tf_op jit(solution)/shard_map/ppermute | solution.py:678
  150.6 5.2 %collective-permute-start.30 = (bf16[208,128]{1,0:T(8,128)(2,1)S(1)}, bf16[208,128]{1,0:T(8,128)(2,1)S(1)}, u32[]{:S(2)}, u32[]{:S(2)}) collective-permute-start(bf16[208,128]{1,0:T(8,128)(2,1)S(1)} %get-tuple-element.142), channel_id=1, source_target_pairs={{0,4},{1,5},{2,6},{3,7},{4,0},{5,1},{6,2},{7,3},{8,12},{9,13},{10,... | collective-permute-start | bytes 159752 | tf_op jit(solution)/shard_map/ppermute | solution.py:678
  150.6 5.2 %collective-permute-start.29 = (bf16[208,128]{1,0:T(8,128)(2,1)S(1)}, bf16[208,128]{1,0:T(8,128)(2,1)S(1)}, u32[]{:S(2)}, u32[]{:S(2)}) collective-permute-start(bf16[208,128]{1,0:T(8,128)(2,1)S(1)} %get-tuple-element.143), channel_id=1, source_target_pairs={{0,2},{1,3},{2,0},{3,1},{4,6},{5,7},{6,4},{7,5},{8,10},{9,11},{10,... | collective-permute-start | bytes 159752 | tf_op jit(solution)/shard_map/ppermute | solution.py:678

commit v3 on v2

--- a/solution.py
+++ b/solution.py
@@ -24,7 +24,7 @@
 NN = (((1,), (0,)), ((), ()))
 TN = (((0,), (0,)), ((), ()))
 TT = (((0,), (1,)), ((), ()))
-VMEM_MIB = {"pack": 2, "project": 22, "attend": 18, "middle": 26, "attend_back": 28, "input_grad": 14, "unpack": 3}
+VMEM_MIB = {"pack": 2, "fetch": 4, "project": 22, "attend": 18, "middle": 26, "attend_back": 28, "input_grad": 14, "unpack": 3}
 
 
 def dot(a, b, dims):
@@ -72,7 +72,7 @@
 def pack_kernel(vec_width, me_ref, flat, vec, q_out, r_out, wide, line):
     wide[...] = flat[...].astype(f32)
     line[...] = jnp.zeros_like(line)
-    line[0:1, 0:vec_width] = vec[...].astype(f32)
+    line[0:1, 0:vec_width] = vec[...].astype(f32).reshape(1, vec_width)
     shifted = pltpu.roll(line[...], (me_ref[0] * vec_width) % 128, 1)
     parts = []
     for start, rows, count in PANELS:
@@ -99,11 +99,29 @@
     )(me, flat, vec)
 
 
-def project_kernel(masks, order, vec_width, me_ref, ends, tokens, *refs):
+def fetch_kernel(source, out, sem):
+    copy = pltpu.make_async_copy(source, out, sem)
+    copy.start()
+    copy.wait()
+
+
+def fetch(array):
+    return pl.pallas_call(
+        fetch_kernel,
+        in_specs=[pl.BlockSpec(memory_space=pl.ANY)],
+        out_specs=resident(),
+        out_shape=jax.ShapeDtypeStruct(array.shape, array.dtype),
+        scratch_shapes=[pltpu.SemaphoreType.DMA],
+        compiler_params=params("fetch"),
+        cost_estimate=cost(0, 2 * array.size * 2),
+        name="fetch",
+    )(array)
+
+
+def project_kernel(rows, masks, order, vec_width, me_ref, ends, tokens, *refs):
     pieces = refs[: len(masks)]
     qkv, keys_extra, query_extra, vec_out, weight, vec = refs[len(masks) :]
     step = pl.program_id(0)
-    rows = tokens.shape[0]
     me = me_ref[0]
 
     @pl.when(step == 0)
@@ -121,14 +139,14 @@
                 vec[pl.ds(row, 2), :] = vec[pl.ds(row, 2), :] + ref[at : at + 16, :].astype(f32)[0:2, :]
         vec_out[...] = vec[...]
 
-    x = tokens[...]
+    here = pl.ds(pl.multiple_of(step * rows, rows), rows)
+    x = tokens[here, :]
     scale = 1.0 / math.sqrt(HEAD_DIM)
     query_bias = jnp.concatenate([vec[j : j + 1, :] for j in range(4)], axis=1)
     value_bias = jnp.concatenate([vec[4 + j : 5 + j, :] for j in range(4)], axis=1)
     queries = ((dot(x, weight[0:512, :], NN) + query_bias) * scale).astype(bf16)
     key_heads = dot(x, weight[512:1024, :], NN).astype(bf16)
     values = (dot(x, weight[1024:1536, :], NN) + value_bias).astype(bf16)
-    here = pl.ds(pl.multiple_of(step * rows, rows), rows)
     qkv[here, 0:512] = queries
     qkv[here, 512:1024] = key_heads
     qkv[here, 1024:1536] = values
@@ -150,12 +168,12 @@
     count = tokens.shape[0]
     sets = ends.shape[1]
     return pl.pallas_call(
-        functools.partial(project_kernel, masks, order, vec_width),
+        functools.partial(project_kernel, rows, masks, order, vec_width),
         grid=(count // rows,),
         in_specs=[
             scalar_spec(),
             whole((1, sets)),
-            pl.BlockSpec((rows, 512), lambda i: (i, 0)),
+            resident(),
         ]
         + [resident() for _ in pieces],
         out_specs=[resident() for _ in range(5)],
@@ -738,13 +756,15 @@
         masks = [0] + spread
         masks = masks + [m + core for m in masks]
         me = owner[None]
-        q_block, r_block = pack(me, pltpu.with_memory_space_constraint(weights.reshape(512, 128), pltpu.HBM), vectors.reshape(1, vec_width), vec_width)
+        q_block, r_block = pack(me, pltpu.with_memory_space_constraint(weights.reshape(512, 128), pltpu.HBM), pltpu.with_memory_space_constraint(vectors, pltpu.HBM), vec_width)
         lines = [swap(q_block, step, count) for step in line[::-1]][::-1]
         q_far = jnp.concatenate([q_block, lines[0], lines[1], after(lines[2], ends)], axis=0)
         q_core = swap(q_far, core, count)
         q_pieces = [q_far] + [swap(q_far, step, count) for step in spread]
         r_far = gather_line(after(r_block, q_core), [z_far], count)
         r_far = gather_line(r_far, [z_near], count)
+        tokens = fetch(after(pltpu.with_memory_space_constraint(tokens, pltpu.HBM), q_far))
+        q_pieces[3] = after(q_pieces[3], tokens)
         q_pieces = q_pieces + [q_core] + [swap(piece, core, count) for piece in q_pieces[1:]]
         r_pieces = [swap(after(r_far, *q_pieces), step, count) for step in spread]
     else:
@@ -774,7 +794,7 @@
         q_pieces = [q_all[4 * i : 4 * i + 4].reshape(-1, 128) for i in range(8)]
         r_pieces = [r_all[4 * i : 4 * i + 4].reshape(-1, 128) for i in range(8)]
     qkv, keys_extra, query_extra, vec, weight = project(
-        me, ends, pltpu.with_memory_space_constraint(tokens, pltpu.HBM), q_pieces, masks, order_in, vec_width
+        me, ends, tokens, q_pieces, masks, order_in, vec_width
     )
     attended_a, offset_a = attend(qkv, query_extra, keys_extra, 0, 3)
     if fast:

time: 157 us -> 155 us (0.987)
  waiting for transfers between devices: 18.6 us -> 17 us
    ppermute x34, waiting for transfers between devices: 18.6 us -> 17 us  [swap(): return lax.ppermute(array, AXES, [(i, i ^ step) for i in range(count)])]
    pallas_call x1 -> x2, Pallas kernels: 5.47 us -> 5.84 us  [the longest x1 4.24 us: project(): pl.pallas_call(functools.partial(project_kernel, rows, masks, order, vec_...]
  transfers between devices with their start and end apart: 34 -> 34, of which waited for: 11 -> 11; matrix products, arithmetic and copies ran while one was open for 2% -> 2% of each run, Pallas kernels for 47% -> 48%
where the time goes in v3:
time: 155 us
  Pallas kernels  101 us (65%)
  starting transfers between devices  32.6 us (21%)
  waiting for transfers between devices  17 us (11%)
  other arithmetic  2.67 us (2%)
    pallas_call x3, Pallas kernels, attend_back(): pl.pallas_call(functools.partial(attend_back_kernel, base, heads, width,...  46.8 us
    ppermute x34, starting transfers between devices, swap(): return lax.ppermute(array, AXES, [(i, i ^ step) for i in range(count)])  32.6 us
    pallas_call x1, Pallas kernels, middle(): pl.pallas_call(functools.partial(middle_kernel, masks, order_in, order_ou...  25.2 us
    ppermute x34, waiting for transfers between devices, swap(): return lax.ppermute(array, AXES, [(i, i ^ step) for i in range(count)])  17 us
    pallas_call x2, Pallas kernels, attend(): pl.pallas_call(functools.partial(attend_kernel, base, rows), grid=(heads,...  16.4 us
    pallas_call x1, Pallas kernels, input_grad(): pl.pallas_call(functools.partial(input_grad_kernel, len(queries), rows),...  5.07 us
    pallas_call x1, Pallas kernels, project(): pl.pallas_call(functools.partial(project_kernel, rows, masks, order, vec_...  4.24 us
  transfers between devices with their start and end apart: 34, of which 11 were waited for; matrix products, arithmetic and copies ran while one was open for 2% of the time, Pallas kernels for 48%

profile of v3, /device:TPU:0, one launch (start us, length us, event | category | flops | bytes accessed | tf_op | source)
XLA Modules:
  0.0 154.7 jit_solution(13025542601100866249)
XLA Ops:
  0.6 1.0 pack.1
  1.6 5.1 %collective-permute-start.2 = (bf16[208,128]{1,0:T(8,128)(2,1)S(1)}, bf16[208,128]{1,0:T(8,128)(2,1)S(1)}, u32[]{:S(2)}, u32[]{:S(2)}) collective-permute-start(bf16[208,128]{1,0:T(8,128)(2,1)S(1)} %get-tuple-element.66), channel_id=1, source_target_pairs={{0,6},{1,7},{2,4},{3,5},{4,2},{5,3},{6,0},{7,1},{8,14},{9,15},{10,... | collective-permute-start | bytes 159752 | tf_op jit(solution)/shard_map/ppermute | solution.py:696
  6.7 0.6 collective-permute-start
  7.3 0.7 select_bitcast_fusion
  8.0 0.3 reduce-window.9
  8.6 0.8 bitcast_select_fusion
  9.3 1.5 collective-permute-done
  10.9 0.9 collective-permute-done.1
  11.8 1.6 %collective-permute-start.5 = (bf16[832,128]{1,0:T(8,128)(2,1)S(1)}, bf16[832,128]{1,0:T(8,128)(2,1)S(1)}, u32[]{:S(2)}, u32[]{:S(2)}) collective-permute-start(bf16[832,128]{1,0:T(8,128)(2,1)S(1)} %constant_dynamic-update-slice_fusion.refs_0_), channel_id=1, source_target_pairs={{0,1},{1,0},{2,3},{3,2},{4,5},{5,4},{6,7},{7,6},{8,9},{9,8},{10,11... | collective-permute-start | bytes 638984 | tf_op jit(solution)/shard_map/ppermute | solution.py:696
  13.4 1.5 collective-permute-start.4
  14.9 0.5 collective-permute-start.3
  15.4 1.6 %fetch.1.tokens = bf16[2048,512]{1,0:T(8,128)(2,1)S(1)} custom-call(bf16[2048,512]{1,0:T(8,128)(2,1)} %source), custom_call_target="tpu_custom_call" | custom-call | bytes 4194304 | tf_op jit(solution)/shard_map/fetch/pallas_call | solution.py:109
  17.0 2.1 %collective-permute-start.10 = (bf16[320,128]{1,0:T(8,128)(2,1)S(1)}, bf16[320,128]{1,0:T(8,128)(2,1)S(1)}, u32[]{:S(2)}, u32[]{:S(2)}) collective-permute-start(bf16[320,128]{1,0:T(8,128)(2,1)S(1)} %get-tuple-element.75), channel_id=1, source_target_pairs={{0,4},{1,5},{2,6},{3,7},{4,0},{5,1},{6,2},{7,3},{8,12},{9,13},{10,... | collective-permute-start | bytes 245768 | tf_op jit(solution)/shard_map/ppermute | solution.py:696
  19.2 0.8 collective-permute-done.5.refs_3_
  20.0 5.3 %collective-permute-done.4.refs_2_ = bf16[832,128]{1,0:T(8,128)(2,1)S(1)} collective-permute-done((bf16[832,128]{1,0:T(8,128)(2,1)S(1)}, bf16[832,128]{1,0:T(8,128)(2,1)S(1)}, u32[]{:S(2)}, u32[]{:S(2)}) %collective-permute-start.4) | collective-permute-done | bytes 213024 | tf_op jit(solution)/shard_map/ppermute | solution.py:696
  25.3 0.5 collective-permute-start.7
  25.8 1.0 collective-permute-start.11
  27.1 4.2 %project.1 = (bf16[2048,1536]{1,0:T(8,128)(2,1)S(1)}, bf16[2048,128]{1,0:T(8,128)(2,1)S(1)}, bf16[2048,128]{1,0:T(8,128)(2,1)S(1)}, f32[48,128]{1,0:T(8,128)S(1)}, bf16[1536,512]{1,0:T(8,128)(2,1)S(1)}) custom-call(s32[1]{0:T(128)} %bitcast.me_ref, s32[1,256]{1,0:T(1,128)S(1)} %bitcast.38, bf16[2048,512]{1,0:T(8,128)(2,1)S(1)} %fetch.1.tokens, ...), custom_call_target="tpu_custom_call" | custom-call | flops 3221225472 | bytes 12000000 | tf_op jit(solution)/shard_map/project/pallas_call | solution.py:170
  31.3 0.7 collective-permute-done.11
  32.0 1.3 collective-permute-start.14
  33.3 0.8 collective-permute-start.13
  34.2 1.4 collective-permute-start.12
  35.6 12.2 %attend.2 = (bf16[2048,384]{1,0:T(8,128)(2,1)S(1)}, f32[3,1,2048]{2,1,0:T(1,128)S(1)}) custom-call(bf16[2048,1536]{1,0:T(8,128)(2,1)S(1)} %get-tuple-element.70.qkv, bf16[2048,128]{1,0:T(8,128)(2,1)S(1)} %get-tuple-element.71.query_extra, bf16[2048,128]{1,0:T(8,128)(2,1)S(1)} %get-tuple-element.80.keys_extra), custom_call_target="tpu_custom_call" | custom-call | flops 12884901888 | bytes 6000000 | tf_op jit(solution)/shard_map/attend/pallas_call | solution.py:242
  47.9 1.5 collective-permute-done.13.refs_2_
  49.4 0.5 collective-permute-start.17
  49.9 4.2 %attend.3 = (bf16[2048,128]{1,0:T(8,128)(2,1)S(1)}, f32[1,1,2048]{2,1,0:T(1,128)S(1)}) custom-call(bf16[2048,1536]{1,0:T(8,128)(2,1)S(1)} %get-tuple-element.70.qkv, bf16[2048,128]{1,0:T(8,128)(2,1)S(1)} %get-tuple-element.71.query_extra, bf16[2048,128]{1,0:T(8,128)(2,1)S(1)} %get-tuple-element.80.keys_extra), custom_call_target="tpu_custom_call" | custom-call | flops 4294967296 | bytes 6000000 | tf_op jit(solution)/shard_map/attend/pallas_call | solution.py:242
  54.2 25.2 %middle.1 = (bf16[2048,512]{1,0:T(8,128)(2,1)}, bf16[2048,512]{1,0:T(8,128)(2,1)S(1)}, bf16[2048,512]{1,0:T(8,128)(2,1)S(1)}, bf16[2048,128]{1,0:T(8,128)(2,1)S(...) custom-call(s32[1]{0:T(128)} %bitcast.me_ref, ...), custom_call_target="tpu_custom_call" | custom-call | flops 16106127360 | bytes 22000000 | tf_op jit(solution)/shard_map/middle/pallas_call | solution.py:469
  79.4 0.5 collective-permute-start.20
  79.9 11.6 %attend_back.3 = (bf16[2048,128]{1,0:T(8,128)(2,1)S(1)}, bf16[128,2048]{1,0:T(8,128)(2,1)S(1)}, bf16[128,2048]{1,0:T(8,128)(2,1)S(1)}, bf16[768,128]{1,0:T(8,128...) custom-call(s32[1]{0:T(128)} %bitcast.me_ref, bf16[2048,512]{1,0:T(8,128)(2,1)S(1)} %fetch.1.tokens, ...), custom_call_target="tpu_custom_call" | custom-call | flops 10737418240 | bytes 12000000 | tf_op jit(solution)/shard_map/attend_back/pallas_call | solution.py:608
  91.5 0.3 add_convert_fusion
  91.8 1.6 %collective-permute-start.23 = (bf16[1280,128]{1,0:T(8,128)(2,1)S(1)}, bf16[1280,128]{1,0:T(8,128)(2,1)S(1)}, u32[]{:S(2)}, u32[]{:S(2)}) collective-permute-start(bf16[1280,128]{1,0:T(8,128)(2,1)S(1)} %get-tuple-element.130), channel_id=1, source_target_pairs={{0,17},{1,16},{2,19},{3,18},{4,21},{5,20},{6,23},{7,22},{8,25},{9,... | collective-permute-start | bytes 983048 | tf_op jit(solution)/shard_map/ppermute | solution.py:696
  93.4 0.5 collective-permute-start.22
  93.9 1.4 collective-permute-start.21
  95.3 23.0 %attend_back.4 = (bf16[2048,256]{1,0:T(8,128)(2,1)S(1)}, bf16[256,2048]{1,0:T(8,128)(2,1)S(1)}, bf16[256,2048]{1,0:T(8,128)(2,1)S(1)}, bf16[1536,128]{1,0:T(8,12...) custom-call(s32[1]{0:T(128)} %bitcast.me_ref, bf16[2048,512]{1,0:T(8,128)(2,1)S(1)} %fetch.1.tokens, ...), custom_call_target="tpu_custom_call" | custom-call | flops 21474836480 | bytes 24000000 | tf_op jit(solution)/shard_map/attend_back/pallas_call | solution.py:608
  118.7 1.0 collective-permute-start.32
  119.6 12.3 %attend_back.5 = (bf16[2048,128]{1,0:T(8,128)(2,1)S(1)}, bf16[128,2048]{1,0:T(8,128)(2,1)S(1)}, bf16[128,2048]{1,0:T(8,128)(2,1)S(1)}, bf16[1024,128]{1,0:T(8,12...) custom-call(s32[1]{0:T(128)} %bitcast.me_ref, bf16[2048,512]{1,0:T(8,128)(2,1)S(1)} %fetch.1.tokens, ...), custom_call_target="tpu_custom_call" | custom-call | flops 10737418240 | bytes 12000000 | tf_op jit(solution)/shard_map/attend_back/pallas_call | solution.py:608
  132.4 1.1 collective-permute-done.25
  133.6 0.7 collective-permute-start.26
  134.3 1.6 %collective-permute-start.27 = (bf16[832,128]{1,0:T(8,128)(2,1)S(1)}, bf16[832,128]{1,0:T(8,128)(2,1)S(1)}, u32[]{:S(2)}, u32[]{:S(2)}) collective-permute-start(bf16[832,128]{1,0:T(8,128)(2,1)S(1)} %bitcast.52), channel_id=1, source_target_pairs={{0,16},{1,17},{2,18},{3,19},{4,20},{5,21},{6,22},{7,23},{8,24},{9,... | collective-permute-start | bytes 638984 | tf_op jit(solution)/shard_map/ppermute | solution.py:696
  135.9 1.4 collective-permute-start.28
  137.3 5.1 %input_grad.1 = f32[2048,512]{1,0:T(8,128)} custom-call(bf16[2048,512]{1,0:T(8,128)(2,1)S(1)} %get-tuple-element.113.refs_0_, bf16[2048,128]{1,0:T(8,128)(2,1)S(1)} %get-tuple-element.96.refs_1_, bf16[2048,256]{1,0:T(8,128)(2,1)S(1)} %get-tuple-element.100.refs_2_, bf16[2048,128]{1,0:T(8,128)(2,1)S(1)} %get-tuple-element.105.refs_3_, ...), custom_call_target="tpu_custom_call" | custom-call | flops 3221225472 | bytes 16000000 | tf_op jit(solution)/shard_map/input_grad/pallas_call | solution.py:650
  142.4 2.0 %collective-permute-start.33 = (bf16[320,128]{1,0:T(8,128)(2,1)S(1)}, bf16[320,128]{1,0:T(8,128)(2,1)S(1)}, u32[]{:S(2)}, u32[]{:S(2)}) collective-permute-start(bf16[320,128]{1,0:T(8,128)(2,1)S(1)} %slice.259), channel_id=1, source_target_pairs={{0,4},{1,5},{2,6},{3,7},{4,0},{5,1},{6,2},{7,3},{8,12},{9,13},{10,... | collective-permute-start | bytes 245768 | tf_op jit(solution)/shard_map/ppermute | solution.py:696
  144.4 1.6 %collective-permute-done.27 = bf16[832,128]{1,0:T(8,128)(2,1)S(1)} collective-permute-done((bf16[832,128]{1,0:T(8,128)(2,1)S(1)}, bf16[832,128]{1,0:T(8,128)(2,1)S(1)}, u32[]{:S(2)}, u32[]{:S(2)}) %collective-permute-start.27) | collective-permute-done | bytes 213024 | tf_op jit(solution)/shard_map/ppermute | solution.py:696
  146.1 2.7 %collective-permute-start.31 = (bf16[208,128]{1,0:T(8,128)(2,1)S(1)}, bf16[208,128]{1,0:T(8,128)(2,1)S(1)}, u32[]{:S(2)}, u32[]{:S(2)}) collective-permute-start(bf16[208,128]{1,0:T(8,128)(2,1)S(1)} %get-tuple-element.145), channel_id=1, source_target_pairs={{0,6},{1,7},{2,4},{3,5},{4,2},{5,3},{6,0},{7,1},{8,14},{9,15},{10,... | collective-permute-start | bytes 159752 | tf_op jit(solution)/shard_map/ppermute | solution.py:696
  148.8 1.8 %collective-permute-start.29 = (bf16[208,128]{1,0:T(8,128)(2,1)S(1)}, bf16[208,128]{1,0:T(8,128)(2,1)S(1)}, u32[]{:S(2)}, u32[]{:S(2)}) collective-permute-start(bf16[208,128]{1,0:T(8,128)(2,1)S(1)} %get-tuple-element.147), channel_id=1, source_target_pairs={{0,2},{1,3},{2,0},{3,1},{4,6},{5,7},{6,4},{7,5},{8,10},{9,11},{10,... | collective-permute-start | bytes 159752 | tf_op jit(solution)/shard_map/ppermute | solution.py:696
  150.6 1.5 collective-permute-done.31.refs_3_
  152.1 1.9 %collective-permute-done.30.refs_2_ = bf16[208,128]{1,0:T(8,128)(2,1)S(1)} collective-permute-done((bf16[208,128]{1,0:T(8,128)(2,1)S(1)}, bf16[208,128]{1,0:T(8,128)(2,1)S(1)}, u32[]{:S(2)}, u32[]{:S(2)}) %collective-permute-start.30) | collective-permute-done | bytes 53280 | tf_op jit(solution)/shard_map/ppermute | solution.py:696
  154.0 0.8 unpack.1
  (62 shorter events, 1.8 us)
Async XLA Ops:
  1.6 9.2 %collective-permute-start.2 = (bf16[208,128]{1,0:T(8,128)(2,1)S(1)}, bf16[208,128]{1,0:T(8,128)(2,1)S(1)}, u32[]{:S(2)}, u32[]{:S(2)}) collective-permute-start(bf16[208,128]{1,0:T(8,128)(2,1)S(1)} %get-tuple-element.66), channel_id=1, source_target_pairs={{0,6},{1,7},{2,4},{3,5},{4,2},{5,3},{6,0},{7,1},{8,14},{9,15},{10,... | collective-permute-start | bytes 159752 | tf_op jit(solution)/shard_map/ppermute | solution.py:696
  6.7 5.0 %collective-permute-start.1 = (bf16[208,128]{1,0:T(8,128)(2,1)S(1)}, bf16[208,128]{1,0:T(8,128)(2,1)S(1)}, u32[]{:S(2)}, u32[]{:S(2)}) collective-permute-start(bf16[208,128]{1,0:T(8,128)(2,1)S(1)} %get-tuple-element.66), channel_id=1, source_target_pairs={{0,4},{1,5},{2,6},{3,7},{4,0},{5,1},{6,2},{7,3},{8,12},{9,13},{10,... | collective-permute-start | bytes 159752 | tf_op jit(solution)/shard_map/ppermute | solution.py:696
  6.7 4.1 %collective-permute-start = (bf16[208,128]{1,0:T(8,128)(2,1)S(1)}, bf16[208,128]{1,0:T(8,128)(2,1)S(1)}, u32[]{:S(2)}, u32[]{:S(2)}) collective-permute-start(bf16[208,128]{1,0:T(8,128)(2,1)S(1)} %get-tuple-element.66), channel_id=1, source_target_pairs={{0,2},{1,3},{2,0},{3,1},{4,6},{5,7},{6,4},{7,5},{8,10},{9,11},{10,... | collective-permute-start | bytes 159752 | tf_op jit(solution)/shard_map/ppermute | solution.py:696
  11.8 5.2 %collective-permute-start.6 = (bf16[832,128]{1,0:T(8,128)(2,1)S(1)}, bf16[832,128]{1,0:T(8,128)(2,1)S(1)}, u32[]{:S(2)}, u32[]{:S(2)}) collective-permute-start(bf16[832,128]{1,0:T(8,128)(2,1)S(1)} %constant_dynamic-update-slice_fusion.refs_0_), channel_id=1, source_target_pairs={{0,8},{1,9},{2,10},{3,11},{4,12},{5,13},{6,14},{7,15},{8,0},{9,1},... | collective-permute-start | bytes 638984 | tf_op jit(solution)/shard_map/ppermute | solution.py:696
  11.8 8.1 %collective-permute-start.5 = (bf16[832,128]{1,0:T(8,128)(2,1)S(1)}, bf16[832,128]{1,0:T(8,128)(2,1)S(1)}, u32[]{:S(2)}, u32[]{:S(2)}) collective-permute-start(bf16[832,128]{1,0:T(8,128)(2,1)S(1)} %constant_dynamic-update-slice_fusion.refs_0_), channel_id=1, source_target_pairs={{0,1},{1,0},{2,3},{3,2},{4,5},{5,4},{6,7},{7,6},{8,9},{9,8},{10,11... | collective-permute-start | bytes 638984 | tf_op jit(solution)/shard_map/ppermute | solution.py:696
  13.4 11.9 %collective-permute-start.4 = (bf16[832,128]{1,0:T(8,128)(2,1)S(1)}, bf16[832,128]{1,0:T(8,128)(2,1)S(1)}, u32[]{:S(2)}, u32[]{:S(2)}) collective-permute-start(bf16[832,128]{1,0:T(8,128)(2,1)S(1)} %constant_dynamic-update-slice_fusion.refs_0_), channel_id=1, source_target_pairs={{0,16},{1,17},{2,18},{3,19},{4,20},{5,21},{6,22},{7,23},{8,24},{9,... | collective-permute-start | bytes 638984 | tf_op jit(solution)/shard_map/ppermute | solution.py:696
  14.9 10.4 %collective-permute-start.3 = (bf16[832,128]{1,0:T(8,128)(2,1)S(1)}, bf16[832,128]{1,0:T(8,128)(2,1)S(1)}, u32[]{:S(2)}, u32[]{:S(2)}) collective-permute-start(bf16[832,128]{1,0:T(8,128)(2,1)S(1)} %constant_dynamic-update-slice_fusion.refs_0_), channel_id=1, source_target_pairs={{0,17},{1,16},{2,19},{3,18},{4,21},{5,20},{6,23},{7,22},{8,25},{9,... | collective-permute-start | bytes 638984 | tf_op jit(solution)/shard_map/ppermute | solution.py:696
  17.0 8.8 %collective-permute-start.10 = (bf16[320,128]{1,0:T(8,128)(2,1)S(1)}, bf16[320,128]{1,0:T(8,128)(2,1)S(1)}, u32[]{:S(2)}, u32[]{:S(2)}) collective-permute-start(bf16[320,128]{1,0:T(8,128)(2,1)S(1)} %get-tuple-element.75), channel_id=1, source_target_pairs={{0,4},{1,5},{2,6},{3,7},{4,0},{5,1},{6,2},{7,3},{8,12},{9,13},{10,... | collective-permute-start | bytes 245768 | tf_op jit(solution)/shard_map/ppermute | solution.py:696
  20.0 7.1 %collective-permute-start.9 = (bf16[832,128]{1,0:T(8,128)(2,1)S(1)}, bf16[832,128]{1,0:T(8,128)(2,1)S(1)}, u32[]{:S(2)}, u32[]{:S(2)}) collective-permute-start(bf16[832,128]{1,0:T(8,128)(2,1)S(1)} %collective-permute-done.5.refs_3_), channel_id=1, source_target_pairs={{0,8},{1,9},{2,10},{3,11},{4,12},{5,13},{6,14},{7,15},{8,0},{9,1},... | collective-permute-start | bytes 638984 | tf_op jit(solution)/shard_map/ppermute | solution.py:696
  25.3 1.5 collective-permute-start.8
  25.3 1.8 %collective-permute-start.7 = (bf16[832,128]{1,0:T(8,128)(2,1)S(1)}, bf16[832,128]{1,0:T(8,128)(2,1)S(1)}, u32[]{:S(2)}, u32[]{:S(2)}) collective-permute-start(bf16[832,128]{1,0:T(8,128)(2,1)S(1)} %collective-permute-done.3.refs_1_), channel_id=1, source_target_pairs={{0,8},{1,9},{2,10},{3,11},{4,12},{5,13},{6,14},{7,15},{8,0},{9,1},... | collective-permute-start | bytes 638984 | tf_op jit(solution)/shard_map/ppermute | solution.py:696
  25.8 6.2 %collective-permute-start.11 = (bf16[640,128]{1,0:T(8,128)(2,1)S(1)}, bf16[640,128]{1,0:T(8,128)(2,1)S(1)}, u32[]{:S(2)}, u32[]{:S(2)}) collective-permute-start(bf16[640,128]{1,0:T(8,128)(2,1)S(1)} %pad_maximum_fusion.3), channel_id=1, source_target_pairs={{0,2},{1,3},{2,0},{3,1},{4,6},{5,7},{6,4},{7,5},{8,10},{9,11},{10,... | collective-permute-start | bytes 491528 | tf_op jit(solution)/shard_map/ppermute | solution.py:696
  32.0 15.9 %collective-permute-start.14 = (bf16[1280,128]{1,0:T(8,128)(2,1)S(1)}, bf16[1280,128]{1,0:T(8,128)(2,1)S(1)}, u32[]{:S(2)}, u32[]{:S(2)}) collective-permute-start(bf16[1280,128]{1,0:T(8,128)(2,1)S(1)} %constant_dynamic-update-slice_fusion.4.refs_0_), channel_id=1, source_target_pairs={{0,1},{1,0},{2,3},{3,2},{4,5},{5,4},{6,7},{7,6},{8,9},{9,8},{10,11... | collective-permute-start | bytes 983048 | tf_op jit(solution)/shard_map/ppermute | solution.py:696
  33.3 16.1 %collective-permute-start.13 = (bf16[1280,128]{1,0:T(8,128)(2,1)S(1)}, bf16[1280,128]{1,0:T(8,128)(2,1)S(1)}, u32[]{:S(2)}, u32[]{:S(2)}) collective-permute-start(bf16[1280,128]{1,0:T(8,128)(2,1)S(1)} %constant_dynamic-update-slice_fusion.4.refs_0_), channel_id=1, source_target_pairs={{0,16},{1,17},{2,18},{3,19},{4,20},{5,21},{6,22},{7,23},{8,24},{9,... | collective-permute-start | bytes 983048 | tf_op jit(solution)/shard_map/ppermute | solution.py:696
  34.2 15.2 %collective-permute-start.12 = (bf16[1280,128]{1,0:T(8,128)(2,1)S(1)}, bf16[1280,128]{1,0:T(8,128)(2,1)S(1)}, u32[]{:S(2)}, u32[]{:S(2)}) collective-permute-start(bf16[1280,128]{1,0:T(8,128)(2,1)S(1)} %constant_dynamic-update-slice_fusion.4.refs_0_), channel_id=1, source_target_pairs={{0,17},{1,16},{2,19},{3,18},{4,21},{5,20},{6,23},{7,22},{8,25},{9,... | collective-permute-start | bytes 983048 | tf_op jit(solution)/shard_map/ppermute | solution.py:696
  47.8 6.3 %collective-permute-start.15 = (bf16[1280,128]{1,0:T(8,128)(2,1)S(1)}, bf16[1280,128]{1,0:T(8,128)(2,1)S(1)}, u32[]{:S(2)}, u32[]{:S(2)}) collective-permute-start(bf16[1280,128]{1,0:T(8,128)(2,1)S(1)} %constant_dynamic-update-slice_fusion.4.refs_0_), channel_id=1, source_target_pairs={{0,8},{1,9},{2,10},{3,11},{4,12},{5,13},{6,14},{7,15},{8,0},{9,1},... | collective-permute-start | bytes 983048 | tf_op jit(solution)/shard_map/ppermute | solution.py:696
  47.9 6.2 %copy-start = (bf16[2048,512]{1,0:T(8,128)(2,1)S(1)}, bf16[2048,512]{1,0:T(8,128)(2,1)}, u32[]{:S(2)}) copy-start(bf16[2048,512]{1,0:T(8,128)(2,1)} %cotangent.1) | copy-start | bytes 6291460
  49.4 4.7 %collective-permute-start.16 = (bf16[1280,128]{1,0:T(8,128)(2,1)S(1)}, bf16[1280,128]{1,0:T(8,128)(2,1)S(1)}, u32[]{:S(2)}, u32[]{:S(2)}) collective-permute-start(bf16[1280,128]{1,0:T(8,128)(2,1)S(1)} %collective-permute-done.12.refs_1_), channel_id=1, source_target_pairs={{0,8},{1,9},{2,10},{3,11},{4,12},{5,13},{6,14},{7,15},{8,0},{9,1},... | collective-permute-start | bytes 983048 | tf_op jit(solution)/shard_map/ppermute | solution.py:696
  49.4 4.7 %collective-permute-start.17 = (bf16[1280,128]{1,0:T(8,128)(2,1)S(1)}, bf16[1280,128]{1,0:T(8,128)(2,1)S(1)}, u32[]{:S(2)}, u32[]{:S(2)}) collective-permute-start(bf16[1280,128]{1,0:T(8,128)(2,1)S(1)} %collective-permute-done.13.refs_2_), channel_id=1, source_target_pairs={{0,8},{1,9},{2,10},{3,11},{4,12},{5,13},{6,14},{7,15},{8,0},{9,1},... | collective-permute-start | bytes 983048 | tf_op jit(solution)/shard_map/ppermute | solution.py:696
  49.9 4.2 %collective-permute-start.18 = (bf16[1280,128]{1,0:T(8,128)(2,1)S(1)}, bf16[1280,128]{1,0:T(8,128)(2,1)S(1)}, u32[]{:S(2)}, u32[]{:S(2)}) collective-permute-start(bf16[1280,128]{1,0:T(8,128)(2,1)S(1)} %collective-permute-done.14.refs_3_), channel_id=1, source_target_pairs={{0,8},{1,9},{2,10},{3,11},{4,12},{5,13},{6,14},{7,15},{8,0},{9,1},... | collective-permute-start | bytes 983048 | tf_op jit(solution)/shard_map/ppermute | solution.py:696
  79.4 12.2 %collective-permute-start.20 = (bf16[5120,128]{1,0:T(8,128)(2,1)S(1)}, bf16[5120,128]{1,0:T(8,128)(2,1)S(1)}, u32[]{:S(2)}, u32[]{:S(2)}) collective-permute-start(bf16[5120,128]{1,0:T(8,128)(2,1)S(1)} %get-tuple-element.95), channel_id=1, source_target_pairs={{0,8},{1,9},{2,10},{3,11},{4,12},{5,13},{6,14},{7,15},{8,0},{9,1},... | collective-permute-start | bytes 3932168 | tf_op jit(solution)/shard_map/ppermute | solution.py:696
  91.4 40.5 %collective-permute-start.19 = (bf16[768,128]{1,0:T(8,128)(2,1)S(1)}, bf16[768,128]{1,0:T(8,128)(2,1)S(1)}, u32[]{:S(2)}, u32[]{:S(2)}) collective-permute-start(bf16[768,128]{1,0:T(8,128)(2,1)S(1)} %get-tuple-element.92), channel_id=1, source_target_pairs={{0,8},{1,9},{2,10},{3,11},{4,12},{5,13},{6,14},{7,15},{8,0},{9,1},... | collective-permute-start | bytes 589832 | tf_op jit(solution)/shard_map/ppermute | solution.py:696
  91.8 26.6 %collective-permute-start.23 = (bf16[1280,128]{1,0:T(8,128)(2,1)S(1)}, bf16[1280,128]{1,0:T(8,128)(2,1)S(1)}, u32[]{:S(2)}, u32[]{:S(2)}) collective-permute-start(bf16[1280,128]{1,0:T(8,128)(2,1)S(1)} %get-tuple-element.130), channel_id=1, source_target_pairs={{0,17},{1,16},{2,19},{3,18},{4,21},{5,20},{6,23},{7,22},{8,25},{9,... | collective-permute-start | bytes 983048 | tf_op jit(solution)/shard_map/ppermute | solution.py:696
  93.4 25.0 %collective-permute-start.22 = (bf16[1280,128]{1,0:T(8,128)(2,1)S(1)}, bf16[1280,128]{1,0:T(8,128)(2,1)S(1)}, u32[]{:S(2)}, u32[]{:S(2)}) collective-permute-start(bf16[1280,128]{1,0:T(8,128)(2,1)S(1)} %get-tuple-element.131), channel_id=1, source_target_pairs={{0,16},{1,17},{2,18},{3,19},{4,20},{5,21},{6,22},{7,23},{8,24},{9,... | collective-permute-start | bytes 983048 | tf_op jit(solution)/shard_map/ppermute | solution.py:696
  93.9 24.5 %collective-permute-start.21 = (bf16[1280,128]{1,0:T(8,128)(2,1)S(1)}, bf16[1280,128]{1,0:T(8,128)(2,1)S(1)}, u32[]{:S(2)}, u32[]{:S(2)}) collective-permute-start(bf16[1280,128]{1,0:T(8,128)(2,1)S(1)} %get-tuple-element.132), channel_id=1, source_target_pairs={{0,1},{1,0},{2,3},{3,2},{4,5},{5,4},{6,7},{7,6},{8,9},{9,8},{10,11... | collective-permute-start | bytes 983048 | tf_op jit(solution)/shard_map/ppermute | solution.py:696
  118.3 13.8 %collective-permute-start.24 = (bf16[1536,128]{1,0:T(8,128)(2,1)S(1)}, bf16[1536,128]{1,0:T(8,128)(2,1)S(1)}, u32[]{:S(2)}, u32[]{:S(2)}) collective-permute-start(bf16[1536,128]{1,0:T(8,128)(2,1)S(1)} %get-tuple-element.108), channel_id=1, source_target_pairs={{0,8},{1,9},{2,10},{3,11},{4,12},{5,13},{6,14},{7,15},{8,0},{9,1},... | collective-permute-start | bytes 1179656 | tf_op jit(solution)/shard_map/ppermute | solution.py:696
  118.7 13.6 %collective-permute-start.32 = (bf16[640,128]{1,0:T(8,128)(2,1)S(1)}, bf16[640,128]{1,0:T(8,128)(2,1)S(1)}, u32[]{:S(2)}, u32[]{:S(2)}) collective-permute-start(bf16[640,128]{1,0:T(8,128)(2,1)S(1)} %slice.258), channel_id=1, source_target_pairs={{0,2},{1,3},{2,0},{3,1},{4,6},{5,7},{6,4},{7,5},{8,10},{9,11},{10,... | collective-permute-start | bytes 491528 | tf_op jit(solution)/shard_map/ppermute | solution.py:696
  131.9 1.5 collective-permute-start.25
  133.6 10.8 %collective-permute-start.26 = (bf16[832,128]{1,0:T(8,128)(2,1)S(1)}, bf16[832,128]{1,0:T(8,128)(2,1)S(1)}, u32[]{:S(2)}, u32[]{:S(2)}) collective-permute-start(bf16[832,128]{1,0:T(8,128)(2,1)S(1)} %bitcast.50), channel_id=1, source_target_pairs={{0,1},{1,0},{2,3},{3,2},{4,5},{5,4},{6,7},{7,6},{8,9},{9,8},{10,11... | collective-permute-start | bytes 638984 | tf_op jit(solution)/shard_map/ppermute | solution.py:696
  134.3 11.7 %collective-permute-start.27 = (bf16[832,128]{1,0:T(8,128)(2,1)S(1)}, bf16[832,128]{1,0:T(8,128)(2,1)S(1)}, u32[]{:S(2)}, u32[]{:S(2)}) collective-permute-start(bf16[832,128]{1,0:T(8,128)(2,1)S(1)} %bitcast.52), channel_id=1, source_target_pairs={{0,16},{1,17},{2,18},{3,19},{4,20},{5,21},{6,22},{7,23},{8,24},{9,... | collective-permute-start | bytes 638984 | tf_op jit(solution)/shard_map/ppermute | solution.py:696
  135.9 10.1 %collective-permute-start.28 = (bf16[832,128]{1,0:T(8,128)(2,1)S(1)}, bf16[832,128]{1,0:T(8,128)(2,1)S(1)}, u32[]{:S(2)}, u32[]{:S(2)}) collective-permute-start(bf16[832,128]{1,0:T(8,128)(2,1)S(1)} %bitcast.53), channel_id=1, source_target_pairs={{0,17},{1,16},{2,19},{3,18},{4,21},{5,20},{6,23},{7,22},{8,25},{9,... | collective-permute-start | bytes 638984 | tf_op jit(solution)/shard_map/ppermute | solution.py:696
  142.4 8.2 %collective-permute-start.33 = (bf16[320,128]{1,0:T(8,128)(2,1)S(1)}, bf16[320,128]{1,0:T(8,128)(2,1)S(1)}, u32[]{:S(2)}, u32[]{:S(2)}) collective-permute-start(bf16[320,128]{1,0:T(8,128)(2,1)S(1)} %slice.259), channel_id=1, source_target_pairs={{0,4},{1,5},{2,6},{3,7},{4,0},{5,1},{6,2},{7,3},{8,12},{9,13},{10,... | collective-permute-start | bytes 245768 | tf_op jit(solution)/shard_map/ppermute | solution.py:696
  146.1 6.0 %collective-permute-start.31 = (bf16[208,128]{1,0:T(8,128)(2,1)S(1)}, bf16[208,128]{1,0:T(8,128)(2,1)S(1)}, u32[]{:S(2)}, u32[]{:S(2)}) collective-permute-start(bf16[208,128]{1,0:T(8,128)(2,1)S(1)} %get-tuple-element.145), channel_id=1, source_target_pairs={{0,6},{1,7},{2,4},{3,5},{4,2},{5,3},{6,0},{7,1},{8,14},{9,15},{10,... | collective-permute-start | bytes 159752 | tf_op jit(solution)/shard_map/ppermute | solution.py:696
  148.8 5.2 %collective-permute-start.30 = (bf16[208,128]{1,0:T(8,128)(2,1)S(1)}, bf16[208,128]{1,0:T(8,128)(2,1)S(1)}, u32[]{:S(2)}, u32[]{:S(2)}) collective-permute-start(bf16[208,128]{1,0:T(8,128)(2,1)S(1)} %get-tuple-element.146), channel_id=1, source_target_pairs={{0,4},{1,5},{2,6},{3,7},{4,0},{5,1},{6,2},{7,3},{8,12},{9,13},{10,... | collective-permute-start | bytes 159752 | tf_op jit(solution)/shard_map/ppermute | solution.py:696
  148.8 5.2 %collective-permute-start.29 = (bf16[208,128]{1,0:T(8,128)(2,1)S(1)}, bf16[208,128]{1,0:T(8,128)(2,1)S(1)}, u32[]{:S(2)}, u32[]{:S(2)}) collective-permute-start(bf16[208,128]{1,0:T(8,128)(2,1)S(1)} %get-tuple-element.147), channel_id=1, source_target_pairs={{0,2},{1,3},{2,0},{3,1},{4,6},{5,7},{6,4},{7,5},{8,10},{9,11},{10,... | collective-permute-start | bytes 159752 | tf_op jit(solution)/shard_map/ppermute | solution.py:696

commit v4 on v3

--- a/solution.py
+++ b/solution.py
@@ -24,7 +24,7 @@
 NN = (((1,), (0,)), ((), ()))
 TN = (((0,), (0,)), ((), ()))
 TT = (((0,), (1,)), ((), ()))
-VMEM_MIB = {"pack": 2, "fetch": 4, "project": 22, "attend": 18, "middle": 26, "attend_back": 28, "input_grad": 14, "unpack": 3}
+VMEM_MIB = {"pack": 2, "fetch": 4, "project": 22, "attend": 30, "middle": 26, "attend_back": 28, "input_grad": 14, "unpack": 3}
 
 
 def dot(a, b, dims):
@@ -237,7 +237,7 @@
     offset_out[local, :, here] = peak[...] + jnp.log(total[...])
 
 
-def attend(qkv, query_extra, keys_extra, base, heads, rows=1024):
+def attend(qkv, query_extra, keys_extra, base, heads, rows=2048):
     count = qkv.shape[0]
     return pl.pallas_call(
         functools.partial(attend_kernel, base, rows),
@@ -765,6 +765,7 @@
         r_far = gather_line(r_far, [z_near], count)
         tokens = fetch(after(pltpu.with_memory_space_constraint(tokens, pltpu.HBM), q_far))
         q_pieces[3] = after(q_pieces[3], tokens)
+        q_pieces[1] = after(q_pieces[1], r_far)
         q_pieces = q_pieces + [q_core] + [swap(piece, core, count) for piece in q_pieces[1:]]
         r_pieces = [swap(after(r_far, *q_pieces), step, count) for step in spread]
     else:

time: 155 us -> 155 us (level)
  waiting for transfers between devices: 17 us -> 19.3 us
    ppermute x34, waiting for transfers between devices: 17 us -> 19.3 us  [swap(): return lax.ppermute(array, AXES, [(i, i ^ step) for i in range(count)])]
  transfers between devices with their start and end apart: 34 -> 34, of which waited for: 11 -> 12; matrix products, arithmetic and copies ran while one was open for 2% -> 2% of each run, Pallas kernels for 48% -> 47%
where the time goes in v4:
time: 155 us; the launch traced here: 154 us
  Pallas kernels  99.6 us (64%)
  starting transfers between devices  31.4 us (20%)
  waiting for transfers between devices  19.3 us (12%)
  other arithmetic  2.66 us (2%)
    pallas_call x3, Pallas kernels, attend_back(): pl.pallas_call(functools.partial(attend_back_kernel, base, heads, width,...  46.8 us
    ppermute x34, starting transfers between devices, swap(): return lax.ppermute(array, AXES, [(i, i ^ step) for i in range(count)])  31.4 us
    pallas_call x1, Pallas kernels, middle(): pl.pallas_call(functools.partial(middle_kernel, masks, order_in, order_ou...  25 us
    ppermute x34, waiting for transfers between devices, swap(): return lax.ppermute(array, AXES, [(i, i ^ step) for i in range(count)])  19.3 us
    pallas_call x2, Pallas kernels, attend(): pl.pallas_call(functools.partial(attend_kernel, base, rows), grid=(heads,...  15.2 us
    pallas_call x1, Pallas kernels, input_grad(): pl.pallas_call(functools.partial(input_grad_kernel, len(queries), rows),...  5.08 us
    pallas_call x1, Pallas kernels, project(): pl.pallas_call(functools.partial(project_kernel, rows, masks, order, vec_...  4.24 us
  transfers between devices with their start and end apart: 34, of which 12 were waited for; matrix products, arithmetic and copies ran while one was open for 2% of the time, Pallas kernels for 47%

profile of v4, /device:TPU:0, one launch (start us, length us, event | category | flops | bytes accessed | tf_op | source)
XLA Modules:
  0.0 154.4 jit_solution(8022998955409344915)
XLA Ops:
  0.6 1.0 pack.1
  1.6 5.1 %collective-permute-start.2 = (bf16[208,128]{1,0:T(8,128)(2,1)S(1)}, bf16[208,128]{1,0:T(8,128)(2,1)S(1)}, u32[]{:S(2)}, u32[]{:S(2)}) collective-permute-start(bf16[208,128]{1,0:T(8,128)(2,1)S(1)} %get-tuple-element.67), channel_id=1, source_target_pairs={{0,6},{1,7},{2,4},{3,5},{4,2},{5,3},{6,0},{7,1},{8,14},{9,15},{10,... | collective-permute-start | bytes 159752 | tf_op jit(solution)/shard_map/ppermute | solution.py:696
  6.7 0.6 collective-permute-start
  7.3 0.7 select_bitcast_fusion
  8.6 0.8 bitcast_select_fusion
  9.3 1.5 collective-permute-done
  10.9 0.9 collective-permute-done.1
  11.8 1.5 collective-permute-done.4.refs_4_
  13.3 2.1 %collective-permute-start.5 = (bf16[320,128]{1,0:T(8,128)(2,1)S(1)}, bf16[320,128]{1,0:T(8,128)(2,1)S(1)}, u32[]{:S(2)}, u32[]{:S(2)}) collective-permute-start(bf16[320,128]{1,0:T(8,128)(2,1)S(1)} %get-tuple-element.71), channel_id=1, source_target_pairs={{0,4},{1,5},{2,6},{3,7},{4,0},{5,1},{6,2},{7,3},{8,12},{9,13},{10,... | collective-permute-start | bytes 245768 | tf_op jit(solution)/shard_map/ppermute | solution.py:696
  15.4 1.5 collective-permute-start.8
  16.9 1.5 collective-permute-start.7
  18.4 0.5 collective-permute-start.3
  18.9 1.6 %fetch.1.tokens = bf16[2048,512]{1,0:T(8,128)(2,1)S(1)} custom-call(bf16[2048,512]{1,0:T(8,128)(2,1)} %source), custom_call_target="tpu_custom_call" | custom-call | bytes 4194304 | tf_op jit(solution)/shard_map/fetch/pallas_call | solution.py:109
  20.5 0.9 collective-permute-start.6
  21.4 2.1 %collective-permute-done.8.refs_3_ = bf16[832,128]{1,0:T(8,128)(2,1)S(1)} collective-permute-done((bf16[832,128]{1,0:T(8,128)(2,1)S(1)}, bf16[832,128]{1,0:T(8,128)(2,1)S(1)}, u32[]{:S(2)}, u32[]{:S(2)}) %collective-permute-start.8) | collective-permute-done | bytes 213024 | tf_op jit(solution)/shard_map/ppermute | solution.py:696
  23.5 4.7 %collective-permute-done.7.refs_2_ = bf16[832,128]{1,0:T(8,128)(2,1)S(1)} collective-permute-done((bf16[832,128]{1,0:T(8,128)(2,1)S(1)}, bf16[832,128]{1,0:T(8,128)(2,1)S(1)}, u32[]{:S(2)}, u32[]{:S(2)}) %collective-permute-start.7) | collective-permute-done | bytes 213024 | tf_op jit(solution)/shard_map/ppermute | solution.py:696
  28.2 0.6 collective-permute-start.9
  28.9 0.7 collective-permute-done.10.refs_6_
  29.9 0.9 collective-permute-start.14
  30.9 1.1 collective-permute-start.13
  32.0 1.4 collective-permute-start.12
  33.4 4.2 %project.1 = (bf16[2048,1536]{1,0:T(8,128)(2,1)S(1)}, bf16[2048,128]{1,0:T(8,128)(2,1)S(1)}, bf16[2048,128]{1,0:T(8,128)(2,1)S(1)}, f32[48,128]{1,0:T(8,128)S(1)}, bf16[1536,512]{1,0:T(8,128)(2,1)S(1)}) custom-call(s32[1]{0:T(128)} %bitcast.me_ref, s32[1,256]{1,0:T(1,128)S(1)} %bitcast.38, bf16[2048,512]{1,0:T(8,128)(2,1)S(1)} %fetch.1.tokens, ...), custom_call_target="tpu_custom_call" | custom-call | flops 3221225472 | bytes 12000000 | tf_op jit(solution)/shard_map/project/pallas_call | solution.py:170
  37.7 11.3 %attend.2 = (bf16[2048,384]{1,0:T(8,128)(2,1)S(1)}, f32[3,1,2048]{2,1,0:T(1,128)S(1)}) custom-call(bf16[2048,1536]{1,0:T(8,128)(2,1)S(1)} %get-tuple-element.74.qkv, bf16[2048,128]{1,0:T(8,128)(2,1)S(1)} %get-tuple-element.75.query_extra, bf16[2048,128]{1,0:T(8,128)(2,1)S(1)} %get-tuple-element.82.keys_extra), custom_call_target="tpu_custom_call" | custom-call | flops 12884901888 | bytes 6000000 | tf_op jit(solution)/shard_map/attend/pallas_call | solution.py:242
  49.1 0.5 collective-permute-start.17
  49.7 3.9 %attend.3 = (bf16[2048,128]{1,0:T(8,128)(2,1)S(1)}, f32[1,1,2048]{2,1,0:T(1,128)S(1)}) custom-call(bf16[2048,1536]{1,0:T(8,128)(2,1)S(1)} %get-tuple-element.74.qkv, bf16[2048,128]{1,0:T(8,128)(2,1)S(1)} %get-tuple-element.75.query_extra, bf16[2048,128]{1,0:T(8,128)(2,1)S(1)} %get-tuple-element.82.keys_extra), custom_call_target="tpu_custom_call" | custom-call | flops 4294967296 | bytes 6000000 | tf_op jit(solution)/shard_map/attend/pallas_call | solution.py:242
  53.7 25.0 %middle.1 = (bf16[2048,512]{1,0:T(8,128)(2,1)}, bf16[2048,512]{1,0:T(8,128)(2,1)S(1)}, bf16[2048,512]{1,0:T(8,128)(2,1)S(1)}, bf16[2048,128]{1,0:T(8,128)(2,1)S(...) custom-call(s32[1]{0:T(128)} %bitcast.me_ref, ...), custom_call_target="tpu_custom_call" | custom-call | flops 16106127360 | bytes 22000000 | tf_op jit(solution)/shard_map/middle/pallas_call | solution.py:469
  78.6 0.4 collective-permute-start.20
  79.0 11.5 %attend_back.3 = (bf16[2048,128]{1,0:T(8,128)(2,1)S(1)}, bf16[128,2048]{1,0:T(8,128)(2,1)S(1)}, bf16[128,2048]{1,0:T(8,128)(2,1)S(1)}, bf16[768,128]{1,0:T(8,128...) custom-call(s32[1]{0:T(128)} %bitcast.me_ref, bf16[2048,512]{1,0:T(8,128)(2,1)S(1)} %fetch.1.tokens, ...), custom_call_target="tpu_custom_call" | custom-call | flops 10737418240 | bytes 12000000 | tf_op jit(solution)/shard_map/attend_back/pallas_call | solution.py:608
  91.0 1.6 %collective-permute-start.23 = (bf16[1280,128]{1,0:T(8,128)(2,1)S(1)}, bf16[1280,128]{1,0:T(8,128)(2,1)S(1)}, u32[]{:S(2)}, u32[]{:S(2)}) collective-permute-start(bf16[1280,128]{1,0:T(8,128)(2,1)S(1)} %get-tuple-element.132), channel_id=1, source_target_pairs={{0,17},{1,16},{2,19},{3,18},{4,21},{5,20},{6,23},{7,22},{8,25},{9,... | collective-permute-start | bytes 983048 | tf_op jit(solution)/shard_map/ppermute | solution.py:696
  92.5 0.9 collective-permute-start.22
  93.4 1.1 collective-permute-start.21
  94.5 23.0 %attend_back.4 = (bf16[2048,256]{1,0:T(8,128)(2,1)S(1)}, bf16[256,2048]{1,0:T(8,128)(2,1)S(1)}, bf16[256,2048]{1,0:T(8,128)(2,1)S(1)}, bf16[1536,128]{1,0:T(8,12...) custom-call(s32[1]{0:T(128)} %bitcast.me_ref, bf16[2048,512]{1,0:T(8,128)(2,1)S(1)} %fetch.1.tokens, ...), custom_call_target="tpu_custom_call" | custom-call | flops 21474836480 | bytes 24000000 | tf_op jit(solution)/shard_map/attend_back/pallas_call | solution.py:608
  117.9 0.9 collective-permute-start.32
  118.8 12.3 %attend_back.5 = (bf16[2048,128]{1,0:T(8,128)(2,1)S(1)}, bf16[128,2048]{1,0:T(8,128)(2,1)S(1)}, bf16[128,2048]{1,0:T(8,128)(2,1)S(1)}, bf16[1024,128]{1,0:T(8,12...) custom-call(s32[1]{0:T(128)} %bitcast.me_ref, bf16[2048,512]{1,0:T(8,128)(2,1)S(1)} %fetch.1.tokens, ...), custom_call_target="tpu_custom_call" | custom-call | flops 10737418240 | bytes 12000000 | tf_op jit(solution)/shard_map/attend_back/pallas_call | solution.py:608
  131.6 1.1 collective-permute-done.25
  132.7 1.0 collective-permute-start.26
  133.7 1.2 collective-permute-start.27
  135.0 1.5 collective-permute-start.28
  136.4 5.1 %input_grad.1 = f32[2048,512]{1,0:T(8,128)} custom-call(bf16[2048,512]{1,0:T(8,128)(2,1)S(1)} %get-tuple-element.115.refs_0_, bf16[2048,128]{1,0:T(8,128)(2,1)S(1)} %get-tuple-element.98.refs_1_, bf16[2048,256]{1,0:T(8,128)(2,1)S(1)} %get-tuple-element.102.refs_2_, bf16[2048,128]{1,0:T(8,128)(2,1)S(1)} %get-tuple-element.107.refs_3_, ...), custom_call_target="tpu_custom_call" | custom-call | flops 3221225472 | bytes 16000000 | tf_op jit(solution)/shard_map/input_grad/pallas_call | solution.py:650
  141.5 0.9 collective-permute-start.33
  142.4 1.7 %collective-permute-done.27 = bf16[832,128]{1,0:T(8,128)(2,1)S(1)} collective-permute-done((bf16[832,128]{1,0:T(8,128)(2,1)S(1)}, bf16[832,128]{1,0:T(8,128)(2,1)S(1)}, u32[]{:S(2)}, u32[]{:S(2)}) %collective-permute-start.27) | collective-permute-done | bytes 213024 | tf_op jit(solution)/shard_map/ppermute | solution.py:696
  144.1 1.6 %collective-permute-done.28 = bf16[832,128]{1,0:T(8,128)(2,1)S(1)} collective-permute-done((bf16[832,128]{1,0:T(8,128)(2,1)S(1)}, bf16[832,128]{1,0:T(8,128)(2,1)S(1)}, u32[]{:S(2)}, u32[]{:S(2)}) %collective-permute-start.28) | collective-permute-done | bytes 213024 | tf_op jit(solution)/shard_map/ppermute | solution.py:696
  145.8 1.5 collective-permute-start.31
  147.3 1.2 collective-permute-start.30
  148.5 1.8 %collective-permute-start.29 = (bf16[208,128]{1,0:T(8,128)(2,1)S(1)}, bf16[208,128]{1,0:T(8,128)(2,1)S(1)}, u32[]{:S(2)}, u32[]{:S(2)}) collective-permute-start(bf16[208,128]{1,0:T(8,128)(2,1)S(1)} %get-tuple-element.149), channel_id=1, source_target_pairs={{0,2},{1,3},{2,0},{3,1},{4,6},{5,7},{6,4},{7,5},{8,10},{9,11},{10,... | collective-permute-start | bytes 159752 | tf_op jit(solution)/shard_map/ppermute | solution.py:696
  150.3 2.0 %collective-permute-done.31.refs_3_ = bf16[208,128]{1,0:T(8,128)(2,1)S(1)} collective-permute-done((bf16[208,128]{1,0:T(8,128)(2,1)S(1)}, bf16[208,128]{1,0:T(8,128)(2,1)S(1)}, u32[]{:S(2)}, u32[]{:S(2)}) %collective-permute-start.31) | collective-permute-done | bytes 53280 | tf_op jit(solution)/shard_map/ppermute | solution.py:696
  152.3 1.4 collective-permute-done.30.refs_2_
  153.6 0.8 unpack.1
  (62 shorter events, 2.6 us)
Async XLA Ops:
  1.6 9.2 %collective-permute-start.2 = (bf16[208,128]{1,0:T(8,128)(2,1)S(1)}, bf16[208,128]{1,0:T(8,128)(2,1)S(1)}, u32[]{:S(2)}, u32[]{:S(2)}) collective-permute-start(bf16[208,128]{1,0:T(8,128)(2,1)S(1)} %get-tuple-element.67), channel_id=1, source_target_pairs={{0,6},{1,7},{2,4},{3,5},{4,2},{5,3},{6,0},{7,1},{8,14},{9,15},{10,... | collective-permute-start | bytes 159752 | tf_op jit(solution)/shard_map/ppermute | solution.py:696
  6.7 5.0 %collective-permute-start.1 = (bf16[208,128]{1,0:T(8,128)(2,1)S(1)}, bf16[208,128]{1,0:T(8,128)(2,1)S(1)}, u32[]{:S(2)}, u32[]{:S(2)}) collective-permute-start(bf16[208,128]{1,0:T(8,128)(2,1)S(1)} %get-tuple-element.67), channel_id=1, source_target_pairs={{0,4},{1,5},{2,6},{3,7},{4,0},{5,1},{6,2},{7,3},{8,12},{9,13},{10,... | collective-permute-start | bytes 159752 | tf_op jit(solution)/shard_map/ppermute | solution.py:696
  6.7 4.1 %collective-permute-start = (bf16[208,128]{1,0:T(8,128)(2,1)S(1)}, bf16[208,128]{1,0:T(8,128)(2,1)S(1)}, u32[]{:S(2)}, u32[]{:S(2)}) collective-permute-start(bf16[208,128]{1,0:T(8,128)(2,1)S(1)} %get-tuple-element.67), channel_id=1, source_target_pairs={{0,2},{1,3},{2,0},{3,1},{4,6},{5,7},{6,4},{7,5},{8,10},{9,11},{10,... | collective-permute-start | bytes 159752 | tf_op jit(solution)/shard_map/ppermute | solution.py:696
  11.8 1.5 collective-permute-start.4
  13.3 7.2 %collective-permute-start.5 = (bf16[320,128]{1,0:T(8,128)(2,1)S(1)}, bf16[320,128]{1,0:T(8,128)(2,1)S(1)}, u32[]{:S(2)}, u32[]{:S(2)}) collective-permute-start(bf16[320,128]{1,0:T(8,128)(2,1)S(1)} %get-tuple-element.71), channel_id=1, source_target_pairs={{0,4},{1,5},{2,6},{3,7},{4,0},{5,1},{6,2},{7,3},{8,12},{9,13},{10,... | collective-permute-start | bytes 245768 | tf_op jit(solution)/shard_map/ppermute | solution.py:696
  15.4 8.1 %collective-permute-start.8 = (bf16[832,128]{1,0:T(8,128)(2,1)S(1)}, bf16[832,128]{1,0:T(8,128)(2,1)S(1)}, u32[]{:S(2)}, u32[]{:S(2)}) collective-permute-start(bf16[832,128]{1,0:T(8,128)(2,1)S(1)} %constant_dynamic-update-slice_fusion.refs_0_), channel_id=1, source_target_pairs={{0,1},{1,0},{2,3},{3,2},{4,5},{5,4},{6,7},{7,6},{8,9},{9,8},{10,11... | collective-permute-start | bytes 638984 | tf_op jit(solution)/shard_map/ppermute | solution.py:696
  16.9 11.3 %collective-permute-start.7 = (bf16[832,128]{1,0:T(8,128)(2,1)S(1)}, bf16[832,128]{1,0:T(8,128)(2,1)S(1)}, u32[]{:S(2)}, u32[]{:S(2)}) collective-permute-start(bf16[832,128]{1,0:T(8,128)(2,1)S(1)} %constant_dynamic-update-slice_fusion.refs_0_), channel_id=1, source_target_pairs={{0,16},{1,17},{2,18},{3,19},{4,20},{5,21},{6,22},{7,23},{8,24},{9,... | collective-permute-start | bytes 638984 | tf_op jit(solution)/shard_map/ppermute | solution.py:696
  18.4 9.8 %collective-permute-start.3 = (bf16[832,128]{1,0:T(8,128)(2,1)S(1)}, bf16[832,128]{1,0:T(8,128)(2,1)S(1)}, u32[]{:S(2)}, u32[]{:S(2)}) collective-permute-start(bf16[832,128]{1,0:T(8,128)(2,1)S(1)} %constant_dynamic-update-slice_fusion.refs_0_), channel_id=1, source_target_pairs={{0,17},{1,16},{2,19},{3,18},{4,21},{5,20},{6,23},{7,22},{8,25},{9,... | collective-permute-start | bytes 638984 | tf_op jit(solution)/shard_map/ppermute | solution.py:696
  20.5 7.7 %collective-permute-start.6 = (bf16[640,128]{1,0:T(8,128)(2,1)S(1)}, bf16[640,128]{1,0:T(8,128)(2,1)S(1)}, u32[]{:S(2)}, u32[]{:S(2)}) collective-permute-start(bf16[640,128]{1,0:T(8,128)(2,1)S(1)} %pad_maximum_fusion.3), channel_id=1, source_target_pairs={{0,2},{1,3},{2,0},{3,1},{4,6},{5,7},{6,4},{7,5},{8,10},{9,11},{10,... | collective-permute-start | bytes 491528 | tf_op jit(solution)/shard_map/ppermute | solution.py:696
  23.5 6.1 %collective-permute-start.11 = (bf16[832,128]{1,0:T(8,128)(2,1)S(1)}, bf16[832,128]{1,0:T(8,128)(2,1)S(1)}, u32[]{:S(2)}, u32[]{:S(2)}) collective-permute-start(bf16[832,128]{1,0:T(8,128)(2,1)S(1)} %collective-permute-done.8.refs_3_), channel_id=1, source_target_pairs={{0,8},{1,9},{2,10},{3,11},{4,12},{5,13},{6,14},{7,15},{8,0},{9,1},... | collective-permute-start | bytes 638984 | tf_op jit(solution)/shard_map/ppermute | solution.py:696
  28.2 1.5 collective-permute-start.10
  28.2 1.7 %collective-permute-start.9 = (bf16[832,128]{1,0:T(8,128)(2,1)S(1)}, bf16[832,128]{1,0:T(8,128)(2,1)S(1)}, u32[]{:S(2)}, u32[]{:S(2)}) collective-permute-start(bf16[832,128]{1,0:T(8,128)(2,1)S(1)} %collective-permute-done.3.refs_1_), channel_id=1, source_target_pairs={{0,8},{1,9},{2,10},{3,11},{4,12},{5,13},{6,14},{7,15},{8,0},{9,1},... | collective-permute-start | bytes 638984 | tf_op jit(solution)/shard_map/ppermute | solution.py:696
  28.8 24.8 %collective-permute-start.15 = (bf16[1280,128]{1,0:T(8,128)(2,1)S(1)}, bf16[1280,128]{1,0:T(8,128)(2,1)S(1)}, u32[]{:S(2)}, u32[]{:S(2)}) collective-permute-start(bf16[1280,128]{1,0:T(8,128)(2,1)S(1)} %constant_dynamic-update-slice_fusion.4.refs_0_), channel_id=1, source_target_pairs={{0,8},{1,9},{2,10},{3,11},{4,12},{5,13},{6,14},{7,15},{8,0},{9,1},... | collective-permute-start | bytes 983048 | tf_op jit(solution)/shard_map/ppermute | solution.py:696
  29.9 19.0 %collective-permute-start.14 = (bf16[1280,128]{1,0:T(8,128)(2,1)S(1)}, bf16[1280,128]{1,0:T(8,128)(2,1)S(1)}, u32[]{:S(2)}, u32[]{:S(2)}) collective-permute-start(bf16[1280,128]{1,0:T(8,128)(2,1)S(1)} %constant_dynamic-update-slice_fusion.4.refs_0_), channel_id=1, source_target_pairs={{0,1},{1,0},{2,3},{3,2},{4,5},{5,4},{6,7},{7,6},{8,9},{9,8},{10,11... | collective-permute-start | bytes 983048 | tf_op jit(solution)/shard_map/ppermute | solution.py:696
  30.9 18.1 %collective-permute-start.13 = (bf16[1280,128]{1,0:T(8,128)(2,1)S(1)}, bf16[1280,128]{1,0:T(8,128)(2,1)S(1)}, u32[]{:S(2)}, u32[]{:S(2)}) collective-permute-start(bf16[1280,128]{1,0:T(8,128)(2,1)S(1)} %constant_dynamic-update-slice_fusion.4.refs_0_), channel_id=1, source_target_pairs={{0,16},{1,17},{2,18},{3,19},{4,20},{5,21},{6,22},{7,23},{8,24},{9,... | collective-permute-start | bytes 983048 | tf_op jit(solution)/shard_map/ppermute | solution.py:696
  32.0 17.0 %collective-permute-start.12 = (bf16[1280,128]{1,0:T(8,128)(2,1)S(1)}, bf16[1280,128]{1,0:T(8,128)(2,1)S(1)}, u32[]{:S(2)}, u32[]{:S(2)}) collective-permute-start(bf16[1280,128]{1,0:T(8,128)(2,1)S(1)} %constant_dynamic-update-slice_fusion.4.refs_0_), channel_id=1, source_target_pairs={{0,17},{1,16},{2,19},{3,18},{4,21},{5,20},{6,23},{7,22},{8,25},{9,... | collective-permute-start | bytes 983048 | tf_op jit(solution)/shard_map/ppermute | solution.py:696
  49.0 4.7 %copy-start = (bf16[2048,512]{1,0:T(8,128)(2,1)S(1)}, bf16[2048,512]{1,0:T(8,128)(2,1)}, u32[]{:S(2)}) copy-start(bf16[2048,512]{1,0:T(8,128)(2,1)} %cotangent.1) | copy-start | bytes 6291460
  49.0 4.6 %collective-permute-start.16 = (bf16[1280,128]{1,0:T(8,128)(2,1)S(1)}, bf16[1280,128]{1,0:T(8,128)(2,1)S(1)}, u32[]{:S(2)}, u32[]{:S(2)}) collective-permute-start(bf16[1280,128]{1,0:T(8,128)(2,1)S(1)} %collective-permute-done.12.refs_1_), channel_id=1, source_target_pairs={{0,8},{1,9},{2,10},{3,11},{4,12},{5,13},{6,14},{7,15},{8,0},{9,1},... | collective-permute-start | bytes 983048 | tf_op jit(solution)/shard_map/ppermute | solution.py:696
  49.1 4.5 %collective-permute-start.17 = (bf16[1280,128]{1,0:T(8,128)(2,1)S(1)}, bf16[1280,128]{1,0:T(8,128)(2,1)S(1)}, u32[]{:S(2)}, u32[]{:S(2)}) collective-permute-start(bf16[1280,128]{1,0:T(8,128)(2,1)S(1)} %collective-permute-done.13.refs_2_), channel_id=1, source_target_pairs={{0,8},{1,9},{2,10},{3,11},{4,12},{5,13},{6,14},{7,15},{8,0},{9,1},... | collective-permute-start | bytes 983048 | tf_op jit(solution)/shard_map/ppermute | solution.py:696
  49.6 4.1 %collective-permute-start.18 = (bf16[1280,128]{1,0:T(8,128)(2,1)S(1)}, bf16[1280,128]{1,0:T(8,128)(2,1)S(1)}, u32[]{:S(2)}, u32[]{:S(2)}) collective-permute-start(bf16[1280,128]{1,0:T(8,128)(2,1)S(1)} %collective-permute-done.14.refs_3_), channel_id=1, source_target_pairs={{0,8},{1,9},{2,10},{3,11},{4,12},{5,13},{6,14},{7,15},{8,0},{9,1},... | collective-permute-start | bytes 983048 | tf_op jit(solution)/shard_map/ppermute | solution.py:696
  78.6 12.1 %collective-permute-start.20 = (bf16[5120,128]{1,0:T(8,128)(2,1)S(1)}, bf16[5120,128]{1,0:T(8,128)(2,1)S(1)}, u32[]{:S(2)}, u32[]{:S(2)}) collective-permute-start(bf16[5120,128]{1,0:T(8,128)(2,1)S(1)} %get-tuple-element.97), channel_id=1, source_target_pairs={{0,8},{1,9},{2,10},{3,11},{4,12},{5,13},{6,14},{7,15},{8,0},{9,1},... | collective-permute-start | bytes 3932168 | tf_op jit(solution)/shard_map/ppermute | solution.py:696
  90.6 40.5 %collective-permute-start.19 = (bf16[768,128]{1,0:T(8,128)(2,1)S(1)}, bf16[768,128]{1,0:T(8,128)(2,1)S(1)}, u32[]{:S(2)}, u32[]{:S(2)}) collective-permute-start(bf16[768,128]{1,0:T(8,128)(2,1)S(1)} %get-tuple-element.94), channel_id=1, source_target_pairs={{0,8},{1,9},{2,10},{3,11},{4,12},{5,13},{6,14},{7,15},{8,0},{9,1},... | collective-permute-start | bytes 589832 | tf_op jit(solution)/shard_map/ppermute | solution.py:696
  91.0 26.6 %collective-permute-start.23 = (bf16[1280,128]{1,0:T(8,128)(2,1)S(1)}, bf16[1280,128]{1,0:T(8,128)(2,1)S(1)}, u32[]{:S(2)}, u32[]{:S(2)}) collective-permute-start(bf16[1280,128]{1,0:T(8,128)(2,1)S(1)} %get-tuple-element.132), channel_id=1, source_target_pairs={{0,17},{1,16},{2,19},{3,18},{4,21},{5,20},{6,23},{7,22},{8,25},{9,... | collective-permute-start | bytes 983048 | tf_op jit(solution)/shard_map/ppermute | solution.py:696
  92.5 25.1 %collective-permute-start.22 = (bf16[1280,128]{1,0:T(8,128)(2,1)S(1)}, bf16[1280,128]{1,0:T(8,128)(2,1)S(1)}, u32[]{:S(2)}, u32[]{:S(2)}) collective-permute-start(bf16[1280,128]{1,0:T(8,128)(2,1)S(1)} %get-tuple-element.133), channel_id=1, source_target_pairs={{0,16},{1,17},{2,18},{3,19},{4,20},{5,21},{6,22},{7,23},{8,24},{9,... | collective-permute-start | bytes 983048 | tf_op jit(solution)/shard_map/ppermute | solution.py:696
  93.4 24.2 %collective-permute-start.21 = (bf16[1280,128]{1,0:T(8,128)(2,1)S(1)}, bf16[1280,128]{1,0:T(8,128)(2,1)S(1)}, u32[]{:S(2)}, u32[]{:S(2)}) collective-permute-start(bf16[1280,128]{1,0:T(8,128)(2,1)S(1)} %get-tuple-element.134), channel_id=1, source_target_pairs={{0,1},{1,0},{2,3},{3,2},{4,5},{5,4},{6,7},{7,6},{8,9},{9,8},{10,11... | collective-permute-start | bytes 983048 | tf_op jit(solution)/shard_map/ppermute | solution.py:696
  117.5 13.8 %collective-permute-start.24 = (bf16[1536,128]{1,0:T(8,128)(2,1)S(1)}, bf16[1536,128]{1,0:T(8,128)(2,1)S(1)}, u32[]{:S(2)}, u32[]{:S(2)}) collective-permute-start(bf16[1536,128]{1,0:T(8,128)(2,1)S(1)} %get-tuple-element.110), channel_id=1, source_target_pairs={{0,8},{1,9},{2,10},{3,11},{4,12},{5,13},{6,14},{7,15},{8,0},{9,1},... | collective-permute-start | bytes 1179656 | tf_op jit(solution)/shard_map/ppermute | solution.py:696
  117.9 13.6 %collective-permute-start.32 = (bf16[640,128]{1,0:T(8,128)(2,1)S(1)}, bf16[640,128]{1,0:T(8,128)(2,1)S(1)}, u32[]{:S(2)}, u32[]{:S(2)}) collective-permute-start(bf16[640,128]{1,0:T(8,128)(2,1)S(1)} %slice.258), channel_id=1, source_target_pairs={{0,2},{1,3},{2,0},{3,1},{4,6},{5,7},{6,4},{7,5},{8,10},{9,11},{10,... | collective-permute-start | bytes 491528 | tf_op jit(solution)/shard_map/ppermute | solution.py:696
  131.1 1.5 collective-permute-start.25
  132.7 9.7 %collective-permute-start.26 = (bf16[832,128]{1,0:T(8,128)(2,1)S(1)}, bf16[832,128]{1,0:T(8,128)(2,1)S(1)}, u32[]{:S(2)}, u32[]{:S(2)}) collective-permute-start(bf16[832,128]{1,0:T(8,128)(2,1)S(1)} %bitcast.50), channel_id=1, source_target_pairs={{0,1},{1,0},{2,3},{3,2},{4,5},{5,4},{6,7},{7,6},{8,9},{9,8},{10,11... | collective-permute-start | bytes 638984 | tf_op jit(solution)/shard_map/ppermute | solution.py:696
  133.7 10.4 %collective-permute-start.27 = (bf16[832,128]{1,0:T(8,128)(2,1)S(1)}, bf16[832,128]{1,0:T(8,128)(2,1)S(1)}, u32[]{:S(2)}, u32[]{:S(2)}) collective-permute-start(bf16[832,128]{1,0:T(8,128)(2,1)S(1)} %bitcast.52), channel_id=1, source_target_pairs={{0,16},{1,17},{2,18},{3,19},{4,20},{5,21},{6,22},{7,23},{8,24},{9,... | collective-permute-start | bytes 638984 | tf_op jit(solution)/shard_map/ppermute | solution.py:696
  135.0 10.7 %collective-permute-start.28 = (bf16[832,128]{1,0:T(8,128)(2,1)S(1)}, bf16[832,128]{1,0:T(8,128)(2,1)S(1)}, u32[]{:S(2)}, u32[]{:S(2)}) collective-permute-start(bf16[832,128]{1,0:T(8,128)(2,1)S(1)} %bitcast.53), channel_id=1, source_target_pairs={{0,17},{1,16},{2,19},{3,18},{4,21},{5,20},{6,23},{7,22},{8,25},{9,... | collective-permute-start | bytes 638984 | tf_op jit(solution)/shard_map/ppermute | solution.py:696
  141.5 8.7 %collective-permute-start.33 = (bf16[320,128]{1,0:T(8,128)(2,1)S(1)}, bf16[320,128]{1,0:T(8,128)(2,1)S(1)}, u32[]{:S(2)}, u32[]{:S(2)}) collective-permute-start(bf16[320,128]{1,0:T(8,128)(2,1)S(1)} %slice.259), channel_id=1, source_target_pairs={{0,4},{1,5},{2,6},{3,7},{4,0},{5,1},{6,2},{7,3},{8,12},{9,13},{10,... | collective-permute-start | bytes 245768 | tf_op jit(solution)/shard_map/ppermute | solution.py:696
  145.8 6.5 %collective-permute-start.31 = (bf16[208,128]{1,0:T(8,128)(2,1)S(1)}, bf16[208,128]{1,0:T(8,128)(2,1)S(1)}, u32[]{:S(2)}, u32[]{:S(2)}) collective-permute-start(bf16[208,128]{1,0:T(8,128)(2,1)S(1)} %get-tuple-element.147), channel_id=1, source_target_pairs={{0,6},{1,7},{2,4},{3,5},{4,2},{5,3},{6,0},{7,1},{8,14},{9,15},{10,... | collective-permute-start | bytes 159752 | tf_op jit(solution)/shard_map/ppermute | solution.py:696
  147.3 6.3 %collective-permute-start.30 = (bf16[208,128]{1,0:T(8,128)(2,1)S(1)}, bf16[208,128]{1,0:T(8,128)(2,1)S(1)}, u32[]{:S(2)}, u32[]{:S(2)}) collective-permute-start(bf16[208,128]{1,0:T(8,128)(2,1)S(1)} %get-tuple-element.148), channel_id=1, source_target_pairs={{0,4},{1,5},{2,6},{3,7},{4,0},{5,1},{6,2},{7,3},{8,12},{9,13},{10,... | collective-permute-start | bytes 159752 | tf_op jit(solution)/shard_map/ppermute | solution.py:696
  148.5 5.1 %collective-permute-start.29 = (bf16[208,128]{1,0:T(8,128)(2,1)S(1)}, bf16[208,128]{1,0:T(8,128)(2,1)S(1)}, u32[]{:S(2)}, u32[]{:S(2)}) collective-permute-start(bf16[208,128]{1,0:T(8,128)(2,1)S(1)} %get-tuple-element.149), channel_id=1, source_target_pairs={{0,2},{1,3},{2,0},{3,1},{4,6},{5,7},{6,4},{7,5},{8,10},{9,11},{10,... | collective-permute-start | bytes 159752 | tf_op jit(solution)/shard_map/ppermute | solution.py:696

commit v5 on v4

--- a/solution.py
+++ b/solution.py
@@ -99,28 +99,48 @@
     )(me, flat, vec)
 
 
-def fetch_kernel(source, out, sem):
+def fetch_kernel(source, ends, out, keys_extra, apart_out, sem):
     copy = pltpu.make_async_copy(source, out, sem)
     copy.start()
+    count = out.shape[0]
+    rows = 512
+
+    def part(i, _):
+        here = pl.ds(pl.multiple_of(i * rows, rows), rows)
+        places = i * rows + lax.broadcasted_iota(jnp.int32, (rows, ends.shape[1]), 0)
+        label = jnp.sum((ends[...] <= places).astype(f32), axis=1, keepdims=True)
+        lane = lax.broadcasted_iota(jnp.int32, (rows, 128), 1)
+        same = lane.astype(f32) == label
+        ones = jnp.where(lane < 8, jnp.where(same, 1.0, 0.0), jnp.where(lane < 32, 1.0, 0.0))
+        keys_extra[here, :] = ones.astype(bf16)
+        apart_out[here, :] = jnp.where((lane < 8) & jnp.logical_not(same), FAR, 0.0).astype(bf16)
+        return 0
+
+    lax.fori_loop(0, count // rows, part, 0)
     copy.wait()
 
 
-def fetch(array):
+def fetch(array, ends):
+    count = array.shape[0]
     return pl.pallas_call(
         fetch_kernel,
-        in_specs=[pl.BlockSpec(memory_space=pl.ANY)],
-        out_specs=resident(),
-        out_shape=jax.ShapeDtypeStruct(array.shape, array.dtype),
+        in_specs=[pl.BlockSpec(memory_space=pl.ANY), resident()],
+        out_specs=[resident() for _ in range(3)],
+        out_shape=[
+            jax.ShapeDtypeStruct(array.shape, array.dtype),
+            jax.ShapeDtypeStruct((count, 128), bf16),
+            jax.ShapeDtypeStruct((count, 128), bf16),
+        ],
         scratch_shapes=[pltpu.SemaphoreType.DMA],
         compiler_params=params("fetch"),
-        cost_estimate=cost(0, 2 * array.size * 2),
+        cost_estimate=cost(0, 6e6),
         name="fetch",
-    )(array)
-
-
-def project_kernel(rows, masks, order, vec_width, me_ref, ends, tokens, *refs):
+    )(array, ends)
+
+
+def project_kernel(rows, masks, order, vec_width, me_ref, apart, tokens, *refs):
     pieces = refs[: len(masks)]
-    qkv, keys_extra, query_extra, vec_out, weight, vec = refs[len(masks) :]
+    qkv, query_extra, vec_out, weight, vec = refs[len(masks) :]
     step = pl.program_id(0)
     me = me_ref[0]
 
@@ -150,36 +170,29 @@
     qkv[here, 0:512] = queries
     qkv[here, 512:1024] = key_heads
     qkv[here, 1024:1536] = values
-    places = step * rows + lax.broadcasted_iota(jnp.int32, (rows, ends.shape[1]), 0)
-    label = jnp.sum((ends[...] <= places).astype(f32), axis=1, keepdims=True)
     lane = lax.broadcasted_iota(jnp.int32, (rows, 128), 1)
-    same = lane.astype(f32) == label
-    keys_extra[here, :] = jnp.where(lane < 8, jnp.where(same, 1.0, 0.0), jnp.where(lane < 32, 1.0, 0.0)).astype(bf16)
-    apart = jnp.where((lane < 8) & jnp.logical_not(same), FAR, 0.0)
     product = queries.astype(f32) * key_heads.astype(f32)
-    extra = apart
+    extra = apart[here, :].astype(f32)
     for h in range(HEADS):
         own = jnp.sum(product[:, 128 * h : 128 * (h + 1)], axis=1, keepdims=True)
         extra = jnp.where(lane == 8 + h, -own, extra)
     query_extra[here, :] = extra.astype(bf16)
 
 
-def project(me, ends, tokens, pieces, masks, order, vec_width, rows=1024):
+def project(me, apart, tokens, pieces, masks, order, vec_width, rows=1024):
     count = tokens.shape[0]
-    sets = ends.shape[1]
     return pl.pallas_call(
         functools.partial(project_kernel, rows, masks, order, vec_width),
         grid=(count // rows,),
         in_specs=[
             scalar_spec(),
-            whole((1, sets)),
+            resident(),
             resident(),
         ]
         + [resident() for _ in pieces],
-        out_specs=[resident() for _ in range(5)],
+        out_specs=[resident() for _ in range(4)],
         out_shape=[
             jax.ShapeDtypeStruct((count, 1536), bf16),
-            jax.ShapeDtypeStruct((count, 128), bf16),
             jax.ShapeDtypeStruct((count, 128), bf16),
             jax.ShapeDtypeStruct((48, 128), f32),
             jax.ShapeDtypeStruct((1536, 512), bf16),
@@ -188,7 +201,7 @@
         compiler_params=params("project"),
         cost_estimate=cost(2 * count * 512 * 1536, 12e6),
         name="project",
-    )(me, ends, tokens, *pieces)
+    )(me, apart, tokens, *pieces)
 
 
 def own_lanes(lane, head):
@@ -763,7 +776,7 @@
         q_pieces = [q_far] + [swap(q_far, step, count) for step in spread]
         r_far = gather_line(after(r_block, q_core), [z_far], count)
         r_far = gather_line(r_far, [z_near], count)
-        tokens = fetch(after(pltpu.with_memory_space_constraint(tokens, pltpu.HBM), q_far))
+        tokens, keys_extra, apart = fetch(after(pltpu.with_memory_space_constraint(tokens, pltpu.HBM), q_far), ends)
         q_pieces[3] = after(q_pieces[3], tokens)
         q_pieces[1] = after(q_pieces[1], r_far)
         q_pieces = q_pieces + [q_core] + [swap(piece, core, count) for piece in q_pieces[1:]]
@@ -771,6 +784,7 @@
     else:
         vec_width = 160
         order_in, order_rest, order_out = [1, 2], [1, 2], [1, 2, 4, 8, 16]
+        tokens, keys_extra, apart = fetch(tokens, ends)
         order_rest_out = order_out
         masks = [4 * i for i in range(8)]
         me = jnp.zeros((1,), jnp.int32)
@@ -794,8 +808,8 @@
         r_all = jnp.concatenate(panels[1:], axis=1)
         q_pieces = [q_all[4 * i : 4 * i + 4].reshape(-1, 128) for i in range(8)]
         r_pieces = [r_all[4 * i : 4 * i + 4].reshape(-1, 128) for i in range(8)]
-    qkv, keys_extra, query_extra, vec, weight = project(
-        me, ends, tokens, q_pieces, masks, order_in, vec_width
+    qkv, query_extra, vec, weight = project(
+        me, apart, tokens, q_pieces, masks, order_in, vec_width
     )
     attended_a, offset_a = attend(qkv, query_extra, keys_extra, 0, 3)
     if fast:

time: 155 us -> 155 us (level)
  no operation moved by 1% of the time
where the time goes in v5:
time: 155 us; the launch traced here: 154 us
  Pallas kernels  99.6 us (64%)
  starting transfers between devices  31.4 us (20%)
  waiting for transfers between devices  19.3 us (12%)
  other arithmetic  2.66 us (2%)
    pallas_call x3, Pallas kernels, attend_back(): pl.pallas_call(functools.partial(attend_back_kernel, base, heads, width,...  46.8 us
    ppermute x34, starting transfers between devices, swap(): return lax.ppermute(array, AXES, [(i, i ^ step) for i in range(count)])  31.4 us
    pallas_call x1, Pallas kernels, middle(): pl.pallas_call(functools.partial(middle_kernel, masks, order_in, order_ou...  25 us
    ppermute x34, waiting for transfers between devices, swap(): return lax.ppermute(array, AXES, [(i, i ^ step) for i in range(count)])  19.3 us
    pallas_call x2, Pallas kernels, attend(): pl.pallas_call(functools.partial(attend_kernel, base, rows), grid=(heads,...  15.2 us
    pallas_call x1, Pallas kernels, input_grad(): pl.pallas_call(functools.partial(input_grad_kernel, len(queries), rows),...  5.07 us
    pallas_call x1, Pallas kernels, project(): pl.pallas_call(functools.partial(project_kernel, rows, masks, order, vec_...  4.21 us
  transfers between devices with their start and end apart: 34, of which 12 were waited for; matrix products, arithmetic and copies ran while one was open for 2% of the time, Pallas kernels for 47%

profile of v5, /device:TPU:0, one launch (start us, length us, event | category | flops | bytes accessed | tf_op | source)
XLA Modules:
  0.0 154.4 jit_solution(15454012291320619013)
XLA Ops:
  0.6 1.0 pack.1
  1.6 5.1 %collective-permute-start.2 = (bf16[208,128]{1,0:T(8,128)(2,1)S(1)}, bf16[208,128]{1,0:T(8,128)(2,1)S(1)}, u32[]{:S(2)}, u32[]{:S(2)}) collective-permute-start(bf16[208,128]{1,0:T(8,128)(2,1)S(1)} %get-tuple-element.69), channel_id=1, source_target_pairs={{0,6},{1,7},{2,4},{3,5},{4,2},{5,3},{6,0},{7,1},{8,14},{9,15},{10,... | collective-permute-start | bytes 159752 | tf_op jit(solution)/shard_map/ppermute | solution.py:709
  6.7 0.6 collective-permute-start
  7.3 0.7 select_bitcast_fusion
  8.6 0.8 bitcast_select_fusion
  9.3 1.5 collective-permute-done
  10.9 0.9 collective-permute-done.1
  11.8 1.5 collective-permute-done.4.refs_4_
  13.3 2.1 %collective-permute-start.5 = (bf16[320,128]{1,0:T(8,128)(2,1)S(1)}, bf16[320,128]{1,0:T(8,128)(2,1)S(1)}, u32[]{:S(2)}, u32[]{:S(2)}) collective-permute-start(bf16[320,128]{1,0:T(8,128)(2,1)S(1)} %get-tuple-element.75), channel_id=1, source_target_pairs={{0,4},{1,5},{2,6},{3,7},{4,0},{5,1},{6,2},{7,3},{8,12},{9,13},{10,... | collective-permute-start | bytes 245768 | tf_op jit(solution)/shard_map/ppermute | solution.py:709
  15.4 1.5 collective-permute-start.8
  16.9 1.5 collective-permute-start.7
  18.4 0.5 collective-permute-start.3
  18.9 1.6 %fetch.1 = (bf16[2048,512]{1,0:T(8,128)(2,1)S(1)}, bf16[2048,128]{1,0:T(8,128)(2,1)S(1)}, bf16[2048,128]{1,0:T(8,128)(2,1)S(1)}) custom-call(bf16[2048,512]{1,0:T(8,128)(2,1)} %source, s32[1,256]{1,0:T(1,128)S(1)} %bitcast.38), custom_call_target="tpu_custom_call" | custom-call | bytes 6000000 | tf_op jit(solution)/shard_map/fetch/pallas_call | solution.py:125
  20.5 0.9 collective-permute-start.6
  21.4 2.1 %collective-permute-done.8.refs_3_ = bf16[832,128]{1,0:T(8,128)(2,1)S(1)} collective-permute-done((bf16[832,128]{1,0:T(8,128)(2,1)S(1)}, bf16[832,128]{1,0:T(8,128)(2,1)S(1)}, u32[]{:S(2)}, u32[]{:S(2)}) %collective-permute-start.8) | collective-permute-done | bytes 213024 | tf_op jit(solution)/shard_map/ppermute | solution.py:709
  23.5 4.7 %collective-permute-done.7.refs_2_ = bf16[832,128]{1,0:T(8,128)(2,1)S(1)} collective-permute-done((bf16[832,128]{1,0:T(8,128)(2,1)S(1)}, bf16[832,128]{1,0:T(8,128)(2,1)S(1)}, u32[]{:S(2)}, u32[]{:S(2)}) %collective-permute-start.7) | collective-permute-done | bytes 213024 | tf_op jit(solution)/shard_map/ppermute | solution.py:709
  28.2 0.6 collective-permute-start.9
  28.9 0.7 collective-permute-done.10.refs_6_
  29.9 0.9 collective-permute-start.14
  30.9 1.1 collective-permute-start.13
  32.0 1.4 collective-permute-start.12
  33.4 4.2 %project.1 = (bf16[2048,1536]{1,0:T(8,128)(2,1)S(1)}, bf16[2048,128]{1,0:T(8,128)(2,1)S(1)}, f32[48,128]{1,0:T(8,128)S(1)}, bf16[1536,512]{1,0:T(8,128)(2,1)S(1)}) custom-call(s32[1]{0:T(128)} %bitcast.me_ref, bf16[2048,128]{1,0:T(8,128)(2,1)S(1)} %get-tuple-element.73.apart, bf16[2048,512]{1,0:T(8,128)(2,1)S(1)} %get-tuple-element.72.tokens, ...), custom_call_target="tpu_custom_call" | custom-call | flops 3221225472 | bytes 12000000 | tf_op jit(solution)/shard_map/project/pallas_call | solution.py:184
  37.6 11.3 %attend.2 = (bf16[2048,384]{1,0:T(8,128)(2,1)S(1)}, f32[3,1,2048]{2,1,0:T(1,128)S(1)}) custom-call(bf16[2048,1536]{1,0:T(8,128)(2,1)S(1)} %get-tuple-element.78.qkv, bf16[2048,128]{1,0:T(8,128)(2,1)S(1)} %get-tuple-element.79.query_extra, bf16[2048,128]{1,0:T(8,128)(2,1)S(1)} %get-tuple-element.86.keys_extra), custom_call_target="tpu_custom_call" | custom-call | flops 12884901888 | bytes 6000000 | tf_op jit(solution)/shard_map/attend/pallas_call | solution.py:255
  49.1 0.5 collective-permute-start.17
  49.6 3.9 %attend.3 = (bf16[2048,128]{1,0:T(8,128)(2,1)S(1)}, f32[1,1,2048]{2,1,0:T(1,128)S(1)}) custom-call(bf16[2048,1536]{1,0:T(8,128)(2,1)S(1)} %get-tuple-element.78.qkv, bf16[2048,128]{1,0:T(8,128)(2,1)S(1)} %get-tuple-element.79.query_extra, bf16[2048,128]{1,0:T(8,128)(2,1)S(1)} %get-tuple-element.86.keys_extra), custom_call_target="tpu_custom_call" | custom-call | flops 4294967296 | bytes 6000000 | tf_op jit(solution)/shard_map/attend/pallas_call | solution.py:255
  53.6 25.0 %middle.1 = (bf16[2048,512]{1,0:T(8,128)(2,1)}, bf16[2048,512]{1,0:T(8,128)(2,1)S(1)}, bf16[2048,512]{1,0:T(8,128)(2,1)S(1)}, bf16[2048,128]{1,0:T(8,128)(2,1)S(...) custom-call(s32[1]{0:T(128)} %bitcast.me_ref, ...), custom_call_target="tpu_custom_call" | custom-call | flops 16106127360 | bytes 22000000 | tf_op jit(solution)/shard_map/middle/pallas_call | solution.py:482
  78.6 0.4 collective-permute-start.20
  79.0 11.5 %attend_back.3 = (bf16[2048,128]{1,0:T(8,128)(2,1)S(1)}, bf16[128,2048]{1,0:T(8,128)(2,1)S(1)}, bf16[128,2048]{1,0:T(8,128)(2,1)S(1)}, bf16[768,128]{1,0:T(8,128...) custom-call(s32[1]{0:T(128)} %bitcast.me_ref, bf16[2048,512]{1,0:T(8,128)(2,1)S(1)} %get-tuple-element.72.tokens, ...), custom_call_target="tpu_custom_call" | custom-call | flops 10737418240 | bytes 12000000 | tf_op jit(solution)/shard_map/attend_back/pallas_call | solution.py:621
  91.0 1.6 %collective-permute-start.23 = (bf16[1280,128]{1,0:T(8,128)(2,1)S(1)}, bf16[1280,128]{1,0:T(8,128)(2,1)S(1)}, u32[]{:S(2)}, u32[]{:S(2)}) collective-permute-start(bf16[1280,128]{1,0:T(8,128)(2,1)S(1)} %get-tuple-element.136), channel_id=1, source_target_pairs={{0,17},{1,16},{2,19},{3,18},{4,21},{5,20},{6,23},{7,22},{8,25},{9,... | collective-permute-start | bytes 983048 | tf_op jit(solution)/shard_map/ppermute | solution.py:709
  92.5 0.9 collective-permute-start.22
  93.4 1.1 collective-permute-start.21
  94.5 23.0 %attend_back.4 = (bf16[2048,256]{1,0:T(8,128)(2,1)S(1)}, bf16[256,2048]{1,0:T(8,128)(2,1)S(1)}, bf16[256,2048]{1,0:T(8,128)(2,1)S(1)}, bf16[1536,128]{1,0:T(8,12...) custom-call(s32[1]{0:T(128)} %bitcast.me_ref, bf16[2048,512]{1,0:T(8,128)(2,1)S(1)} %get-tuple-element.72.tokens, ...), custom_call_target="tpu_custom_call" | custom-call | flops 21474836480 | bytes 24000000 | tf_op jit(solution)/shard_map/attend_back/pallas_call | solution.py:621
  117.9 0.9 collective-permute-start.32
  118.8 12.3 %attend_back.5 = (bf16[2048,128]{1,0:T(8,128)(2,1)S(1)}, bf16[128,2048]{1,0:T(8,128)(2,1)S(1)}, bf16[128,2048]{1,0:T(8,128)(2,1)S(1)}, bf16[1024,128]{1,0:T(8,12...) custom-call(s32[1]{0:T(128)} %bitcast.me_ref, bf16[2048,512]{1,0:T(8,128)(2,1)S(1)} %get-tuple-element.72.tokens, ...), custom_call_target="tpu_custom_call" | custom-call | flops 10737418240 | bytes 12000000 | tf_op jit(solution)/shard_map/attend_back/pallas_call | solution.py:621
  131.6 1.1 collective-permute-done.25
  132.8 1.0 collective-permute-start.26
  133.8 1.2 collective-permute-start.27
  134.9 1.5 collective-permute-start.28
  136.5 5.1 %input_grad.1 = f32[2048,512]{1,0:T(8,128)} custom-call(bf16[2048,512]{1,0:T(8,128)(2,1)S(1)} %get-tuple-element.119.refs_0_, bf16[2048,128]{1,0:T(8,128)(2,1)S(1)} %get-tuple-element.102.refs_1_, bf16[2048,256]{1,0:T(8,128)(2,1)S(1)} %get-tuple-element.106.refs_2_, bf16[2048,128]{1,0:T(8,128)(2,1)S(1)} %get-tuple-element.111.refs_3_, ...), custom_call_target="tpu_custom_call" | custom-call | flops 3221225472 | bytes 16000000 | tf_op jit(solution)/shard_map/input_grad/pallas_call | solution.py:663
  141.5 0.9 collective-permute-start.33
  142.4 1.7 %collective-permute-done.27 = bf16[832,128]{1,0:T(8,128)(2,1)S(1)} collective-permute-done((bf16[832,128]{1,0:T(8,128)(2,1)S(1)}, bf16[832,128]{1,0:T(8,128)(2,1)S(1)}, u32[]{:S(2)}, u32[]{:S(2)}) %collective-permute-start.27) | collective-permute-done | bytes 213024 | tf_op jit(solution)/shard_map/ppermute | solution.py:709
  144.1 1.6 %collective-permute-done.28 = bf16[832,128]{1,0:T(8,128)(2,1)S(1)} collective-permute-done((bf16[832,128]{1,0:T(8,128)(2,1)S(1)}, bf16[832,128]{1,0:T(8,128)(2,1)S(1)}, u32[]{:S(2)}, u32[]{:S(2)}) %collective-permute-start.28) | collective-permute-done | bytes 213024 | tf_op jit(solution)/shard_map/ppermute | solution.py:709
  145.8 1.5 collective-permute-start.31
  147.3 1.2 collective-permute-start.30
  148.5 1.8 %collective-permute-start.29 = (bf16[208,128]{1,0:T(8,128)(2,1)S(1)}, bf16[208,128]{1,0:T(8,128)(2,1)S(1)}, u32[]{:S(2)}, u32[]{:S(2)}) collective-permute-start(bf16[208,128]{1,0:T(8,128)(2,1)S(1)} %get-tuple-element.153), channel_id=1, source_target_pairs={{0,2},{1,3},{2,0},{3,1},{4,6},{5,7},{6,4},{7,5},{8,10},{9,11},{10,... | collective-permute-start | bytes 159752 | tf_op jit(solution)/shard_map/ppermute | solution.py:709
  150.3 1.9 %collective-permute-done.31.refs_3_ = bf16[208,128]{1,0:T(8,128)(2,1)S(1)} collective-permute-done((bf16[208,128]{1,0:T(8,128)(2,1)S(1)}, bf16[208,128]{1,0:T(8,128)(2,1)S(1)}, u32[]{:S(2)}, u32[]{:S(2)}) %collective-permute-start.31) | collective-permute-done | bytes 53280 | tf_op jit(solution)/shard_map/ppermute | solution.py:709
  152.2 1.4 collective-permute-done.30.refs_2_
  153.7 0.8 unpack.1
  (62 shorter events, 2.6 us)
Async XLA Ops:
  1.6 9.2 %collective-permute-start.2 = (bf16[208,128]{1,0:T(8,128)(2,1)S(1)}, bf16[208,128]{1,0:T(8,128)(2,1)S(1)}, u32[]{:S(2)}, u32[]{:S(2)}) collective-permute-start(bf16[208,128]{1,0:T(8,128)(2,1)S(1)} %get-tuple-element.69), channel_id=1, source_target_pairs={{0,6},{1,7},{2,4},{3,5},{4,2},{5,3},{6,0},{7,1},{8,14},{9,15},{10,... | collective-permute-start | bytes 159752 | tf_op jit(solution)/shard_map/ppermute | solution.py:709
  6.7 5.0 %collective-permute-start.1 = (bf16[208,128]{1,0:T(8,128)(2,1)S(1)}, bf16[208,128]{1,0:T(8,128)(2,1)S(1)}, u32[]{:S(2)}, u32[]{:S(2)}) collective-permute-start(bf16[208,128]{1,0:T(8,128)(2,1)S(1)} %get-tuple-element.69), channel_id=1, source_target_pairs={{0,4},{1,5},{2,6},{3,7},{4,0},{5,1},{6,2},{7,3},{8,12},{9,13},{10,... | collective-permute-start | bytes 159752 | tf_op jit(solution)/shard_map/ppermute | solution.py:709
  6.7 4.1 %collective-permute-start = (bf16[208,128]{1,0:T(8,128)(2,1)S(1)}, bf16[208,128]{1,0:T(8,128)(2,1)S(1)}, u32[]{:S(2)}, u32[]{:S(2)}) collective-permute-start(bf16[208,128]{1,0:T(8,128)(2,1)S(1)} %get-tuple-element.69), channel_id=1, source_target_pairs={{0,2},{1,3},{2,0},{3,1},{4,6},{5,7},{6,4},{7,5},{8,10},{9,11},{10,... | collective-permute-start | bytes 159752 | tf_op jit(solution)/shard_map/ppermute | solution.py:709
  11.8 1.5 collective-permute-start.4
  13.3 7.2 %collective-permute-start.5 = (bf16[320,128]{1,0:T(8,128)(2,1)S(1)}, bf16[320,128]{1,0:T(8,128)(2,1)S(1)}, u32[]{:S(2)}, u32[]{:S(2)}) collective-permute-start(bf16[320,128]{1,0:T(8,128)(2,1)S(1)} %get-tuple-element.75), channel_id=1, source_target_pairs={{0,4},{1,5},{2,6},{3,7},{4,0},{5,1},{6,2},{7,3},{8,12},{9,13},{10,... | collective-permute-start | bytes 245768 | tf_op jit(solution)/shard_map/ppermute | solution.py:709
  15.4 8.1 %collective-permute-start.8 = (bf16[832,128]{1,0:T(8,128)(2,1)S(1)}, bf16[832,128]{1,0:T(8,128)(2,1)S(1)}, u32[]{:S(2)}, u32[]{:S(2)}) collective-permute-start(bf16[832,128]{1,0:T(8,128)(2,1)S(1)} %constant_dynamic-update-slice_fusion.refs_0_), channel_id=1, source_target_pairs={{0,1},{1,0},{2,3},{3,2},{4,5},{5,4},{6,7},{7,6},{8,9},{9,8},{10,11... | collective-permute-start | bytes 638984 | tf_op jit(solution)/shard_map/ppermute | solution.py:709
  16.9 11.3 %collective-permute-start.7 = (bf16[832,128]{1,0:T(8,128)(2,1)S(1)}, bf16[832,128]{1,0:T(8,128)(2,1)S(1)}, u32[]{:S(2)}, u32[]{:S(2)}) collective-permute-start(bf16[832,128]{1,0:T(8,128)(2,1)S(1)} %constant_dynamic-update-slice_fusion.refs_0_), channel_id=1, source_target_pairs={{0,16},{1,17},{2,18},{3,19},{4,20},{5,21},{6,22},{7,23},{8,24},{9,... | collective-permute-start | bytes 638984 | tf_op jit(solution)/shard_map/ppermute | solution.py:709
  18.4 9.8 %collective-permute-start.3 = (bf16[832,128]{1,0:T(8,128)(2,1)S(1)}, bf16[832,128]{1,0:T(8,128)(2,1)S(1)}, u32[]{:S(2)}, u32[]{:S(2)}) collective-permute-start(bf16[832,128]{1,0:T(8,128)(2,1)S(1)} %constant_dynamic-update-slice_fusion.refs_0_), channel_id=1, source_target_pairs={{0,17},{1,16},{2,19},{3,18},{4,21},{5,20},{6,23},{7,22},{8,25},{9,... | collective-permute-start | bytes 638984 | tf_op jit(solution)/shard_map/ppermute | solution.py:709
  20.5 7.7 %collective-permute-start.6 = (bf16[640,128]{1,0:T(8,128)(2,1)S(1)}, bf16[640,128]{1,0:T(8,128)(2,1)S(1)}, u32[]{:S(2)}, u32[]{:S(2)}) collective-permute-start(bf16[640,128]{1,0:T(8,128)(2,1)S(1)} %pad_maximum_fusion.3), channel_id=1, source_target_pairs={{0,2},{1,3},{2,0},{3,1},{4,6},{5,7},{6,4},{7,5},{8,10},{9,11},{10,... | collective-permute-start | bytes 491528 | tf_op jit(solution)/shard_map/ppermute | solution.py:709
  23.5 6.1 %collective-permute-start.11 = (bf16[832,128]{1,0:T(8,128)(2,1)S(1)}, bf16[832,128]{1,0:T(8,128)(2,1)S(1)}, u32[]{:S(2)}, u32[]{:S(2)}) collective-permute-start(bf16[832,128]{1,0:T(8,128)(2,1)S(1)} %collective-permute-done.8.refs_3_), channel_id=1, source_target_pairs={{0,8},{1,9},{2,10},{3,11},{4,12},{5,13},{6,14},{7,15},{8,0},{9,1},... | collective-permute-start | bytes 638984 | tf_op jit(solution)/shard_map/ppermute | solution.py:709
  28.2 1.5 collective-permute-start.10
  28.2 1.7 %collective-permute-start.9 = (bf16[832,128]{1,0:T(8,128)(2,1)S(1)}, bf16[832,128]{1,0:T(8,128)(2,1)S(1)}, u32[]{:S(2)}, u32[]{:S(2)}) collective-permute-start(bf16[832,128]{1,0:T(8,128)(2,1)S(1)} %collective-permute-done.3.refs_1_), channel_id=1, source_target_pairs={{0,8},{1,9},{2,10},{3,11},{4,12},{5,13},{6,14},{7,15},{8,0},{9,1},... | collective-permute-start | bytes 638984 | tf_op jit(solution)/shard_map/ppermute | solution.py:709
  28.8 24.8 %collective-permute-start.15 = (bf16[1280,128]{1,0:T(8,128)(2,1)S(1)}, bf16[1280,128]{1,0:T(8,128)(2,1)S(1)}, u32[]{:S(2)}, u32[]{:S(2)}) collective-permute-start(bf16[1280,128]{1,0:T(8,128)(2,1)S(1)} %constant_dynamic-update-slice_fusion.4.refs_0_), channel_id=1, source_target_pairs={{0,8},{1,9},{2,10},{3,11},{4,12},{5,13},{6,14},{7,15},{8,0},{9,1},... | collective-permute-start | bytes 983048 | tf_op jit(solution)/shard_map/ppermute | solution.py:709
  29.9 19.0 %collective-permute-start.14 = (bf16[1280,128]{1,0:T(8,128)(2,1)S(1)}, bf16[1280,128]{1,0:T(8,128)(2,1)S(1)}, u32[]{:S(2)}, u32[]{:S(2)}) collective-permute-start(bf16[1280,128]{1,0:T(8,128)(2,1)S(1)} %constant_dynamic-update-slice_fusion.4.refs_0_), channel_id=1, source_target_pairs={{0,1},{1,0},{2,3},{3,2},{4,5},{5,4},{6,7},{7,6},{8,9},{9,8},{10,11... | collective-permute-start | bytes 983048 | tf_op jit(solution)/shard_map/ppermute | solution.py:709
  30.9 18.1 %collective-permute-start.13 = (bf16[1280,128]{1,0:T(8,128)(2,1)S(1)}, bf16[1280,128]{1,0:T(8,128)(2,1)S(1)}, u32[]{:S(2)}, u32[]{:S(2)}) collective-permute-start(bf16[1280,128]{1,0:T(8,128)(2,1)S(1)} %constant_dynamic-update-slice_fusion.4.refs_0_), channel_id=1, source_target_pairs={{0,16},{1,17},{2,18},{3,19},{4,20},{5,21},{6,22},{7,23},{8,24},{9,... | collective-permute-start | bytes 983048 | tf_op jit(solution)/shard_map/ppermute | solution.py:709
  32.0 17.0 %collective-permute-start.12 = (bf16[1280,128]{1,0:T(8,128)(2,1)S(1)}, bf16[1280,128]{1,0:T(8,128)(2,1)S(1)}, u32[]{:S(2)}, u32[]{:S(2)}) collective-permute-start(bf16[1280,128]{1,0:T(8,128)(2,1)S(1)} %constant_dynamic-update-slice_fusion.4.refs_0_), channel_id=1, source_target_pairs={{0,17},{1,16},{2,19},{3,18},{4,21},{5,20},{6,23},{7,22},{8,25},{9,... | collective-permute-start | bytes 983048 | tf_op jit(solution)/shard_map/ppermute | solution.py:709
  48.9 4.7 %copy-start = (bf16[2048,512]{1,0:T(8,128)(2,1)S(1)}, bf16[2048,512]{1,0:T(8,128)(2,1)}, u32[]{:S(2)}) copy-start(bf16[2048,512]{1,0:T(8,128)(2,1)} %cotangent.1) | copy-start | bytes 6291460
  49.0 4.6 %collective-permute-start.16 = (bf16[1280,128]{1,0:T(8,128)(2,1)S(1)}, bf16[1280,128]{1,0:T(8,128)(2,1)S(1)}, u32[]{:S(2)}, u32[]{:S(2)}) collective-permute-start(bf16[1280,128]{1,0:T(8,128)(2,1)S(1)} %collective-permute-done.12.refs_1_), channel_id=1, source_target_pairs={{0,8},{1,9},{2,10},{3,11},{4,12},{5,13},{6,14},{7,15},{8,0},{9,1},... | collective-permute-start | bytes 983048 | tf_op jit(solution)/shard_map/ppermute | solution.py:709
  49.1 4.5 %collective-permute-start.17 = (bf16[1280,128]{1,0:T(8,128)(2,1)S(1)}, bf16[1280,128]{1,0:T(8,128)(2,1)S(1)}, u32[]{:S(2)}, u32[]{:S(2)}) collective-permute-start(bf16[1280,128]{1,0:T(8,128)(2,1)S(1)} %collective-permute-done.13.refs_2_), channel_id=1, source_target_pairs={{0,8},{1,9},{2,10},{3,11},{4,12},{5,13},{6,14},{7,15},{8,0},{9,1},... | collective-permute-start | bytes 983048 | tf_op jit(solution)/shard_map/ppermute | solution.py:709
  49.6 4.1 %collective-permute-start.18 = (bf16[1280,128]{1,0:T(8,128)(2,1)S(1)}, bf16[1280,128]{1,0:T(8,128)(2,1)S(1)}, u32[]{:S(2)}, u32[]{:S(2)}) collective-permute-start(bf16[1280,128]{1,0:T(8,128)(2,1)S(1)} %collective-permute-done.14.refs_3_), channel_id=1, source_target_pairs={{0,8},{1,9},{2,10},{3,11},{4,12},{5,13},{6,14},{7,15},{8,0},{9,1},... | collective-permute-start | bytes 983048 | tf_op jit(solution)/shard_map/ppermute | solution.py:709
  78.6 12.1 %collective-permute-start.20 = (bf16[5120,128]{1,0:T(8,128)(2,1)S(1)}, bf16[5120,128]{1,0:T(8,128)(2,1)S(1)}, u32[]{:S(2)}, u32[]{:S(2)}) collective-permute-start(bf16[5120,128]{1,0:T(8,128)(2,1)S(1)} %get-tuple-element.101), channel_id=1, source_target_pairs={{0,8},{1,9},{2,10},{3,11},{4,12},{5,13},{6,14},{7,15},{8,0},{9,1},... | collective-permute-start | bytes 3932168 | tf_op jit(solution)/shard_map/ppermute | solution.py:709
  90.6 40.5 %collective-permute-start.19 = (bf16[768,128]{1,0:T(8,128)(2,1)S(1)}, bf16[768,128]{1,0:T(8,128)(2,1)S(1)}, u32[]{:S(2)}, u32[]{:S(2)}) collective-permute-start(bf16[768,128]{1,0:T(8,128)(2,1)S(1)} %get-tuple-element.98), channel_id=1, source_target_pairs={{0,8},{1,9},{2,10},{3,11},{4,12},{5,13},{6,14},{7,15},{8,0},{9,1},... | collective-permute-start | bytes 589832 | tf_op jit(solution)/shard_map/ppermute | solution.py:709
  91.0 26.6 %collective-permute-start.23 = (bf16[1280,128]{1,0:T(8,128)(2,1)S(1)}, bf16[1280,128]{1,0:T(8,128)(2,1)S(1)}, u32[]{:S(2)}, u32[]{:S(2)}) collective-permute-start(bf16[1280,128]{1,0:T(8,128)(2,1)S(1)} %get-tuple-element.136), channel_id=1, source_target_pairs={{0,17},{1,16},{2,19},{3,18},{4,21},{5,20},{6,23},{7,22},{8,25},{9,... | collective-permute-start | bytes 983048 | tf_op jit(solution)/shard_map/ppermute | solution.py:709
  92.5 25.1 %collective-permute-start.22 = (bf16[1280,128]{1,0:T(8,128)(2,1)S(1)}, bf16[1280,128]{1,0:T(8,128)(2,1)S(1)}, u32[]{:S(2)}, u32[]{:S(2)}) collective-permute-start(bf16[1280,128]{1,0:T(8,128)(2,1)S(1)} %get-tuple-element.137), channel_id=1, source_target_pairs={{0,16},{1,17},{2,18},{3,19},{4,20},{5,21},{6,22},{7,23},{8,24},{9,... | collective-permute-start | bytes 983048 | tf_op jit(solution)/shard_map/ppermute | solution.py:709
  93.4 24.2 %collective-permute-start.21 = (bf16[1280,128]{1,0:T(8,128)(2,1)S(1)}, bf16[1280,128]{1,0:T(8,128)(2,1)S(1)}, u32[]{:S(2)}, u32[]{:S(2)}) collective-permute-start(bf16[1280,128]{1,0:T(8,128)(2,1)S(1)} %get-tuple-element.138), channel_id=1, source_target_pairs={{0,1},{1,0},{2,3},{3,2},{4,5},{5,4},{6,7},{7,6},{8,9},{9,8},{10,11... | collective-permute-start | bytes 983048 | tf_op jit(solution)/shard_map/ppermute | solution.py:709
  117.6 13.8 %collective-permute-start.24 = (bf16[1536,128]{1,0:T(8,128)(2,1)S(1)}, bf16[1536,128]{1,0:T(8,128)(2,1)S(1)}, u32[]{:S(2)}, u32[]{:S(2)}) collective-permute-start(bf16[1536,128]{1,0:T(8,128)(2,1)S(1)} %get-tuple-element.114), channel_id=1, source_target_pairs={{0,8},{1,9},{2,10},{3,11},{4,12},{5,13},{6,14},{7,15},{8,0},{9,1},... | collective-permute-start | bytes 1179656 | tf_op jit(solution)/shard_map/ppermute | solution.py:709
  117.9 13.6 %collective-permute-start.32 = (bf16[640,128]{1,0:T(8,128)(2,1)S(1)}, bf16[640,128]{1,0:T(8,128)(2,1)S(1)}, u32[]{:S(2)}, u32[]{:S(2)}) collective-permute-start(bf16[640,128]{1,0:T(8,128)(2,1)S(1)} %slice.258), channel_id=1, source_target_pairs={{0,2},{1,3},{2,0},{3,1},{4,6},{5,7},{6,4},{7,5},{8,10},{9,11},{10,... | collective-permute-start | bytes 491528 | tf_op jit(solution)/shard_map/ppermute | solution.py:709
  131.1 1.5 collective-permute-start.25
  132.8 9.7 %collective-permute-start.26 = (bf16[832,128]{1,0:T(8,128)(2,1)S(1)}, bf16[832,128]{1,0:T(8,128)(2,1)S(1)}, u32[]{:S(2)}, u32[]{:S(2)}) collective-permute-start(bf16[832,128]{1,0:T(8,128)(2,1)S(1)} %bitcast.50), channel_id=1, source_target_pairs={{0,1},{1,0},{2,3},{3,2},{4,5},{5,4},{6,7},{7,6},{8,9},{9,8},{10,11... | collective-permute-start | bytes 638984 | tf_op jit(solution)/shard_map/ppermute | solution.py:709
  133.8 10.4 %collective-permute-start.27 = (bf16[832,128]{1,0:T(8,128)(2,1)S(1)}, bf16[832,128]{1,0:T(8,128)(2,1)S(1)}, u32[]{:S(2)}, u32[]{:S(2)}) collective-permute-start(bf16[832,128]{1,0:T(8,128)(2,1)S(1)} %bitcast.52), channel_id=1, source_target_pairs={{0,16},{1,17},{2,18},{3,19},{4,20},{5,21},{6,22},{7,23},{8,24},{9,... | collective-permute-start | bytes 638984 | tf_op jit(solution)/shard_map/ppermute | solution.py:709
  134.9 10.8 %collective-permute-start.28 = (bf16[832,128]{1,0:T(8,128)(2,1)S(1)}, bf16[832,128]{1,0:T(8,128)(2,1)S(1)}, u32[]{:S(2)}, u32[]{:S(2)}) collective-permute-start(bf16[832,128]{1,0:T(8,128)(2,1)S(1)} %bitcast.53), channel_id=1, source_target_pairs={{0,17},{1,16},{2,19},{3,18},{4,21},{5,20},{6,23},{7,22},{8,25},{9,... | collective-permute-start | bytes 638984 | tf_op jit(solution)/shard_map/ppermute | solution.py:709
  141.5 8.8 %collective-permute-start.33 = (bf16[320,128]{1,0:T(8,128)(2,1)S(1)}, bf16[320,128]{1,0:T(8,128)(2,1)S(1)}, u32[]{:S(2)}, u32[]{:S(2)}) collective-permute-start(bf16[320,128]{1,0:T(8,128)(2,1)S(1)} %slice.259), channel_id=1, source_target_pairs={{0,4},{1,5},{2,6},{3,7},{4,0},{5,1},{6,2},{7,3},{8,12},{9,13},{10,... | collective-permute-start | bytes 245768 | tf_op jit(solution)/shard_map/ppermute | solution.py:709
  145.8 6.4 %collective-permute-start.31 = (bf16[208,128]{1,0:T(8,128)(2,1)S(1)}, bf16[208,128]{1,0:T(8,128)(2,1)S(1)}, u32[]{:S(2)}, u32[]{:S(2)}) collective-permute-start(bf16[208,128]{1,0:T(8,128)(2,1)S(1)} %get-tuple-element.151), channel_id=1, source_target_pairs={{0,6},{1,7},{2,4},{3,5},{4,2},{5,3},{6,0},{7,1},{8,14},{9,15},{10,... | collective-permute-start | bytes 159752 | tf_op jit(solution)/shard_map/ppermute | solution.py:709
  147.3 6.3 %collective-permute-start.30 = (bf16[208,128]{1,0:T(8,128)(2,1)S(1)}, bf16[208,128]{1,0:T(8,128)(2,1)S(1)}, u32[]{:S(2)}, u32[]{:S(2)}) collective-permute-start(bf16[208,128]{1,0:T(8,128)(2,1)S(1)} %get-tuple-element.152), channel_id=1, source_target_pairs={{0,4},{1,5},{2,6},{3,7},{4,0},{5,1},{6,2},{7,3},{8,12},{9,13},{10,... | collective-permute-start | bytes 159752 | tf_op jit(solution)/shard_map/ppermute | solution.py:709
  148.5 5.2 %collective-permute-start.29 = (bf16[208,128]{1,0:T(8,128)(2,1)S(1)}, bf16[208,128]{1,0:T(8,128)(2,1)S(1)}, u32[]{:S(2)}, u32[]{:S(2)}) collective-permute-start(bf16[208,128]{1,0:T(8,128)(2,1)S(1)} %get-tuple-element.153), channel_id=1, source_target_pairs={{0,2},{1,3},{2,0},{3,1},{4,6},{5,7},{6,4},{7,5},{8,10},{9,11},{10,... | collective-permute-start | bytes 159752 | tf_op jit(solution)/shard_map/ppermute | solution.py:709
